TPU v7x, 32 devices: a whole 2x2x4 slice. The times are simulated.
32 devices in a mesh: groups: 2 (over y), seq: 4 (over z), mp: 2 (over x), sub: 2 (over core).
Axes of the slice: x: 2, y: 2, z: 4, core: 2. Of those that a mesh axis runs over, the one named last changes fastest.
Arguments:
- seq_in: bfloat16 [4096, 1536], P(('groups', 'seq'), ('mp', 'sub')), parts along dimension 0, may hold values from -48 to 48
- conv_gain: float32 [3, 1536], replicated, may hold values from 0.1 to 1.9
- conv_weight: bfloat16 [3, 3, 1536, 1536], P(None, None, None, ('mp', 'sub')), may hold values from -0.09375 to 0.09375
- w_q: bfloat16 [1536, 1024], P(None, 'mp'), may hold values from -0.102062073 to 0.102062073
- w_k: bfloat16 [1536, 1024], P(None, 'mp'), may hold values from -0.102062073 to 0.102062073
- w_v: bfloat16 [1536, 1024], P(None, 'mp'), may hold values from -0.15625 to 0.15625
- w_o: bfloat16 [1024, 1536], P('mp'), may hold values from -0.1875 to 0.1875
Outputs:
- seq_out: bfloat16 [4096, 1536], P(('groups', 'seq', 'sub'), 'mp'), parts along dimension 0
There are 2 independent parts, one for each index of `groups`. A program takes and returns all parts, laid end to end along the dimension named above; an argument that names none is the same for every part. Nothing has to cross between parts.
All inputs are finite; a program needn't handle non-finite values.
Results may differ from a plain program's by a relative error of at most 0.015.
Values may be sent and summed in bfloat16 or wider, within the bound.
No kernel may reach another device: no remote copies, remote signals or barrier semaphores. Data moves between devices by JAX's collectives and lax.ppermute only.
A program may use at most 128 MiB of HBM per device.

v0:
```python
import math

import jax
import jax.numpy as jnp
from jax import lax
from jax.sharding import PartitionSpec as P

HEAD = 128
LAYERS = 3
BINS_DEV = 512


def passed_along(x, axis, by):
    devices = lax.axis_size(axis)
    pairs = [(i, i + by) for i in range(devices) if 0 <= i + by < devices]
    return lax.ppermute(x, axis, pairs)


def tower_section(stream_shard, gain_row, weight_taps, dilation):
    rows_here = stream_shard.shape[0]
    gathered = lax.all_gather(stream_shard, ("mp", "sub"), axis=1, tiled=True)
    widened = gathered.astype(jnp.float32)
    normed = (
        widened * lax.rsqrt(jnp.mean(widened * widened, axis=1, keepdims=True) + 1e-06) * gain_row
    )
    hidden = jax.nn.gelu(normed).astype(jnp.bfloat16)
    tap_terms = jnp.einsum("rc,jco->jro", hidden, weight_taps, preferred_element_type=jnp.float32)
    span_rows = min(dilation, rows_here)
    hop_count = max(dilation // rows_here, 1)
    lower_part = passed_along(
        tap_terms[0, rows_here - span_rows :].astype(jnp.bfloat16), "seq", hop_count
    ).astype(jnp.float32)
    upper_part = passed_along(
        tap_terms[2, :span_rows].astype(jnp.bfloat16), "seq", -hop_count
    ).astype(jnp.float32)
    before = jnp.concatenate([lower_part, tap_terms[0, : rows_here - span_rows]], axis=0)
    after = jnp.concatenate([tap_terms[2, span_rows:], upper_part], axis=0)
    return (stream_shard.astype(jnp.float32) + before + tap_terms[1] + after).astype(jnp.bfloat16)


def per_device(seq_in, conv_gain, conv_weight, w_q, w_k, w_v, w_o):
    rows_here = seq_in.shape[0]
    dilations = (BINS_DEV // 4, BINS_DEV, 2 * BINS_DEV)
    stream = seq_in
    for section_index in range(LAYERS):
        stream = tower_section(
            stream, conv_gain[section_index], conv_weight[section_index], dilations[section_index]
        )
    query_rows = rows_here // lax.axis_size("sub")
    mp_width = w_o.shape[1] // lax.axis_size("mp")
    widest = lax.all_gather(stream, ("mp", "sub"), axis=1, tiled=True)
    query_inputs = lax.dynamic_slice_in_dim(
        widest, lax.axis_index("sub") * query_rows, query_rows, 0
    )
    residual_part = lax.dynamic_slice_in_dim(
        query_inputs, lax.axis_index("mp") * mp_width, mp_width, 1
    )
    heads_here = w_q.shape[1] // HEAD
    queries = (
        jnp.dot(query_inputs, w_q, preferred_element_type=jnp.float32)
        .astype(jnp.bfloat16)
        .reshape(query_rows, heads_here, HEAD)
    )
    keys = (
        jnp.dot(query_inputs, w_k, preferred_element_type=jnp.float32)
        .astype(jnp.bfloat16)
        .reshape(query_rows, heads_here, HEAD)
    )
    values = (
        jnp.dot(query_inputs, w_v, preferred_element_type=jnp.float32)
        .astype(jnp.bfloat16)
        .reshape(query_rows, heads_here, HEAD)
    )
    score_scale = 1.0 / math.sqrt(HEAD)
    running_top = jnp.full((heads_here, query_rows), -1e30, jnp.float32)
    running_numer = jnp.zeros((query_rows, heads_here, HEAD), jnp.float32)
    key_rows = lax.all_gather(keys, ("seq", "sub"), axis=0, tiled=True)
    value_rows = lax.all_gather(values, ("seq", "sub"), axis=0, tiled=True)
    scores = (
        jnp.einsum("qhe,khe->hqk", queries, key_rows, preferred_element_type=jnp.float32)
        * score_scale
    )
    new_top = jnp.maximum(running_top, jnp.max(scores, axis=-1))
    expw = jnp.exp(scores - new_top[:, :, None])
    factor = jnp.exp(running_top - new_top)
    new_denom = jnp.sum(expw, axis=-1)
    contrib = jnp.einsum(
        "hqk,khe->qhe", expw.astype(jnp.bfloat16), value_rows, preferred_element_type=jnp.float32
    )
    new_numer = running_numer * factor.T[:, :, None] + contrib
    attended = (
        (new_numer / new_denom.T[:, :, None])
        .astype(jnp.bfloat16)
        .reshape(query_rows, heads_here * HEAD)
    )
    column_weight = lax.all_to_all(w_o, "mp", split_axis=1, concat_axis=0, tiled=True)
    every_head = lax.all_gather(attended, "mp", axis=1, tiled=True)
    shares = jnp.dot(every_head, column_weight, preferred_element_type=jnp.float32)
    return (residual_part.astype(jnp.float32) + shares).astype(jnp.bfloat16)


def solution(mesh):
    placed = (
        P(("groups", "seq"), ("mp", "sub")),
        P(),
        P(None, None, None, ("mp", "sub")),
        P(None, "mp"),
        P(None, "mp"),
        P(None, "mp"),
        P("mp", None),
    )
    return jax.shard_map(
        per_device,
        mesh=mesh,
        in_specs=placed,
        out_specs=P(("groups", "seq", "sub"), "mp"),
        check_vma=False,
    )
```

profile of v0, /device:TPU:0, one launch (start us, length us, event | category | flops | bytes accessed | tf_op | source)
XLA Modules:
  0.0 252.3 jit_solution(15815357984765979070)
XLA Ops:
  6.5 0.7 all-gather.7.cloned.1.call-update
  7.3 0.9 slice_reduce_fusion
  8.2 23.1 %all-gather.7.cloned.1.call-done = bf16[512,1536]{1,0:T(8,128)(2,1)} async-done(((bf16[512,384]{1,0:T(8,128)(2,1)}), bf16[512,1536]{1,0:T(8,128)(2,1)}) %all-gather.7.cloned.1.call-update) | async-done | bytes 1572880 | tf_op jit(solution)/shard_map/all_gather | solution.py:21
  31.3 1.8 fusion.15
  33.1 5.6 %fusion.124 = (bf16[3,512,384]{2,1,0:T(8,128)(2,1)S(1)}, f32[3,512,384]{2,1,0:T(8,128)S(1)}) fusion(bf16[3,3,1536,384]{3,2,1,0:T(8,128)(2,1)} %param.9, bf16[512,1536]{1,0:T(8,128)(2,1)} %all-gather.7.cloned.1.call-done, f32[1536]{0:T(1024)S(1)} %get-tuple-element.6, f32[512]{0:T(512)S(1)} %add_rsqrt_fusion.2), kind=kOutput, calls=%fused_computation.142 | convolution fusion | flops 1821966336 | bytes 8658944 | tf_op jit(solution)/shard_map/rc,jco->jro/dot_general | solution.py:27
  38.7 3.5 %collective-permute-start = (bf16[128,384]{1,0:T(8,128)(2,1)S(1)}, bf16[128,384]{1,0:T(8,128)(2,1)S(1)}, u32[]{:S(2)}, u32[]{:S(2)}) collective-permute-start(bf16[128,384]{1,0:T(8,128)(2,1)S(1)} %get-tuple-element.15), channel_id=1, source_target_pairs={{0,4},{4,8},{8,12},{1,5},{5,9},{9,13},{2,6},{6,10},{10,14},{3,7},{... | collective-permute-start | bytes 294920 | tf_op jit(solution)/shard_map/ppermute | solution.py:16
  42.3 1.3 collective-permute-start.1
  43.6 0.1 slice_bitcast_fusion.3
  43.7 1.0 collective-permute-done
  44.7 4.1 %collective-permute-done.1 = bf16[128,384]{1,0:T(8,128)(2,1)S(1)} collective-permute-done((bf16[128,384]{1,0:T(8,128)(2,1)S(1)}, bf16[128,384]{1,0:T(8,128)(2,1)S(1)}, u32[]{:S(2)}, u32[]{:S(2)}) %collective-permute-start.1) | collective-permute-done | bytes 98336 | tf_op jit(solution)/shard_map/ppermute | solution.py:16
  48.8 0.9 fusion.101
  49.9 18.8 %all-gather.9.cloned.1.call-done = bf16[512,1536]{1,0:T(8,128)(2,1)} async-done(((bf16[512,384]{1,0:T(8,128)(2,1)}), bf16[512,1536]{1,0:T(8,128)(2,1)}) %all-gather.9.cloned.1.call-update) | async-done | bytes 1572880 | tf_op jit(solution)/shard_map/all_gather | solution.py:21
  68.7 1.8 fusion.24
  70.5 5.6 %fusion.125 = (bf16[3,512,384]{2,1,0:T(8,128)(2,1)S(1)}, f32[3,512,384]{2,1,0:T(8,128)S(1)}) fusion(bf16[3,3,1536,384]{3,2,1,0:T(8,128)(2,1)} %param.9, bf16[512,1536]{1,0:T(8,128)(2,1)} %all-gather.9.cloned.1.call-done, f32[1536]{0:T(1024)S(1)} %get-tuple-element.7, f32[512]{0:T(512)S(1)} %add_rsqrt_fusion.1), kind=kOutput, calls=%fused_computation.143 | convolution fusion | flops 1821966336 | bytes 8658944 | tf_op jit(solution)/shard_map/rc,jco->jro/dot_general | solution.py:27
  76.1 0.1 slice_bitcast_fusion.8
  76.2 3.4 %collective-permute-start.2 = (bf16[512,384]{1,0:T(8,128)(2,1)S(1)}, bf16[512,384]{1,0:T(8,128)(2,1)S(1)}, u32[]{:S(2)}, u32[]{:S(2)}) collective-permute-start(bf16[512,384]{1,0:T(8,128)(2,1)S(1)} %get-tuple-element.12), channel_id=1, source_target_pairs={{0,4},{4,8},{8,12},{1,5},{5,9},{9,13},{2,6},{6,10},{10,14},{3,7},{... | collective-permute-start | bytes 1179656 | tf_op jit(solution)/shard_map/ppermute | solution.py:16
  79.6 1.3 collective-permute-start.3
  80.9 7.4 %collective-permute-done.2 = bf16[512,384]{1,0:T(8,128)(2,1)S(1)} collective-permute-done((bf16[512,384]{1,0:T(8,128)(2,1)S(1)}, bf16[512,384]{1,0:T(8,128)(2,1)S(1)}, u32[]{:S(2)}, u32[]{:S(2)}) %collective-permute-start.2) | collective-permute-done | bytes 393248 | tf_op jit(solution)/shard_map/ppermute | solution.py:16
  88.4 4.1 %collective-permute-done.3 = bf16[512,384]{1,0:T(8,128)(2,1)S(1)} collective-permute-done((bf16[512,384]{1,0:T(8,128)(2,1)S(1)}, bf16[512,384]{1,0:T(8,128)(2,1)S(1)}, u32[]{:S(2)}, u32[]{:S(2)}) %collective-permute-start.3) | collective-permute-done | bytes 393248 | tf_op jit(solution)/shard_map/ppermute | solution.py:16
  92.5 1.0 fusion.98
  93.5 18.8 %all-gather.11.cloned.1.call-done = bf16[512,1536]{1,0:T(8,128)(2,1)} async-done(((bf16[512,384]{1,0:T(8,128)(2,1)}), bf16[512,1536]{1,0:T(8,128)(2,1)}) %all-gather.11.cloned.1.call-update) | async-done | bytes 1572880 | tf_op jit(solution)/shard_map/all_gather | solution.py:21
  112.3 1.8 fusion.33
  114.2 5.6 %fusion.126 = (bf16[3,512,384]{2,1,0:T(8,128)(2,1)S(1)}, f32[3,512,384]{2,1,0:T(8,128)S(1)}) fusion(bf16[3,3,1536,384]{3,2,1,0:T(8,128)(2,1)} %param.9, bf16[512,1536]{1,0:T(8,128)(2,1)} %all-gather.11.cloned.1.call-done, f32[1536]{0:T(1024)S(1)} %get-tuple-element.5, f32[512]{0:T(512)S(1)} %add_rsqrt_fusion), kind=kOutput, calls=%fused_computation.144 | convolution fusion | flops 1821966336 | bytes 8658944 | tf_op jit(solution)/shard_map/rc,jco->jro/dot_general | solution.py:27
  119.8 0.1 slice_bitcast_fusion.6
  119.9 4.3 %collective-permute-start.4 = (bf16[512,384]{1,0:T(8,128)(2,1)S(1)}, bf16[512,384]{1,0:T(8,128)(2,1)S(1)}, u32[]{:S(2)}, u32[]{:S(2)}) collective-permute-start(bf16[512,384]{1,0:T(8,128)(2,1)S(1)} %get-tuple-element.10), channel_id=1, source_target_pairs={{0,8},{4,12},{1,9},{5,13},{2,10},{6,14},{3,11},{7,15},{16,24},{20,... | collective-permute-start | bytes 1179656 | tf_op jit(solution)/shard_map/ppermute | solution.py:16
  124.2 1.3 collective-permute-start.5
  125.5 7.5 %collective-permute-done.4 = bf16[512,384]{1,0:T(8,128)(2,1)S(1)} collective-permute-done((bf16[512,384]{1,0:T(8,128)(2,1)S(1)}, bf16[512,384]{1,0:T(8,128)(2,1)S(1)}, u32[]{:S(2)}, u32[]{:S(2)}) %collective-permute-start.4) | collective-permute-done | bytes 393248 | tf_op jit(solution)/shard_map/ppermute | solution.py:16
  133.0 13.4 %collective-permute-done.5 = bf16[512,384]{1,0:T(8,128)(2,1)S(1)} collective-permute-done((bf16[512,384]{1,0:T(8,128)(2,1)S(1)}, bf16[512,384]{1,0:T(8,128)(2,1)S(1)}, u32[]{:S(2)}, u32[]{:S(2)}) %collective-permute-start.5) | collective-permute-done | bytes 393248 | tf_op jit(solution)/shard_map/ppermute | solution.py:16
  146.4 1.0 fusion.95
  147.4 0.0 all-gather.15.cloned.1.call-start
  147.5 17.0 %all-gather.13.cloned.1.call-done = bf16[512,1536]{1,0:T(8,128)(2,1)} async-done(((bf16[512,384]{1,0:T(8,128)(2,1)}), bf16[512,1536]{1,0:T(8,128)(2,1)}) %all-gather.13.cloned.1.call-update) | async-done | bytes 1572880 | tf_op jit(solution)/shard_map/all_gather | solution.py:51
  164.4 1.7 fusion.86
  166.2 0.8 copy.29
  166.9 0.2 all-gather.17.cloned.1.call-start
  167.2 2.2 convolution_convert_fusion
  169.4 0.8 copy.19
  170.3 1.6 copy.17
  171.8 3.7 %all-to-all-start = ((bf16[512,2,768]{0,2,1:T(8,128)(2,1)}), bf16[512,2,768]{0,2,1:T(8,128)(2,1)S(1)}, u32[]{:S(2)}, u32[]{:S(2)}) async-start(bf16[512,2,768]{0,2,1:T(8,128)(2,1)} %bitcast.118), calls=%async_computation | async-start | bytes 3145728 | tf_op jit(solution)/shard_map/all_to_all | solution.py:96
  175.6 19.9 %all-to-all-done = bf16[512,2,768]{0,2,1:T(8,128)(2,1)S(1)} async-done(((bf16[512,2,768]{0,2,1:T(8,128)(2,1)}), bf16[512,2,768]{0,2,1:T(8,128)(2,1)S(1)}, u32[]{:S(2)}, u32[]{:S(2)}) %all-to-all-start) | async-done | bytes 1572896 | tf_op jit(solution)/shard_map/all_to_all | solution.py:96
  195.4 1.6 copy.18
  197.1 2.2 fusion.85
  199.3 2.9 %multiply_reduce_fusion = (f32[4,256]{1,0:T(4,128)S(1)}, f32[4,256,2048]{2,1,0:T(8,128)S(1)}) fusion(bf16[2048,4,128]{2,0,1:T(8,128)(2,1)} %all-gather.15.cloned.1.call-done, bf16[32,4,8,128]{3,2,1,0:T(8,128)(2,1)S(1)} %fusion.85), kind=kOutput, calls=%fused_computation.1 | convolution fusion | flops 541064192 | bytes 10752000 | tf_op jit(solution)/shard_map/qhe,khe->hqk/dot_general | solution.py:80
  202.3 3.2 %copy-done.1 = f32[4,256,2048]{2,1,0:T(8,128)} copy-done((f32[4,256,2048]{2,1,0:T(8,128)}, f32[4,256,2048]{2,1,0:T(8,128)S(1)}, u32[]{:S(2)}) %copy-start.1) | copy-done | bytes 8388632
  205.5 1.6 fusion
  207.1 20.9 %all-gather.17.cloned.1.call-done = bf16[2048,4,128]{0,2,1:T(8,128)(2,1)} async-done(((bf16[256,4,128]{0,2,1:T(8,128)(2,1)}), bf16[2048,4,128]{0,2,1:T(8,128)(2,1)}) %all-gather.17.cloned.1.call-update) | async-done | bytes 2097168 | tf_op jit(solution)/shard_map/all_gather | solution.py:78
  228.0 5.9 %fusion.90 = bf16[256,4,128]{0,2,1:T(8,128)(2,1)S(1)} fusion(bf16[2048,4,128]{0,2,1:T(8,128)(2,1)} %all-gather.17.cloned.1.call-done, f32[4,256,2048]{2,1,0:T(8,128)} %copy-done.1, f32[4,256]{1,0:T(4,128)S(1)} %get-tuple-element.17, f32[256,4]{0,1:T(4,128)S(1)} %bitcast.123, f32[256,4]{0,1:T(4,128)S(1)} %get-tuple-element.16), kind=kOutput, calls=%fused_computation.89 | convolution fusion | flops 543555584 | bytes 10760192 | tf_op jit(solution)/shard_map/hqk,khe->qhe/dot_general | solution.py:87
  234.0 9.1 %all_gather.27 = bf16[256,1024]{0,1:T(8,128)(2,1)S(1)} all-gather(bf16[256,512]{0,1:T(8,128)(2,1)S(1)} %bitcast.122), channel_id=1, replica_groups=mesh['groups'=2,'seq'=4,'mp'=2,'sub'=2] {'mp'}, dimensions={1}, use_global_device_ids=true | all-gather | bytes 786432 | tf_op jit(solution)/shard_map/all_gather | solution.py:97
  243.1 2.4 fusion.78
  (30 shorter events, 0.3 us)
Async XLA Ops:
  6.5 157.9 %copy-start = (bf16[1536,512]{1,0:T(8,128)(2,1)S(1)}, bf16[1536,512]{1,0:T(8,128)(2,1)}, u32[]{:S(2)}) copy-start(bf16[1536,512]{1,0:T(8,128)(2,1)} %param.11) | copy-start | bytes 4718596
  6.5 24.8 %all-gather.7.cloned.1.call-start = ((), (), s32[]{:S(2)}) async-start(), calls=%async_computation.1 | async-start | bytes 1966080 | tf_op jit(solution)/shard_map/all_gather | solution.py:21
  7.3 61.4 %all-gather.9.cloned.1.call-start = ((), (), s32[]{:S(2)}) async-start(), calls=%async_computation.2 | async-start | bytes 1966080 | tf_op jit(solution)/shard_map/all_gather | solution.py:21
  38.7 10.1 %copy-start.6 = (bf16[512,384]{1,0:T(8,128)(2,1)S(1)}, bf16[512,384]{1,0:T(8,128)(2,1)}, u32[]{:S(2)}) copy-start(bf16[512,384]{1,0:T(8,128)(2,1)} %param.7) | copy-start | bytes 1179652
  38.7 6.0 %collective-permute-start = (bf16[128,384]{1,0:T(8,128)(2,1)S(1)}, bf16[128,384]{1,0:T(8,128)(2,1)S(1)}, u32[]{:S(2)}, u32[]{:S(2)}) collective-permute-start(bf16[128,384]{1,0:T(8,128)(2,1)S(1)} %get-tuple-element.15), channel_id=1, source_target_pairs={{0,4},{4,8},{8,12},{1,5},{5,9},{9,13},{2,6},{6,10},{10,14},{3,7},{... | collective-permute-start | bytes 294920 | tf_op jit(solution)/shard_map/ppermute | solution.py:16
  42.3 6.6 %collective-permute-start.1 = (bf16[128,384]{1,0:T(8,128)(2,1)S(1)}, bf16[128,384]{1,0:T(8,128)(2,1)S(1)}, u32[]{:S(2)}, u32[]{:S(2)}) collective-permute-start(bf16[128,384]{1,0:T(8,128)(2,1)S(1)} %get-tuple-element.14), channel_id=1, source_target_pairs={{4,0},{8,4},{12,8},{5,1},{9,5},{13,9},{6,2},{10,6},{14,10},{7,3},{... | collective-permute-start | bytes 294920 | tf_op jit(solution)/shard_map/ppermute | solution.py:16
  49.8 62.5 %all-gather.11.cloned.1.call-start = ((), (), s32[]{:S(2)}) async-start(), calls=%async_computation.3 | async-start | bytes 1966080 | tf_op jit(solution)/shard_map/all_gather | solution.py:21
  70.5 22.0 %copy-start.3 = (bf16[512,384]{1,0:T(8,128)(2,1)S(1)}, bf16[512,384]{1,0:T(8,128)(2,1)}, u32[]{:S(2)}) copy-start(bf16[512,384]{1,0:T(8,128)(2,1)} %fusion.101) | copy-start | bytes 1179652
  76.2 12.2 %collective-permute-start.2 = (bf16[512,384]{1,0:T(8,128)(2,1)S(1)}, bf16[512,384]{1,0:T(8,128)(2,1)S(1)}, u32[]{:S(2)}, u32[]{:S(2)}) collective-permute-start(bf16[512,384]{1,0:T(8,128)(2,1)S(1)} %get-tuple-element.12), channel_id=1, source_target_pairs={{0,4},{4,8},{8,12},{1,5},{5,9},{9,13},{2,6},{6,10},{10,14},{3,7},{... | collective-permute-start | bytes 1179656 | tf_op jit(solution)/shard_map/ppermute | solution.py:16
  79.6 12.9 %collective-permute-start.3 = (bf16[512,384]{1,0:T(8,128)(2,1)S(1)}, bf16[512,384]{1,0:T(8,128)(2,1)S(1)}, u32[]{:S(2)}, u32[]{:S(2)}) collective-permute-start(bf16[512,384]{1,0:T(8,128)(2,1)S(1)} %get-tuple-element.13), channel_id=1, source_target_pairs={{4,0},{8,4},{12,8},{5,1},{9,5},{13,9},{6,2},{10,6},{14,10},{7,3},{... | collective-permute-start | bytes 1179656 | tf_op jit(solution)/shard_map/ppermute | solution.py:16
  93.5 71.0 %all-gather.13.cloned.1.call-start = ((), (), s32[]{:S(2)}) async-start(), calls=%async_computation.4 | async-start | bytes 1966080 | tf_op jit(solution)/shard_map/all_gather | solution.py:51
  114.1 32.3 %copy-start.4 = (bf16[512,384]{1,0:T(8,128)(2,1)S(1)}, bf16[512,384]{1,0:T(8,128)(2,1)}, u32[]{:S(2)}) copy-start(bf16[512,384]{1,0:T(8,128)(2,1)} %fusion.98) | copy-start | bytes 1179652
  119.9 13.1 %collective-permute-start.4 = (bf16[512,384]{1,0:T(8,128)(2,1)S(1)}, bf16[512,384]{1,0:T(8,128)(2,1)S(1)}, u32[]{:S(2)}, u32[]{:S(2)}) collective-permute-start(bf16[512,384]{1,0:T(8,128)(2,1)S(1)} %get-tuple-element.10), channel_id=1, source_target_pairs={{0,8},{4,12},{1,9},{5,13},{2,10},{6,14},{3,11},{7,15},{16,24},{20,... | collective-permute-start | bytes 1179656 | tf_op jit(solution)/shard_map/ppermute | solution.py:16
  124.2 22.2 %collective-permute-start.5 = (bf16[512,384]{1,0:T(8,128)(2,1)S(1)}, bf16[512,384]{1,0:T(8,128)(2,1)S(1)}, u32[]{:S(2)}, u32[]{:S(2)}) collective-permute-start(bf16[512,384]{1,0:T(8,128)(2,1)S(1)} %get-tuple-element.11), channel_id=1, source_target_pairs={{8,0},{12,4},{9,1},{13,5},{10,2},{14,6},{11,3},{15,7},{24,16},{28,... | collective-permute-start | bytes 1179656 | tf_op jit(solution)/shard_map/ppermute | solution.py:16
  147.4 51.9 %all-gather.15.cloned.1.call-start = ((), (), s32[]{:S(2)}) async-start(), calls=%async_computation.5 | async-start | bytes 2359296 | tf_op jit(solution)/shard_map/all_gather | solution.py:77
  147.5 22.8 %copy-start.5 = (bf16[512,1536]{1,0:T(8,128)(2,1)S(1)}, bf16[512,1536]{1,0:T(8,128)(2,1)}, u32[]{:S(2)}) copy-start(bf16[512,1536]{1,0:T(8,128)(2,1)} %param.13) | copy-start | bytes 4718596
  166.9 61.1 %all-gather.17.cloned.1.call-start = ((), (), s32[]{:S(2)}) async-start(), calls=%async_computation.6 | async-start | bytes 2359296 | tf_op jit(solution)/shard_map/all_gather | solution.py:78
  171.8 23.6 %all-to-all-start = ((bf16[512,2,768]{0,2,1:T(8,128)(2,1)}), bf16[512,2,768]{0,2,1:T(8,128)(2,1)S(1)}, u32[]{:S(2)}, u32[]{:S(2)}) async-start(bf16[512,2,768]{0,2,1:T(8,128)(2,1)} %bitcast.118), calls=%async_computation | async-start | bytes 3145728 | tf_op jit(solution)/shard_map/all_to_all | solution.py:96
  202.3 3.2 %copy-start.1 = (f32[4,256,2048]{2,1,0:T(8,128)}, f32[4,256,2048]{2,1,0:T(8,128)S(1)}, u32[]{:S(2)}) copy-start(f32[4,256,2048]{2,1,0:T(8,128)S(1)} %get-tuple-element.25) | copy-start | bytes 25165828
  228.0 15.1 %copy-start.2 = (bf16[2,512,768]{2,1,0:T(8,128)(2,1)S(1)}, bf16[2,512,768]{2,1,0:T(8,128)(2,1)}, u32[]{:S(2)}) copy-start(bf16[2,512,768]{2,1,0:T(8,128)(2,1)} %copy.18) | copy-start | bytes 4718596
Sparse Core Ops, SparseCore 0:
  8.9 22.3 all-gather.6
  49.9 18.7 all-gather.8
  93.6 18.6 all-gather.10
  147.5 16.8 all-gather.12
  167.1 29.0 all-gather.14
  197.6 30.3 all-gather.16
where the time goes:
time: 253 us; the launch traced here: 252 us
  waiting for transfers between devices  157 us (62%)
  matrix products  34.3 us (14%)
  starting transfers between devices  19.2 us (8%)
  between operations  13.7 us (5%)
  other arithmetic  9.91 us (4%)
  local copies, waits for them, and re-layouts  9.22 us (4%)
  blocking collectives  9.14 us (4%)
    all_gather x3, waiting for transfers between devices, tower_section(): gathered = lax.all_gather(stream_shard, ('mp', 'sub'), axis=1, tiled=True)  60.7 us
    ppermute x6, waiting for transfers between devices, passed_along(): return lax.ppermute(x, axis, pairs)  37.6 us
    all_gather x1, waiting for transfers between devices, per_device(): value_rows = lax.all_gather(values, ('seq', 'sub'), axis=0, tiled=True)  20.9 us
    all_to_all x1, waiting for transfers between devices, per_device(): lax.all_to_all(w_o, 'mp', split_axis=1, concat_axis=0, tiled=True)  19.9 us
    all_gather x1, waiting for transfers between devices, per_device(): widest = lax.all_gather(stream, ('mp', 'sub'), axis=1, tiled=True)  17 us
    dot_general x3, matrix products, tower_section(): jnp.einsum('rc,jco->jro', hidden, weight_taps, preferred_element_type=jnp...  16.9 us
    ppermute x6, starting transfers between devices, passed_along(): return lax.ppermute(x, axis, pairs)  15.1 us
    all_gather x1, blocking collectives, per_device(): every_head = lax.all_gather(attended, 'mp', axis=1, tiled=True)  9.14 us
  transfers between devices with their start and end apart: 13, of which 12 were waited for; matrix products, arithmetic and copies ran while one was open for 6% of the time, Pallas kernels for 0%

commit v1 on v0

--- a/solution.py
+++ b/solution.py
@@ -1,13 +1,429 @@
+import functools
 import math
 
 import jax
 import jax.numpy as jnp
 from jax import lax
+from jax.experimental import pallas as pl
+from jax.experimental.pallas import tpu as pltpu
 from jax.sharding import PartitionSpec as P
 
 HEAD = 128
 LAYERS = 3
 BINS_DEV = 512
+F32 = jnp.float32
+BF16 = jnp.bfloat16
+VMEM_LIMIT = 48 * 1024 * 1024
+
+
+def swap(x, axis):
+    return lax.ppermute(x, axis, [(0, 1), (1, 0)])
+
+
+def swap_both(x):
+    return lax.ppermute(x, ("mp", "sub"), [(i, 3 - i) for i in range(4)])
+
+
+def rotate(x, by):
+    n = lax.axis_size("seq")
+    return lax.ppermute(x, "seq", [(i, (i + by) % n) for i in range(n)])
+
+
+def gather_parts(x):
+    across = swap(x, "mp")
+    return x, swap(x, "sub"), across, swap(across, "sub")
+
+
+def fill_hidden(scalars, parts, gain_ref, hidden):
+    width = parts[0].shape[-1]
+    wide = [part[...].astype(F32) for part in parts]
+    squares = wide[0] * wide[0]
+    for x in wide[1:]:
+        squares = squares + x * x
+    mean = jnp.sum(squares, axis=1, keepdims=True) / (4 * width)
+    scale = lax.rsqrt(mean + 1e-06)
+    for p, x in enumerate(wide):
+        columns = pl.ds(pl.multiple_of(scalars[p] * width, 128), width)
+        normed = x * scale * gain_ref[0, :, columns]
+        hidden[:, columns] = jax.nn.gelu(normed).astype(BF16)
+
+
+def dot(a, b):
+    return jnp.dot(a, b, preferred_element_type=F32)
+
+
+def first_edge_kernel(scalars, p0, p1, p2, p3, gain, w, acc, up, down, hidden):
+    tap = pl.program_id(0)
+    b = up.shape[0]
+
+    @pl.when(tap == 0)
+    def _():
+        fill_hidden(scalars, (p0, p1, p2, p3), gain, hidden)
+
+    terms = dot(hidden[...], w[0, 0])
+
+    @pl.when(tap == 0)
+    def _():
+        acc[1] = terms[:b]
+        up[...] = terms[b:].astype(BF16)
+
+    @pl.when(tap == 1)
+    def _():
+        acc[0] = terms[:b]
+        acc[3] = terms[b:]
+
+    @pl.when(tap == 2)
+    def _():
+        down[...] = terms[:b].astype(BF16)
+        acc[2] = terms[b:]
+
+
+def first_middle_kernel(
+    scalars, p0, p1, p2, p3, edge, gain, w, acc_in, lower, upper, out, hidden, acc
+):
+    tap = pl.program_id(0)
+    b = lower.shape[0]
+
+    @pl.when(tap == 0)
+    def _():
+        fill_hidden(scalars, (p0, p1, p2, p3), gain, hidden)
+
+    terms = dot(hidden[...], w[0, 0])
+
+    @pl.when(tap == 0)
+    def _():
+        acc[0] = acc_in[2] + terms[:b]
+        out[3] = (
+            edge[b:].astype(F32) + acc_in[3] + upper[...].astype(F32) + terms[b:]
+        ).astype(BF16)
+
+    @pl.when(tap == 1)
+    def _():
+        acc[1] = acc_in[1] + terms[:b]
+        acc[0] = acc[0] + terms[b:]
+
+    @pl.when(tap == 2)
+    def _():
+        out[0] = (
+            edge[:b].astype(F32) + acc_in[0] + lower[...].astype(F32) + terms[:b]
+        ).astype(BF16)
+        out[1] = (p0[:b].astype(F32) + acc[1] + terms[b:]).astype(BF16)
+        out[2] = (p0[b:].astype(F32) + acc[0]).astype(BF16)
+
+
+def second_early_kernel(scalars, p0, p1, p2, p3, gain, w, acc, hidden):
+    tap = pl.program_id(0)
+    b = p0.shape[0] // 2
+
+    @pl.when(tap == 0)
+    def _():
+        acc[...] = jnp.zeros_like(acc)
+        fill_hidden(scalars, (p0, p1, p2, p3), gain, hidden)
+
+    terms = dot(hidden[...], w[0, 0])
+    for i in range(2):
+        place = scalars[4 + i] + 2 - tap
+        acc[place] = acc[place] + terms[i * b : (i + 1) * b]
+
+
+def second_late_kernel(
+    scalars, p0, p1, p2, p3, early, gain, w, acc_in, even, odd, hidden, acc, kept
+):
+    tap = pl.program_id(0)
+    b = p0.shape[0] // 2
+
+    @pl.when(tap == 0)
+    def _():
+        acc[...] = acc_in[...]
+        for i in range(2):
+            kept[scalars[4 + i]] = early[i * b : (i + 1) * b]
+            kept[scalars[6 + i]] = p0[i * b : (i + 1) * b]
+        fill_hidden(scalars, (p0, p1, p2, p3), gain, hidden)
+
+    terms = dot(hidden[...], w[0, 0])
+    for i in range(2):
+        place = scalars[6 + i] + 2 - tap
+        acc[place] = acc[place] + terms[i * b : (i + 1) * b]
+
+    @pl.when(tap == 2)
+    def _():
+        for k in range(4):
+            out = even if k % 2 == 0 else odd
+            half = pl.ds((k // 2) * b, b)
+            out[half, :] = (kept[k].astype(F32) + acc[k + 1]).astype(BF16)
+
+
+def third_kernel(scalars, p0, p1, p2, p3, gain, w, out, hidden, acc):
+    step = pl.program_id(0)
+    b = p0.shape[0] // 2
+
+    @pl.when(step == 0)
+    def _():
+        fill_hidden(scalars, (p0, p1, p2, p3), gain, hidden)
+        acc[...] = p0[...].astype(F32) + dot(hidden[...], w[0, 0])
+
+    @pl.when(step == 1)
+    def _():
+        acc[:b] = acc[:b] + dot(hidden[b:], w[0, 0])
+
+    @pl.when(step == 2)
+    def _():
+        acc[b:] = acc[b:] + dot(hidden[:b], w[0, 0])
+        out[...] = acc[...].astype(BF16)
+
+
+def project_kernel(scalars, p0, p1, p2, p3, w_q, w_k, w_v, out, rows):
+    width = p0.shape[1]
+    for p, part in enumerate((p0, p1, p2, p3)):
+        rows[:, pl.ds(pl.multiple_of(scalars[p] * width, 128), width)] = part[...]
+    for i, w in enumerate((w_q, w_k, w_v)):
+        made = dot(rows[...], w[...]).astype(BF16)
+        for h in range(out.shape[0]):
+            out[h, :, i * HEAD : (i + 1) * HEAD] = made[:, h * HEAD : (h + 1) * HEAD]
+
+
+def attend_kernel(scalars, *refs):
+    own, other = refs[:8], refs[8:16]
+    out, queries, keys, values = refs[16:]
+    b = own[0].shape[0]
+    sub = scalars[8]
+    z = scalars[9]
+    for c in range(2):
+        for s in range(4):
+            i = c * 4 + s
+            queries[c, sub, s] = own[i][:, :HEAD]
+            queries[c, 1 - sub, s] = other[i][:, :HEAD]
+            for o, ref in enumerate((own[i], other[i])):
+                here = pl.ds((i * 2 + o) * b, b)
+                keys[here, :] = ref[:, HEAD : 2 * HEAD]
+                values[here, :] = ref[:, 2 * HEAD :]
+    factor = math.log2(math.e) / math.sqrt(HEAD)
+    for k in range(4):
+        for a in range(2):
+            s = lax.rem(z - 2 * sub - a + 4, 4)
+            q = queries[k % 2, k // 2, s]
+            scores = lax.dot_general(
+                q, keys[...], (((1,), (1,)), ((), ())), preferred_element_type=F32
+            )
+            top = jnp.max(scores, axis=1, keepdims=True)
+            expw = jnp.exp2((scores - top) * factor)
+            denom = jnp.sum(expw, axis=1, keepdims=True)
+            numer = dot(expw.astype(BF16), values[...])
+            out[k, a * b : (a + 1) * b, :] = (numer / denom).astype(BF16)
+
+
+def finish_kernel(scalars, *refs):
+    own, other, rest = refs[:4], refs[4:8], refs[8:12]
+    w_own, w_near, w_far, out, mixed, residual = refs[12:]
+    sub, z = scalars[8], scalars[9]
+    b, width = rest[0].shape
+    half = 4 * HEAD
+    for s in range(4):
+        head = lax.rem(z - s + 4, 4)
+        mixed[:, pl.ds(pl.multiple_of(head * HEAD, HEAD), HEAD)] = own[s][...]
+        place = lax.rem(head + 2 * (1 - sub) + 2, 4)
+        mixed[:, pl.ds(pl.multiple_of(half + place * HEAD, HEAD), HEAD)] = other[s][...]
+        turn = lax.rem(z - s + 4, 4)
+        rows = pl.ds(pl.multiple_of((turn // 2) * b, b), b)
+        columns = pl.ds(pl.multiple_of(lax.rem(turn, 2) * width, 128), width)
+        residual[rows, columns] = rest[s][...]
+    shares = dot(mixed[:, :half], w_own[...])
+    shares = shares + dot(mixed[:, half : half + 2 * HEAD], w_near[...])
+    shares = shares + dot(mixed[:, half + 2 * HEAD :], w_far[...])
+    out[...] = (residual[...].astype(F32) + shares).astype(BF16)
+
+
+def whole(x):
+    zeros = (0,) * x.ndim
+    return pl.BlockSpec(x.shape, lambda *_: zeros)
+
+
+def call(kernel, scalars, args, outs, scratch, grid=(1,), specs=None, flops=0):
+    specs = specs or {}
+    in_specs = [specs.get(i, None) or whole(a) for i, a in enumerate(args)]
+    moved = sum(a.size * a.dtype.itemsize for i, a in enumerate(args) if i not in specs)
+    moved += sum(math.prod(o.shape) * o.dtype.itemsize for o in outs)
+    single = len(outs) == 1
+    return pl.pallas_call(
+        kernel,
+        out_shape=outs[0] if single else outs,
+        grid_spec=pltpu.PrefetchScalarGridSpec(
+            num_scalar_prefetch=1,
+            grid=grid,
+            in_specs=in_specs,
+            out_specs=whole(outs[0]) if single else [whole(o) for o in outs],
+            scratch_shapes=scratch,
+        ),
+        compiler_params=pltpu.CompilerParams(
+            dimension_semantics=("arbitrary",) * len(grid), vmem_limit_bytes=VMEM_LIMIT
+        ),
+        cost_estimate=pl.CostEstimate(flops=flops, transcendentals=0, bytes_accessed=moved),
+        name=kernel.__name__,
+    )(scalars, *args)
+
+
+def struct(shape, dtype=BF16):
+    return jax.ShapeDtypeStruct(shape, dtype)
+
+
+def pick(x, index):
+    return lax.dynamic_index_in_dim(x, index, 0, keepdims=False)
+
+
+def per_device_fast(seq_in, conv_gain, conv_weight, w_q, w_k, w_v, w_o):
+    rows, width = seq_in.shape
+    channels = 4 * width
+    n = 4
+    b = rows // n
+    z, mp, sub = (lax.axis_index(a) for a in ("seq", "mp", "sub"))
+    place = mp * 2 + sub
+    turns = [lax.rem(z - s + n, n) for s in range(n)]
+    scalars = jnp.stack(
+        [place, place ^ 1, place ^ 2, place ^ 3] + turns + [sub, z, mp]
+    ).astype(jnp.int32)
+    gains = conv_gain.reshape(LAYERS, 1, channels)
+    hidden = pltpu.VMEM((2 * b, channels), BF16)
+
+    def tap_specs(layer, at_gain, at_w, first=0):
+        return {
+            at_gain: pl.BlockSpec((1, 1, channels), lambda j, _: (layer, 0, 0)),
+            at_w: pl.BlockSpec(
+                (1, 1, channels, width), lambda j, _: (layer, lax.rem(j + first, 3), 0, 0)
+            ),
+        }
+
+    flops = 2 * 2 * b * channels * 3 * width
+
+    edge = jnp.concatenate([seq_in[:b], seq_in[3 * b :]], axis=0)
+    middle = seq_in[b : 3 * b]
+    edge_parts = gather_parts(edge)
+    middle_parts = gather_parts(middle)
+    acc, up, down = call(
+        first_edge_kernel,
+        scalars,
+        (*edge_parts, gains, conv_weight),
+        [struct((n, b, width), F32), struct((b, width)), struct((b, width))],
+        [hidden],
+        grid=(3,),
+        specs=tap_specs(0, 4, 5),
+        flops=flops,
+    )
+    lower = lax.ppermute(up, "seq", [(i, i + 1) for i in range(n - 1)])
+    upper = lax.ppermute(down, "seq", [(i + 1, i) for i in range(n - 1)])
+    stream = call(
+        first_middle_kernel,
+        scalars,
+        (*middle_parts, edge, gains, conv_weight, acc, lower, upper),
+        [struct((n, b, width))],
+        [hidden, pltpu.VMEM((2, b, width), F32)],
+        grid=(3,),
+        specs=tap_specs(0, 5, 6),
+        flops=flops,
+    )
+
+    dealt = [pick(stream, z)]
+    for s in range(1, n):
+        dealt.append(rotate(pick(stream, lax.rem(z + s, n)), s))
+
+    early = jnp.concatenate(dealt[:2], axis=0)
+    late = jnp.concatenate(dealt[2:], axis=0)
+    early_parts = gather_parts(early)
+    late_parts = gather_parts(late)
+    acc = call(
+        second_early_kernel,
+        scalars,
+        (*early_parts, gains, conv_weight),
+        [struct((n + 2, b, width), F32)],
+        [hidden],
+        grid=(3,),
+        specs=tap_specs(1, 4, 5),
+        flops=flops,
+    )
+    pairs = call(
+        second_late_kernel,
+        scalars,
+        (*late_parts, early, gains, conv_weight, acc),
+        [struct((2 * b, width)), struct((2 * b, width))],
+        [hidden, pltpu.VMEM((n + 2, b, width), F32), pltpu.VMEM((n, b, width), BF16)],
+        grid=(3,),
+        specs=tap_specs(1, 5, 6),
+        flops=flops,
+    )
+
+    out_width = w_o.shape[1] // 2
+    half_rows = w_o.shape[0] // 2
+    asked = lax.dynamic_slice(
+        w_o, (sub * half_rows, (1 - mp) * out_width), (half_rows, out_width)
+    )
+    w_near = swap(asked, "mp")
+    w_far = swap(w_near, "sub")
+
+    final = [
+        call(
+            third_kernel,
+            scalars,
+            (*gather_parts(pair), gains, conv_weight),
+            [struct((2 * b, width))],
+            [hidden, pltpu.VMEM((2 * b, width), F32)],
+            grid=(3,),
+            specs=tap_specs(2, 4, 5, first=1),
+            flops=flops * 2 // 3,
+        )
+        for pair in pairs
+    ]
+
+    received = []
+    for pair in final:
+        halves = pair.reshape(2, b, width)
+        mine, theirs = pick(halves, sub), pick(halves, 1 - sub)
+        projected = call(
+            project_kernel,
+            scalars,
+            (mine, swap(theirs, "sub"), swap(mine, "mp"), swap_both(theirs), w_q, w_k, w_v),
+            [struct((n, b, 3 * HEAD))],
+            [pltpu.VMEM((b, channels), BF16)],
+            flops=2 * b * channels * 3 * n * HEAD,
+        )
+        received.append(pick(projected, z))
+        for s in range(1, n):
+            received.append(rotate(pick(projected, lax.rem(z + s, n)), s))
+    swapped = [swap(x, "sub") for x in received]
+    attended = call(
+        attend_kernel,
+        scalars,
+        (*received, *swapped),
+        [struct((n, 2 * b, HEAD))],
+        [
+            pltpu.VMEM((2, 2, n, b, HEAD), BF16),
+            pltpu.VMEM((16 * b, HEAD), BF16),
+            pltpu.VMEM((16 * b, HEAD), BF16),
+        ],
+        flops=4 * 8 * b * 16 * b * HEAD,
+    )
+
+    kept = [final[0][:b], final[1][:b], final[0][b:], final[1][b:]]
+    kept = jnp.stack(kept)
+    rest = []
+    for s in range(n):
+        steps = [(2 * (i % 2) + j + s) % n for i in range(n) for j in range(2)]
+        pairs_of = [(i * 2 + j, steps[i * 2 + j] * 2 + i // 2) for i in range(n) for j in range(2)]
+        target = lax.rem(2 * lax.rem(z, 2) + sub + s, n)
+        rest.append(lax.ppermute(pick(kept, target), ("seq", "sub"), pairs_of))
+
+    heads = [pick(attended, z)]
+    for s in range(1, n):
+        heads.append(rotate(pick(attended, lax.rem(z + s, n)), s))
+    others = [swap(x, "mp") for x in heads]
+    args = (*heads, *others, *rest, w_o, w_near, w_far)
+    return call(
+        finish_kernel,
+        scalars,
+        args,
+        [struct((2 * b, out_width))],
+        [pltpu.VMEM((2 * b, 8 * HEAD), BF16), pltpu.VMEM((2 * b, out_width), BF16)],
+        specs={12: pl.BlockSpec((n * HEAD, out_width), lambda i, ids: (0, ids[10]))},
+        flops=2 * 2 * b * 8 * HEAD * out_width,
+    )
 
 
 def passed_along(x, axis, by):
@@ -109,8 +525,10 @@
         P(None, "mp"),
         P("mp", None),
     )
+    sizes = dict(mesh.shape)
+    dealt = sizes["seq"] == 4 and sizes["mp"] == 2 and sizes["sub"] == 2
     return jax.shard_map(
-        per_device,
+        per_device_fast if dealt else per_device,
         mesh=mesh,
         in_specs=placed,
         out_specs=P(("groups", "seq", "sub"), "mp"),

time: 253 us -> 145 us (0.57)
  waiting for transfers between devices: 157 us -> 37.8 us
  starting transfers between devices: 19.2 us -> 61 us
  Pallas kernels: 0 us -> 41.3 us
  matrix products: 34.3 us -> 0 us
  between operations: 13.7 us -> 0.46 us
  other arithmetic: 9.91 us -> 0.11 us
  blocking collectives: 9.14 us -> 0 us
  local copies, waits for them, and re-layouts: 9.22 us -> 3.91 us
    all_gather x6 -> x0, waiting for transfers between devices: 98.6 us -> none  [the longest x3 60.7 us: tower_section(): gathered = lax.all_gather(stream_shard, ('mp', 'sub'), axis=1, tiled=True)]
    ppermute x6 -> x56, starting transfers between devices: 15.1 us -> 61 us  [the longest x12 24 us: rotate(): return lax.ppermute(x, 'seq', [(i, (i + by) % n) for i in range(n)])]
    pallas_call x0 -> x10, Pallas kernels: none -> 41.3 us  [call(): pl.pallas_call(kernel, out_shape=outs[0] if single else outs, grid_spec=p...]
    dot_general x9 -> x0, matrix products: 34.3 us -> none  [the longest x3 16.9 us: tower_section(): jnp.einsum('rc,jco->jro', hidden, weight_taps, preferred_element_type=jnp...]
    all_to_all x1 -> x0, waiting for transfers between devices: 19.9 us -> none  [per_device(): lax.all_to_all(w_o, 'mp', split_axis=1, concat_axis=0, tiled=True)]
    all_gather x1 -> x0, blocking collectives: 9.14 us -> none  [per_device(): every_head = lax.all_gather(attended, 'mp', axis=1, tiled=True)]
    reduce_sum x4 -> x0, other arithmetic: 6.99 us -> none  [the longest x3 5.37 us: tower_section(): jnp.mean(widened * widened, axis=1, keepdims=True) + 1e-06]
    unnamed x15 -> x9, local copies, waits for them, and re-layouts: 4.83 us -> 0.04 us
  transfers between devices with their start and end apart: 13 -> 56, of which waited for: 12 -> 18; matrix products, arithmetic and copies ran while one was open for 6% -> 2% of each run, Pallas kernels for 0% -> 20%
where the time goes in v1:
time: 145 us
  starting transfers between devices  61 us (42%)
  Pallas kernels  41.3 us (28%)
  waiting for transfers between devices  37.8 us (26%)
  local copies, waits for them, and re-layouts  3.91 us (3%)
    pallas_call x10, Pallas kernels, call(): pl.pallas_call(kernel, out_shape=outs[0] if single else outs, grid_spec=p...  41.3 us
    ppermute x36, waiting for transfers between devices, swap(): return lax.ppermute(x, axis, [(0, 1), (1, 0)])  24.9 us
    ppermute x12, starting transfers between devices, rotate(): return lax.ppermute(x, 'seq', [(i, (i + by) % n) for i in range(n)])  24 us
    ppermute x36, starting transfers between devices, swap(): return lax.ppermute(x, axis, [(0, 1), (1, 0)])  19.3 us
    ppermute x4, starting transfers between devices, per_device_fast(): rest.append(lax.ppermute(pick(kept, target), ('seq', 'sub'), pairs_of))  10.6 us
    ppermute x12, waiting for transfers between devices, rotate(): return lax.ppermute(x, 'seq', [(i, (i + by) % n) for i in range(n)])  7.42 us
    ppermute x1, waiting for transfers between devices, per_device_fast(): upper = lax.ppermute(down, 'seq', [(i + 1, i) for i in range(n - 1)])  4.12 us
    ppermute x1, starting transfers between devices, per_device_fast(): lower = lax.ppermute(up, 'seq', [(i, i + 1) for i in range(n - 1)])  3.73 us
  transfers between devices with their start and end apart: 56, of which 18 were waited for; matrix products, arithmetic and copies ran while one was open for 2% of the time, Pallas kernels for 20%

profile of v1, /device:TPU:0, one launch (start us, length us, event | category | flops | bytes accessed | tf_op | source)
XLA Modules:
  0.0 144.5 jit_solution(11386805362787731055)
XLA Ops:
  0.0 1.0 fusion
  1.0 3.0 %collective-permute-start.4 = (bf16[256,384]{1,0:T(8,128)(2,1)S(1)}, bf16[256,384]{1,0:T(8,128)(2,1)S(1)}, u32[]{:S(2)}, u32[]{:S(2)}) collective-permute-start(bf16[256,384]{1,0:T(8,128)(2,1)S(1)} %pad_maximum_fusion.1.p0.edge), channel_id=1, source_target_pairs={{0,2},{2,0},{1,3},{3,1},{4,6},{6,4},{5,7},{7,5},{8,10},{10,8},{9,1... | collective-permute-start | bytes 589832 | tf_op jit(solution)/shard_map/ppermute | solution.py:20
  5.1 4.6 %collective-permute-done.4.p2 = bf16[256,384]{1,0:T(8,128)(2,1)S(1)} collective-permute-done((bf16[256,384]{1,0:T(8,128)(2,1)S(1)}, bf16[256,384]{1,0:T(8,128)(2,1)S(1)}, u32[]{:S(2)}, u32[]{:S(2)}) %collective-permute-start.4) | collective-permute-done | bytes 196640 | tf_op jit(solution)/shard_map/ppermute | solution.py:20
  10.2 2.9 %collective-permute-done.1.p2 = bf16[256,384]{1,0:T(8,128)(2,1)S(1)} collective-permute-done((bf16[256,384]{1,0:T(8,128)(2,1)S(1)}, bf16[256,384]{1,0:T(8,128)(2,1)S(1)}, u32[]{:S(2)}, u32[]{:S(2)}) %collective-permute-start.1) | collective-permute-done | bytes 196640 | tf_op jit(solution)/shard_map/ppermute | solution.py:20
  14.0 5.4 %first_edge_kernel.1 = (f32[4,128,384]{2,1,0:T(8,128)S(1)}, bf16[128,384]{1,0:T(8,128)(2,1)S(1)}, bf16[128,384]{1,0:T(8,128)(2,1)S(1)}) custom-call(s32[11]{0:T(128)S(1)} %stack.62.scalars, bf16[256,384]{1,0:T(8,128)(2,1)S(1)} %pad_maximum_fusion.1.p0.edge, bf16[256,384]{1,0:T(8,128)(2,1)S(1)} %collective-permute-done.3.p1, ...), custom_call_target="tpu_custom_call" | custom-call | flops 905969664 | bytes 1769472 | tf_op jit(solution)/shard_map/first_edge_kernel/pallas_call | solution.py:247
  19.4 3.7 %collective-permute-start.6 = (bf16[128,384]{1,0:T(8,128)(2,1)S(1)}, bf16[128,384]{1,0:T(8,128)(2,1)S(1)}, u32[]{:S(2)}, u32[]{:S(2)}) collective-permute-start(bf16[128,384]{1,0:T(8,128)(2,1)S(1)} %get-tuple-element.11), channel_id=1, source_target_pairs={{0,4},{4,8},{8,12},{1,5},{5,9},{9,13},{2,6},{6,10},{10,14},{3,7},{... | collective-permute-start | bytes 294920 | tf_op jit(solution)/shard_map/ppermute | solution.py:311
  23.1 1.3 collective-permute-start.7
  24.5 1.4 collective-permute-done.6.lower
  25.8 4.1 %collective-permute-done.7.upper = bf16[128,384]{1,0:T(8,128)(2,1)S(1)} collective-permute-done((bf16[128,384]{1,0:T(8,128)(2,1)S(1)}, bf16[128,384]{1,0:T(8,128)(2,1)S(1)}, u32[]{:S(2)}, u32[]{:S(2)}) %collective-permute-start.7) | collective-permute-done | bytes 98336 | tf_op jit(solution)/shard_map/ppermute | solution.py:312
  29.9 5.5 %first_middle_kernel.1 = bf16[4,128,384]{2,1,0:T(8,128)(2,1)S(1)} custom-call(s32[11]{0:T(128)S(1)} %stack.62.scalars, bf16[256,384]{1,0:T(8,128)(2,1)S(1)} %slice.21.p0, bf16[256,384]{1,0:T(8,128)(2,1)S(1)} %collective-permute-done.p1, bf16[256,384]{1,0:T(8,128)(2,1)S(1)} %collective-permute-done.1.p2, bf16[256,384]{1,0:T(8,128)(2,1)S(1)} %collective-permute-done.2.p3, ...), custom_call_target="tpu_custom_call" | custom-call | flops 905969664 | bytes 2359296 | tf_op jit(solution)/shard_map/first_middle_kernel/pallas_call | solution.py:247
  35.5 1.6 %collective-permute-start.13 = (bf16[128,384]{1,0:T(8,128)(2,1)S(1)}, bf16[128,384]{1,0:T(8,128)(2,1)S(1)}, u32[]{:S(2)}, u32[]{:S(2)}) collective-permute-start(bf16[128,384]{1,0:T(8,128)(2,1)S(1)} %get-tuple-element.28), channel_id=1, source_target_pairs={{0,4},{4,8},{8,12},{12,0},{1,5},{5,9},{9,13},{13,1},{2,6},{6,10},{... | collective-permute-start | bytes 294920 | tf_op jit(solution)/shard_map/ppermute | solution.py:29
  37.1 1.1 collective-permute-start.8
  38.2 2.8 %collective-permute-start.9 = (bf16[128,384]{1,0:T(8,128)(2,1)S(1)}, bf16[128,384]{1,0:T(8,128)(2,1)S(1)}, u32[]{:S(2)}, u32[]{:S(2)}) collective-permute-start(bf16[128,384]{1,0:T(8,128)(2,1)S(1)} %get-tuple-element.29), channel_id=1, source_target_pairs={{0,12},{4,0},{8,4},{12,8},{1,13},{5,1},{9,5},{13,9},{2,14},{6,2},{... | collective-permute-start | bytes 294920 | tf_op jit(solution)/shard_map/ppermute | solution.py:29
  41.0 2.0 %collective-permute-done.13 = bf16[128,384]{1,0:T(8,128)(2,1)S(1)} collective-permute-done((bf16[128,384]{1,0:T(8,128)(2,1)S(1)}, bf16[128,384]{1,0:T(8,128)(2,1)S(1)}, u32[]{:S(2)}, u32[]{:S(2)}) %collective-permute-start.13) | collective-permute-done | bytes 98336 | tf_op jit(solution)/shard_map/ppermute | solution.py:29
  43.1 1.6 %collective-permute-start.15 = (bf16[256,384]{1,0:T(8,128)(2,1)S(1)}, bf16[256,384]{1,0:T(8,128)(2,1)S(1)}, u32[]{:S(2)}, u32[]{:S(2)}) collective-permute-start(bf16[256,384]{1,0:T(8,128)(2,1)S(1)} %pad_maximum_fusion.2.p0.early), channel_id=1, source_target_pairs={{0,2},{2,0},{1,3},{3,1},{4,6},{6,4},{5,7},{7,5},{8,10},{10,8},{9,1... | collective-permute-start | bytes 589832 | tf_op jit(solution)/shard_map/ppermute | solution.py:20
  44.6 1.5 %collective-permute-done.8 = bf16[128,384]{1,0:T(8,128)(2,1)S(1)} collective-permute-done((bf16[128,384]{1,0:T(8,128)(2,1)S(1)}, bf16[128,384]{1,0:T(8,128)(2,1)S(1)}, u32[]{:S(2)}, u32[]{:S(2)}) %collective-permute-start.8) | collective-permute-done | bytes 98336 | tf_op jit(solution)/shard_map/ppermute | solution.py:29
  46.1 1.6 %collective-permute-start.11 = (bf16[256,384]{1,0:T(8,128)(2,1)S(1)}, bf16[256,384]{1,0:T(8,128)(2,1)S(1)}, u32[]{:S(2)}, u32[]{:S(2)}) collective-permute-start(bf16[256,384]{1,0:T(8,128)(2,1)S(1)} %constant_dynamic-update-slice_fusion.p0), channel_id=1, source_target_pairs={{0,2},{2,0},{1,3},{3,1},{4,6},{6,4},{5,7},{7,5},{8,10},{10,8},{9,1... | collective-permute-start | bytes 589832 | tf_op jit(solution)/shard_map/ppermute | solution.py:20
  47.7 1.8 %collective-permute-done.15.p2 = bf16[256,384]{1,0:T(8,128)(2,1)S(1)} collective-permute-done((bf16[256,384]{1,0:T(8,128)(2,1)S(1)}, bf16[256,384]{1,0:T(8,128)(2,1)S(1)}, u32[]{:S(2)}, u32[]{:S(2)}) %collective-permute-start.15) | collective-permute-done | bytes 196640 | tf_op jit(solution)/shard_map/ppermute | solution.py:20
  50.0 3.0 %collective-permute-done.11.p2 = bf16[256,384]{1,0:T(8,128)(2,1)S(1)} collective-permute-done((bf16[256,384]{1,0:T(8,128)(2,1)S(1)}, bf16[256,384]{1,0:T(8,128)(2,1)S(1)}, u32[]{:S(2)}, u32[]{:S(2)}) %collective-permute-start.11) | collective-permute-done | bytes 196640 | tf_op jit(solution)/shard_map/ppermute | solution.py:20
  53.0 5.4 %second_early_kernel.1.acc_in = f32[6,128,384]{2,1,0:T(8,128)S(1)} custom-call(s32[11]{0:T(128)S(1)} %stack.62.scalars, bf16[256,384]{1,0:T(8,128)(2,1)S(1)} %pad_maximum_fusion.2.p0.early, bf16[256,384]{1,0:T(8,128)(2,1)S(1)} %collective-permute-done.14.p1, bf16[256,384]{1,0:T(8,128)(2,1)S(1)} %collective-permute-done.15.p2, ...), custom_call_target="tpu_custom_call" | custom-call | flops 905969664 | bytes 1966080 | tf_op jit(solution)/shard_map/second_early_kernel/pallas_call | solution.py:247
  58.5 5.5 %second_late_kernel.1 = (bf16[256,384]{1,0:T(8,128)(2,1)S(1)}, bf16[256,384]{1,0:T(8,128)(2,1)S(1)}) custom-call(s32[11]{0:T(128)S(1)} %stack.62.scalars, bf16[256,384]{1,0:T(8,128)(2,1)S(1)} %constant_dynamic-update-slice_fusion.p0, bf16[256,384]{1,0:T(8,128)(2,1)S(1)} %collective-permute-done.10.p1, bf16[256,384]{1,0:T(8,128)(2,1)S(1)} %collective-permute-done.11.p2, ...), custom_call_target="tpu_custom_call" | custom-call | flops 905969664 | bytes 2555904 | tf_op jit(solution)/shard_map/second_late_kernel/pallas_call | solution.py:247
  64.0 1.6 %collective-permute-start.27 = (bf16[256,384]{1,0:T(8,128)(2,1)S(1)}, bf16[256,384]{1,0:T(8,128)(2,1)S(1)}, u32[]{:S(2)}, u32[]{:S(2)}) collective-permute-start(bf16[256,384]{1,0:T(8,128)(2,1)S(1)} %get-tuple-element.14.p0), channel_id=1, source_target_pairs={{0,2},{2,0},{1,3},{3,1},{4,6},{6,4},{5,7},{7,5},{8,10},{10,8},{9,1... | collective-permute-start | bytes 589832 | tf_op jit(solution)/shard_map/ppermute | solution.py:20
  66.1 5.7 %collective-permute-done.27.p2 = bf16[256,384]{1,0:T(8,128)(2,1)S(1)} collective-permute-done((bf16[256,384]{1,0:T(8,128)(2,1)S(1)}, bf16[256,384]{1,0:T(8,128)(2,1)S(1)}, u32[]{:S(2)}, u32[]{:S(2)}) %collective-permute-start.27) | collective-permute-done | bytes 196640 | tf_op jit(solution)/shard_map/ppermute | solution.py:20
  72.5 1.5 %collective-permute-start.54 = (bf16[256,768]{1,0:T(8,128)(2,1)}, bf16[256,768]{1,0:T(8,128)(2,1)S(1)}, u32[]{:S(2)}, u32[]{:S(2)}) collective-permute-start(bf16[256,768]{1,0:T(8,128)(2,1)} %dynamic_slice.102), channel_id=1, source_target_pairs={{0,2},{2,0},{1,3},{3,1},{4,6},{6,4},{5,7},{7,5},{8,10},{10,8},{9,1... | collective-permute-start | bytes 1179656 | tf_op jit(solution)/shard_map/ppermute | solution.py:20
  74.2 1.3 collective-permute-done.18.p2
  75.6 4.9 %third_kernel.3 = bf16[256,384]{1,0:T(8,128)(2,1)S(1)} custom-call(s32[11]{0:T(128)S(1)} %stack.62.scalars, bf16[256,384]{1,0:T(8,128)(2,1)S(1)} %get-tuple-element.14.p0, bf16[256,384]{1,0:T(8,128)(2,1)S(1)} %collective-permute-done.26.p1, bf16[256,384]{1,0:T(8,128)(2,1)S(1)} %collective-permute-done.27.p2, ...), custom_call_target="tpu_custom_call" | custom-call | flops 603979776 | bytes 983040 | tf_op jit(solution)/shard_map/third_kernel/pallas_call | solution.py:247
  81.1 1.2 collective-permute-start.31
  83.0 5.2 %third_kernel.2 = bf16[256,384]{1,0:T(8,128)(2,1)S(1)} custom-call(s32[11]{0:T(128)S(1)} %stack.62.scalars, bf16[256,384]{1,0:T(8,128)(2,1)S(1)} %get-tuple-element.13.p0, bf16[256,384]{1,0:T(8,128)(2,1)S(1)} %collective-permute-done.17.p1, bf16[256,384]{1,0:T(8,128)(2,1)S(1)} %collective-permute-done.18.p2, ...), custom_call_target="tpu_custom_call" | custom-call | flops 603979776 | bytes 983040 | tf_op jit(solution)/shard_map/third_kernel/pallas_call | solution.py:247
  88.7 1.0 collective-permute-start.22
  90.4 1.3 project_kernel.3
  91.9 2.6 %collective-permute-start.32 = (bf16[128,384]{1,0:T(8,128)(2,1)S(1)}, bf16[128,384]{1,0:T(8,128)(2,1)S(1)}, u32[]{:S(2)}, u32[]{:S(2)}) collective-permute-start(bf16[128,384]{1,0:T(8,128)(2,1)S(1)} %get-tuple-element.21), channel_id=1, source_target_pairs={{0,4},{4,8},{8,12},{12,0},{1,5},{5,9},{9,13},{13,1},{2,6},{6,10},{... | collective-permute-start | bytes 294920 | tf_op jit(solution)/shard_map/ppermute | solution.py:29
  95.9 2.2 %collective-permute-start.34 = (bf16[128,384]{1,0:T(8,128)(2,1)S(1)}, bf16[128,384]{1,0:T(8,128)(2,1)S(1)}, u32[]{:S(2)}, u32[]{:S(2)}) collective-permute-start(bf16[128,384]{1,0:T(8,128)(2,1)S(1)} %get-tuple-element.19), channel_id=1, source_target_pairs={{0,12},{4,0},{8,4},{12,8},{1,13},{5,1},{9,5},{13,9},{2,14},{6,2},{... | collective-permute-start | bytes 294920 | tf_op jit(solution)/shard_map/ppermute | solution.py:29
  98.1 1.3 project_kernel.2
  99.9 4.7 %collective-permute-start.24 = (bf16[128,384]{1,0:T(8,128)(2,1)S(1)}, bf16[128,384]{1,0:T(8,128)(2,1)S(1)}, u32[]{:S(2)}, u32[]{:S(2)}) collective-permute-start(bf16[128,384]{1,0:T(8,128)(2,1)S(1)} %get-tuple-element.24), channel_id=1, source_target_pairs={{0,8},{4,12},{8,0},{12,4},{1,9},{5,13},{9,1},{13,5},{2,10},{6,14},... | collective-permute-start | bytes 294920 | tf_op jit(solution)/shard_map/ppermute | solution.py:29
  104.8 4.1 %collective-permute-start.25 = (bf16[128,384]{1,0:T(8,128)(2,1)S(1)}, bf16[128,384]{1,0:T(8,128)(2,1)S(1)}, u32[]{:S(2)}, u32[]{:S(2)}) collective-permute-start(bf16[128,384]{1,0:T(8,128)(2,1)S(1)} %get-tuple-element.23), channel_id=1, source_target_pairs={{0,12},{4,0},{8,4},{12,8},{1,13},{5,1},{9,5},{13,9},{2,14},{6,2},{... | collective-permute-start | bytes 294920 | tf_op jit(solution)/shard_map/ppermute | solution.py:29
  109.3 2.0 %collective-permute-done.24.refs_2_ = bf16[128,384]{1,0:T(8,128)(2,1)S(1)} collective-permute-done((bf16[128,384]{1,0:T(8,128)(2,1)S(1)}, bf16[128,384]{1,0:T(8,128)(2,1)S(1)}, u32[]{:S(2)}, u32[]{:S(2)}) %collective-permute-start.24) | collective-permute-done | bytes 98336 | tf_op jit(solution)/shard_map/ppermute | solution.py:29
  111.4 2.0 %collective-permute-done.25.refs_3_ = bf16[128,384]{1,0:T(8,128)(2,1)S(1)} collective-permute-done((bf16[128,384]{1,0:T(8,128)(2,1)S(1)}, bf16[128,384]{1,0:T(8,128)(2,1)S(1)}, u32[]{:S(2)}, u32[]{:S(2)}) %collective-permute-start.25) | collective-permute-done | bytes 98336 | tf_op jit(solution)/shard_map/ppermute | solution.py:29
  115.3 4.2 %collective-permute-start.51 = (bf16[128,384]{1,0:T(8,128)(2,1)S(1)}, bf16[128,384]{1,0:T(8,128)(2,1)S(1)}, u32[]{:S(2)}, u32[]{:S(2)}) collective-permute-start(bf16[128,384]{1,0:T(8,128)(2,1)S(1)} %get-tuple-element.17), channel_id=1, source_target_pairs={{0,4},{1,8},{4,12},{5,0},{8,5},{9,9},{12,13},{13,1},{2,6},{3,10},{... | collective-permute-start | bytes 294920 | tf_op jit(solution)/shard_map/ppermute | solution.py:411
  119.6 3.2 %collective-permute-start.52 = (bf16[128,384]{1,0:T(8,128)(2,1)S(1)}, bf16[128,384]{1,0:T(8,128)(2,1)S(1)}, u32[]{:S(2)}, u32[]{:S(2)}) collective-permute-start(bf16[128,384]{1,0:T(8,128)(2,1)S(1)} %get-tuple-element.16), channel_id=1, source_target_pairs={{0,8},{1,12},{4,0},{5,4},{8,9},{9,13},{12,1},{13,5},{2,10},{3,14},... | collective-permute-start | bytes 294920 | tf_op jit(solution)/shard_map/ppermute | solution.py:411
  122.8 4.8 %attend_kernel.1 = bf16[4,256,128]{2,1,0:T(8,128)(2,1)S(1)} custom-call(s32[11]{0:T(128)S(1)} %stack.62.scalars, bf16[128,384]{1,0:T(8,128)(2,1)S(1)} %get-tuple-element.26.refs_0_, bf16[128,384]{1,0:T(8,128)(2,1)S(1)} %collective-permute-done.23.refs_1_, bf16[128,384]{1,0:T(8,128)(2,1)S(1)} %collective-permute-done.24.refs_2_, ...), custom_call_target="tpu_custom_call" | custom-call | flops 1073741824 | bytes 1835008 | tf_op jit(solution)/shard_map/attend_kernel/pallas_call | solution.py:247
  127.7 2.6 %collective-permute-start.44 = (bf16[256,128]{1,0:T(8,128)(2,1)S(1)}, bf16[256,128]{1,0:T(8,128)(2,1)S(1)}, u32[]{:S(2)}, u32[]{:S(2)}) collective-permute-start(bf16[256,128]{1,0:T(8,128)(2,1)S(1)} %get-tuple-element.34), channel_id=1, source_target_pairs={{0,8},{4,12},{8,0},{12,4},{1,9},{5,13},{9,1},{13,5},{2,10},{6,14},... | collective-permute-start | bytes 196616 | tf_op jit(solution)/shard_map/ppermute | solution.py:29
  130.2 1.3 collective-permute-start.45
  131.5 2.5 %collective-permute-start.53 = (bf16[128,384]{1,0:T(8,128)(2,1)S(1)}, bf16[128,384]{1,0:T(8,128)(2,1)S(1)}, u32[]{:S(2)}, u32[]{:S(2)}) collective-permute-start(bf16[128,384]{1,0:T(8,128)(2,1)S(1)} %get-tuple-element.15), channel_id=1, source_target_pairs={{0,12},{1,0},{4,4},{5,8},{8,13},{9,1},{12,5},{13,9},{2,14},{3,2},{... | collective-permute-start | bytes 294920 | tf_op jit(solution)/shard_map/ppermute | solution.py:411
  134.0 1.4 collective-permute-start.46
  136.1 1.3 collective-permute-start.48
  139.1 1.4 collective-permute-done.47.refs_5_
  140.5 1.4 collective-permute-done.48.refs_6_
  142.5 2.0 %finish_kernel.1 = bf16[256,768]{1,0:T(8,128)(2,1)} custom-call(s32[11]{0:T(128)S(1)} %stack.62.scalars, bf16[256,128]{1,0:T(8,128)(2,1)S(1)} %get-tuple-element.36.refs_0_, bf16[256,128]{1,0:T(8,128)(2,1)S(1)} %collective-permute-done.43.refs_1_, bf16[256,128]{1,0:T(8,128)(2,1)S(1)} %collective-permute-done.44.refs_2_, ...), custom_call_target="tpu_custom_call" | custom-call | flops 402653184 | bytes 2097152 | tf_op jit(solution)/shard_map/finish_kernel/pallas_call | solution.py:247
  (101 shorter events, 14.9 us)
Async XLA Ops:
  1.0 8.7 %collective-permute-start.4 = (bf16[256,384]{1,0:T(8,128)(2,1)S(1)}, bf16[256,384]{1,0:T(8,128)(2,1)S(1)}, u32[]{:S(2)}, u32[]{:S(2)}) collective-permute-start(bf16[256,384]{1,0:T(8,128)(2,1)S(1)} %pad_maximum_fusion.1.p0.edge), channel_id=1, source_target_pairs={{0,2},{2,0},{1,3},{3,1},{4,6},{6,4},{5,7},{7,5},{8,10},{10,8},{9,1... | collective-permute-start | bytes 589832 | tf_op jit(solution)/shard_map/ppermute | solution.py:20
  4.9 8.2 %collective-permute-start.1 = (bf16[256,384]{1,0:T(8,128)(2,1)S(1)}, bf16[256,384]{1,0:T(8,128)(2,1)S(1)}, u32[]{:S(2)}, u32[]{:S(2)}) collective-permute-start(bf16[256,384]{1,0:T(8,128)(2,1)S(1)} %slice.21.p0), channel_id=1, source_target_pairs={{0,2},{2,0},{1,3},{3,1},{4,6},{6,4},{5,7},{7,5},{8,10},{10,8},{9,1... | collective-permute-start | bytes 589832 | tf_op jit(solution)/shard_map/ppermute | solution.py:20
  5.0 8.9 %collective-permute-start.3 = (bf16[256,384]{1,0:T(8,128)(2,1)S(1)}, bf16[256,384]{1,0:T(8,128)(2,1)S(1)}, u32[]{:S(2)}, u32[]{:S(2)}) collective-permute-start(bf16[256,384]{1,0:T(8,128)(2,1)S(1)} %pad_maximum_fusion.1.p0.edge), channel_id=1, source_target_pairs={{0,1},{1,0},{2,3},{3,2},{4,5},{5,4},{6,7},{7,6},{8,9},{9,8},{10,11... | collective-permute-start | bytes 589832 | tf_op jit(solution)/shard_map/ppermute | solution.py:20
  9.7 14.7 %collective-permute-start = (bf16[256,384]{1,0:T(8,128)(2,1)S(1)}, bf16[256,384]{1,0:T(8,128)(2,1)S(1)}, u32[]{:S(2)}, u32[]{:S(2)}) collective-permute-start(bf16[256,384]{1,0:T(8,128)(2,1)S(1)} %slice.21.p0), channel_id=1, source_target_pairs={{0,1},{1,0},{2,3},{3,2},{4,5},{5,4},{6,7},{7,6},{8,9},{9,8},{10,11... | collective-permute-start | bytes 589832 | tf_op jit(solution)/shard_map/ppermute | solution.py:20
  13.1 11.3 %collective-permute-start.2 = (bf16[256,384]{1,0:T(8,128)(2,1)S(1)}, bf16[256,384]{1,0:T(8,128)(2,1)S(1)}, u32[]{:S(2)}, u32[]{:S(2)}) collective-permute-start(bf16[256,384]{1,0:T(8,128)(2,1)S(1)} %collective-permute-done.1.p2), channel_id=1, source_target_pairs={{0,1},{1,0},{2,3},{3,2},{4,5},{5,4},{6,7},{7,6},{8,9},{9,8},{10,11... | collective-permute-start | bytes 589832 | tf_op jit(solution)/shard_map/ppermute | solution.py:20
  19.4 6.4 %collective-permute-start.6 = (bf16[128,384]{1,0:T(8,128)(2,1)S(1)}, bf16[128,384]{1,0:T(8,128)(2,1)S(1)}, u32[]{:S(2)}, u32[]{:S(2)}) collective-permute-start(bf16[128,384]{1,0:T(8,128)(2,1)S(1)} %get-tuple-element.11), channel_id=1, source_target_pairs={{0,4},{4,8},{8,12},{1,5},{5,9},{9,13},{2,6},{6,10},{10,14},{3,7},{... | collective-permute-start | bytes 294920 | tf_op jit(solution)/shard_map/ppermute | solution.py:311
  23.1 6.8 %collective-permute-start.7 = (bf16[128,384]{1,0:T(8,128)(2,1)S(1)}, bf16[128,384]{1,0:T(8,128)(2,1)S(1)}, u32[]{:S(2)}, u32[]{:S(2)}) collective-permute-start(bf16[128,384]{1,0:T(8,128)(2,1)S(1)} %get-tuple-element.12), channel_id=1, source_target_pairs={{4,0},{8,4},{12,8},{5,1},{9,5},{13,9},{6,2},{10,6},{14,10},{7,3},{... | collective-permute-start | bytes 294920 | tf_op jit(solution)/shard_map/ppermute | solution.py:312
  35.5 7.6 %collective-permute-start.13 = (bf16[128,384]{1,0:T(8,128)(2,1)S(1)}, bf16[128,384]{1,0:T(8,128)(2,1)S(1)}, u32[]{:S(2)}, u32[]{:S(2)}) collective-permute-start(bf16[128,384]{1,0:T(8,128)(2,1)S(1)} %get-tuple-element.28), channel_id=1, source_target_pairs={{0,4},{4,8},{8,12},{12,0},{1,5},{5,9},{9,13},{13,1},{2,6},{6,10},{... | collective-permute-start | bytes 294920 | tf_op jit(solution)/shard_map/ppermute | solution.py:29
  37.1 9.0 %collective-permute-start.8 = (bf16[128,384]{1,0:T(8,128)(2,1)S(1)}, bf16[128,384]{1,0:T(8,128)(2,1)S(1)}, u32[]{:S(2)}, u32[]{:S(2)}) collective-permute-start(bf16[128,384]{1,0:T(8,128)(2,1)S(1)} %get-tuple-element.30), channel_id=1, source_target_pairs={{0,8},{4,12},{8,0},{12,4},{1,9},{5,13},{9,1},{13,5},{2,10},{6,14},... | collective-permute-start | bytes 294920 | tf_op jit(solution)/shard_map/ppermute | solution.py:29
  38.2 7.9 %collective-permute-start.9 = (bf16[128,384]{1,0:T(8,128)(2,1)S(1)}, bf16[128,384]{1,0:T(8,128)(2,1)S(1)}, u32[]{:S(2)}, u32[]{:S(2)}) collective-permute-start(bf16[128,384]{1,0:T(8,128)(2,1)S(1)} %get-tuple-element.29), channel_id=1, source_target_pairs={{0,12},{4,0},{8,4},{12,8},{1,13},{5,1},{9,5},{13,9},{2,14},{6,2},{... | collective-permute-start | bytes 294920 | tf_op jit(solution)/shard_map/ppermute | solution.py:29
  43.1 6.4 %collective-permute-start.15 = (bf16[256,384]{1,0:T(8,128)(2,1)S(1)}, bf16[256,384]{1,0:T(8,128)(2,1)S(1)}, u32[]{:S(2)}, u32[]{:S(2)}) collective-permute-start(bf16[256,384]{1,0:T(8,128)(2,1)S(1)} %pad_maximum_fusion.2.p0.early), channel_id=1, source_target_pairs={{0,2},{2,0},{1,3},{3,1},{4,6},{6,4},{5,7},{7,5},{8,10},{10,8},{9,1... | collective-permute-start | bytes 589832 | tf_op jit(solution)/shard_map/ppermute | solution.py:20
  46.1 6.9 %collective-permute-start.11 = (bf16[256,384]{1,0:T(8,128)(2,1)S(1)}, bf16[256,384]{1,0:T(8,128)(2,1)S(1)}, u32[]{:S(2)}, u32[]{:S(2)}) collective-permute-start(bf16[256,384]{1,0:T(8,128)(2,1)S(1)} %constant_dynamic-update-slice_fusion.p0), channel_id=1, source_target_pairs={{0,2},{2,0},{1,3},{3,1},{4,6},{6,4},{5,7},{7,5},{8,10},{10,8},{9,1... | collective-permute-start | bytes 589832 | tf_op jit(solution)/shard_map/ppermute | solution.py:20
  47.7 5.3 %collective-permute-start.14 = (bf16[256,384]{1,0:T(8,128)(2,1)S(1)}, bf16[256,384]{1,0:T(8,128)(2,1)S(1)}, u32[]{:S(2)}, u32[]{:S(2)}) collective-permute-start(bf16[256,384]{1,0:T(8,128)(2,1)S(1)} %pad_maximum_fusion.2.p0.early), channel_id=1, source_target_pairs={{0,1},{1,0},{2,3},{3,2},{4,5},{5,4},{6,7},{7,6},{8,9},{9,8},{10,11... | collective-permute-start | bytes 589832 | tf_op jit(solution)/shard_map/ppermute | solution.py:20
  49.5 9.0 %collective-permute-start.10 = (bf16[256,384]{1,0:T(8,128)(2,1)S(1)}, bf16[256,384]{1,0:T(8,128)(2,1)S(1)}, u32[]{:S(2)}, u32[]{:S(2)}) collective-permute-start(bf16[256,384]{1,0:T(8,128)(2,1)S(1)} %constant_dynamic-update-slice_fusion.p0), channel_id=1, source_target_pairs={{0,1},{1,0},{2,3},{3,2},{4,5},{5,4},{6,7},{7,6},{8,9},{9,8},{10,11... | collective-permute-start | bytes 589832 | tf_op jit(solution)/shard_map/ppermute | solution.py:20
  53.0 5.5 %collective-permute-start.12 = (bf16[256,384]{1,0:T(8,128)(2,1)S(1)}, bf16[256,384]{1,0:T(8,128)(2,1)S(1)}, u32[]{:S(2)}, u32[]{:S(2)}) collective-permute-start(bf16[256,384]{1,0:T(8,128)(2,1)S(1)} %collective-permute-done.11.p2), channel_id=1, source_target_pairs={{0,1},{1,0},{2,3},{3,2},{4,5},{5,4},{6,7},{7,6},{8,9},{9,8},{10,11... | collective-permute-start | bytes 589832 | tf_op jit(solution)/shard_map/ppermute | solution.py:20
  64.0 7.8 %collective-permute-start.27 = (bf16[256,384]{1,0:T(8,128)(2,1)S(1)}, bf16[256,384]{1,0:T(8,128)(2,1)S(1)}, u32[]{:S(2)}, u32[]{:S(2)}) collective-permute-start(bf16[256,384]{1,0:T(8,128)(2,1)S(1)} %get-tuple-element.14.p0), channel_id=1, source_target_pairs={{0,2},{2,0},{1,3},{3,1},{4,6},{6,4},{5,7},{7,5},{8,10},{10,8},{9,1... | collective-permute-start | bytes 589832 | tf_op jit(solution)/shard_map/ppermute | solution.py:20
  65.5 10.0 %collective-permute-start.18 = (bf16[256,384]{1,0:T(8,128)(2,1)S(1)}, bf16[256,384]{1,0:T(8,128)(2,1)S(1)}, u32[]{:S(2)}, u32[]{:S(2)}) collective-permute-start(bf16[256,384]{1,0:T(8,128)(2,1)S(1)} %get-tuple-element.13.p0), channel_id=1, source_target_pairs={{0,2},{2,0},{1,3},{3,1},{4,6},{6,4},{5,7},{7,5},{8,10},{10,8},{9,1... | collective-permute-start | bytes 589832 | tf_op jit(solution)/shard_map/ppermute | solution.py:20
  66.1 9.5 %collective-permute-start.26 = (bf16[256,384]{1,0:T(8,128)(2,1)S(1)}, bf16[256,384]{1,0:T(8,128)(2,1)S(1)}, u32[]{:S(2)}, u32[]{:S(2)}) collective-permute-start(bf16[256,384]{1,0:T(8,128)(2,1)S(1)} %get-tuple-element.14.p0), channel_id=1, source_target_pairs={{0,1},{1,0},{2,3},{3,2},{4,5},{5,4},{6,7},{7,6},{8,9},{9,8},{10,11... | collective-permute-start | bytes 589832 | tf_op jit(solution)/shard_map/ppermute | solution.py:20
  72.5 27.0 %collective-permute-start.54 = (bf16[256,768]{1,0:T(8,128)(2,1)}, bf16[256,768]{1,0:T(8,128)(2,1)S(1)}, u32[]{:S(2)}, u32[]{:S(2)}) collective-permute-start(bf16[256,768]{1,0:T(8,128)(2,1)} %dynamic_slice.102), channel_id=1, source_target_pairs={{0,2},{2,0},{1,3},{3,1},{4,6},{6,4},{5,7},{7,5},{8,10},{10,8},{9,1... | collective-permute-start | bytes 1179656 | tf_op jit(solution)/shard_map/ppermute | solution.py:20
  74.0 8.3 %collective-permute-start.17 = (bf16[256,384]{1,0:T(8,128)(2,1)S(1)}, bf16[256,384]{1,0:T(8,128)(2,1)S(1)}, u32[]{:S(2)}, u32[]{:S(2)}) collective-permute-start(bf16[256,384]{1,0:T(8,128)(2,1)S(1)} %get-tuple-element.13.p0), channel_id=1, source_target_pairs={{0,1},{1,0},{2,3},{3,2},{4,5},{5,4},{6,7},{7,6},{8,9},{9,8},{10,11... | collective-permute-start | bytes 589832 | tf_op jit(solution)/shard_map/ppermute | solution.py:20
  75.6 7.4 %collective-permute-start.19 = (bf16[256,384]{1,0:T(8,128)(2,1)S(1)}, bf16[256,384]{1,0:T(8,128)(2,1)S(1)}, u32[]{:S(2)}, u32[]{:S(2)}) collective-permute-start(bf16[256,384]{1,0:T(8,128)(2,1)S(1)} %collective-permute-done.18.p2), channel_id=1, source_target_pairs={{0,1},{1,0},{2,3},{3,2},{4,5},{5,4},{6,7},{7,6},{8,9},{9,8},{10,11... | collective-permute-start | bytes 589832 | tf_op jit(solution)/shard_map/ppermute | solution.py:20
  80.6 8.1 %collective-permute-start.29 = (bf16[128,384]{1,0:T(8,128)(2,1)S(1)}, bf16[128,384]{1,0:T(8,128)(2,1)S(1)}, u32[]{:S(2)}, u32[]{:S(2)}) collective-permute-start(bf16[128,384]{1,0:T(8,128)(2,1)S(1)} %get-tuple-element.41), channel_id=1, source_target_pairs={{0,1},{1,0},{2,3},{3,2},{4,5},{5,4},{6,7},{7,6},{8,9},{9,8},{10,11... | collective-permute-start | bytes 294920 | tf_op jit(solution)/shard_map/ppermute | solution.py:20
  81.1 9.3 %collective-permute-start.31 = (bf16[128,384]{1,0:T(8,128)(2,1)S(1)}, bf16[128,384]{1,0:T(8,128)(2,1)S(1)}, u32[]{:S(2)}, u32[]{:S(2)}) collective-permute-start(bf16[128,384]{1,0:T(8,128)(2,1)S(1)} %get-tuple-element.41), channel_id=1, source_target_pairs={{0,3},{1,2},{2,1},{3,0},{4,7},{5,6},{6,5},{7,4},{8,11},{9,10},{10,... | collective-permute-start | bytes 294920 | tf_op jit(solution)/shard_map/ppermute | solution.py:24
  82.4 7.3 %collective-permute-start.30 = (bf16[128,384]{1,0:T(8,128)(2,1)S(1)}, bf16[128,384]{1,0:T(8,128)(2,1)S(1)}, u32[]{:S(2)}, u32[]{:S(2)}) collective-permute-start(bf16[128,384]{1,0:T(8,128)(2,1)S(1)} %get-tuple-element.42.p0), channel_id=1, source_target_pairs={{0,2},{2,0},{1,3},{3,1},{4,6},{6,4},{5,7},{7,5},{8,10},{10,8},{9,1... | collective-permute-start | bytes 294920 | tf_op jit(solution)/shard_map/ppermute | solution.py:20
  88.2 6.3 %collective-permute-start.20 = (bf16[128,384]{1,0:T(8,128)(2,1)S(1)}, bf16[128,384]{1,0:T(8,128)(2,1)S(1)}, u32[]{:S(2)}, u32[]{:S(2)}) collective-permute-start(bf16[128,384]{1,0:T(8,128)(2,1)S(1)} %get-tuple-element.43), channel_id=1, source_target_pairs={{0,1},{1,0},{2,3},{3,2},{4,5},{5,4},{6,7},{7,6},{8,9},{9,8},{10,11... | collective-permute-start | bytes 294920 | tf_op jit(solution)/shard_map/ppermute | solution.py:20
  88.7 9.4 %collective-permute-start.22 = (bf16[128,384]{1,0:T(8,128)(2,1)S(1)}, bf16[128,384]{1,0:T(8,128)(2,1)S(1)}, u32[]{:S(2)}, u32[]{:S(2)}) collective-permute-start(bf16[128,384]{1,0:T(8,128)(2,1)S(1)} %get-tuple-element.43), channel_id=1, source_target_pairs={{0,3},{1,2},{2,1},{3,0},{4,7},{5,6},{6,5},{7,4},{8,11},{9,10},{10,... | collective-permute-start | bytes 294920 | tf_op jit(solution)/shard_map/ppermute | solution.py:24
  89.7 6.2 %collective-permute-start.21 = (bf16[128,384]{1,0:T(8,128)(2,1)S(1)}, bf16[128,384]{1,0:T(8,128)(2,1)S(1)}, u32[]{:S(2)}, u32[]{:S(2)}) collective-permute-start(bf16[128,384]{1,0:T(8,128)(2,1)S(1)} %get-tuple-element.44.p0), channel_id=1, source_target_pairs={{0,2},{2,0},{1,3},{3,1},{4,6},{6,4},{5,7},{7,5},{8,10},{10,8},{9,1... | collective-permute-start | bytes 294920 | tf_op jit(solution)/shard_map/ppermute | solution.py:20
  91.9 8.0 %collective-permute-start.32 = (bf16[128,384]{1,0:T(8,128)(2,1)S(1)}, bf16[128,384]{1,0:T(8,128)(2,1)S(1)}, u32[]{:S(2)}, u32[]{:S(2)}) collective-permute-start(bf16[128,384]{1,0:T(8,128)(2,1)S(1)} %get-tuple-element.21), channel_id=1, source_target_pairs={{0,4},{4,8},{8,12},{12,0},{1,5},{5,9},{9,13},{13,1},{2,6},{6,10},{... | collective-permute-start | bytes 294920 | tf_op jit(solution)/shard_map/ppermute | solution.py:29
  94.5 10.2 %collective-permute-start.33 = (bf16[128,384]{1,0:T(8,128)(2,1)S(1)}, bf16[128,384]{1,0:T(8,128)(2,1)S(1)}, u32[]{:S(2)}, u32[]{:S(2)}) collective-permute-start(bf16[128,384]{1,0:T(8,128)(2,1)S(1)} %get-tuple-element.20), channel_id=1, source_target_pairs={{0,8},{4,12},{8,0},{12,4},{1,9},{5,13},{9,1},{13,5},{2,10},{6,14},... | collective-permute-start | bytes 294920 | tf_op jit(solution)/shard_map/ppermute | solution.py:29
  95.9 8.8 %collective-permute-start.34 = (bf16[128,384]{1,0:T(8,128)(2,1)S(1)}, bf16[128,384]{1,0:T(8,128)(2,1)S(1)}, u32[]{:S(2)}, u32[]{:S(2)}) collective-permute-start(bf16[128,384]{1,0:T(8,128)(2,1)S(1)} %get-tuple-element.19), channel_id=1, source_target_pairs={{0,12},{4,0},{8,4},{12,8},{1,13},{5,1},{9,5},{13,9},{2,14},{6,2},{... | collective-permute-start | bytes 294920 | tf_op jit(solution)/shard_map/ppermute | solution.py:29
  98.1 10.7 %collective-permute-start.39 = (bf16[128,384]{1,0:T(8,128)(2,1)S(1)}, bf16[128,384]{1,0:T(8,128)(2,1)S(1)}, u32[]{:S(2)}, u32[]{:S(2)}) collective-permute-start(bf16[128,384]{1,0:T(8,128)(2,1)S(1)} %get-tuple-element.22.refs_4_), channel_id=1, source_target_pairs={{0,1},{1,0},{2,3},{3,2},{4,5},{5,4},{6,7},{7,6},{8,9},{9,8},{10,11... | collective-permute-start | bytes 294920 | tf_op jit(solution)/shard_map/ppermute | solution.py:20
  99.5 9.5 %collective-permute-start.23 = (bf16[128,384]{1,0:T(8,128)(2,1)S(1)}, bf16[128,384]{1,0:T(8,128)(2,1)S(1)}, u32[]{:S(2)}, u32[]{:S(2)}) collective-permute-start(bf16[128,384]{1,0:T(8,128)(2,1)S(1)} %get-tuple-element.25), channel_id=1, source_target_pairs={{0,4},{4,8},{8,12},{12,0},{1,5},{5,9},{9,13},{13,1},{2,6},{6,10},{... | collective-permute-start | bytes 294920 | tf_op jit(solution)/shard_map/ppermute | solution.py:29
  99.9 11.4 %collective-permute-start.24 = (bf16[128,384]{1,0:T(8,128)(2,1)S(1)}, bf16[128,384]{1,0:T(8,128)(2,1)S(1)}, u32[]{:S(2)}, u32[]{:S(2)}) collective-permute-start(bf16[128,384]{1,0:T(8,128)(2,1)S(1)} %get-tuple-element.24), channel_id=1, source_target_pairs={{0,8},{4,12},{8,0},{12,4},{1,9},{5,13},{9,1},{13,5},{2,10},{6,14},... | collective-permute-start | bytes 294920 | tf_op jit(solution)/shard_map/ppermute | solution.py:29
  104.7 23.0 %collective-permute-start.55 = (bf16[256,768]{1,0:T(8,128)(2,1)S(1)}, bf16[256,768]{1,0:T(8,128)(2,1)S(1)}, u32[]{:S(2)}, u32[]{:S(2)}) collective-permute-start(bf16[256,768]{1,0:T(8,128)(2,1)S(1)} %collective-permute-done.54.refs_13_), channel_id=1, source_target_pairs={{0,1},{1,0},{2,3},{3,2},{4,5},{5,4},{6,7},{7,6},{8,9},{9,8},{10,11... | collective-permute-start | bytes 1179656 | tf_op jit(solution)/shard_map/ppermute | solution.py:20
  104.8 8.6 %collective-permute-start.25 = (bf16[128,384]{1,0:T(8,128)(2,1)S(1)}, bf16[128,384]{1,0:T(8,128)(2,1)S(1)}, u32[]{:S(2)}, u32[]{:S(2)}) collective-permute-start(bf16[128,384]{1,0:T(8,128)(2,1)S(1)} %get-tuple-element.23), channel_id=1, source_target_pairs={{0,12},{4,0},{8,4},{12,8},{1,13},{5,1},{9,5},{13,9},{2,14},{6,2},{... | collective-permute-start | bytes 294920 | tf_op jit(solution)/shard_map/ppermute | solution.py:29
  113.9 5.7 %collective-permute-start.37 = (bf16[128,384]{1,0:T(8,128)(2,1)S(1)}, bf16[128,384]{1,0:T(8,128)(2,1)S(1)}, u32[]{:S(2)}, u32[]{:S(2)}) collective-permute-start(bf16[128,384]{1,0:T(8,128)(2,1)S(1)} %collective-permute-done.24.refs_2_), channel_id=1, source_target_pairs={{0,1},{1,0},{2,3},{3,2},{4,5},{5,4},{6,7},{7,6},{8,9},{9,8},{10,11... | collective-permute-start | bytes 294920 | tf_op jit(solution)/shard_map/ppermute | solution.py:20
  114.0 8.8 %collective-permute-start.38 = (bf16[128,384]{1,0:T(8,128)(2,1)S(1)}, bf16[128,384]{1,0:T(8,128)(2,1)S(1)}, u32[]{:S(2)}, u32[]{:S(2)}) collective-permute-start(bf16[128,384]{1,0:T(8,128)(2,1)S(1)} %collective-permute-done.25.refs_3_), channel_id=1, source_target_pairs={{0,1},{1,0},{2,3},{3,2},{4,5},{5,4},{6,7},{7,6},{8,9},{9,8},{10,11... | collective-permute-start | bytes 294920 | tf_op jit(solution)/shard_map/ppermute | solution.py:20
  114.7 15.6 %collective-permute-start.50 = (bf16[128,384]{1,0:T(8,128)(2,1)S(1)}, bf16[128,384]{1,0:T(8,128)(2,1)S(1)}, u32[]{:S(2)}, u32[]{:S(2)}) collective-permute-start(bf16[128,384]{1,0:T(8,128)(2,1)S(1)} %get-tuple-element.18), channel_id=1, source_target_pairs={{0,0},{1,4},{4,8},{5,12},{8,1},{9,5},{12,9},{13,13},{2,2},{3,6},{6... | collective-permute-start | bytes 294920 | tf_op jit(solution)/shard_map/ppermute | solution.py:411
  115.3 16.2 %collective-permute-start.51 = (bf16[128,384]{1,0:T(8,128)(2,1)S(1)}, bf16[128,384]{1,0:T(8,128)(2,1)S(1)}, u32[]{:S(2)}, u32[]{:S(2)}) collective-permute-start(bf16[128,384]{1,0:T(8,128)(2,1)S(1)} %get-tuple-element.17), channel_id=1, source_target_pairs={{0,4},{1,8},{4,12},{5,0},{8,5},{9,9},{12,13},{13,1},{2,6},{3,10},{... | collective-permute-start | bytes 294920 | tf_op jit(solution)/shard_map/ppermute | solution.py:411
  119.6 14.4 %collective-permute-start.52 = (bf16[128,384]{1,0:T(8,128)(2,1)S(1)}, bf16[128,384]{1,0:T(8,128)(2,1)S(1)}, u32[]{:S(2)}, u32[]{:S(2)}) collective-permute-start(bf16[128,384]{1,0:T(8,128)(2,1)S(1)} %get-tuple-element.16), channel_id=1, source_target_pairs={{0,8},{1,12},{4,0},{5,4},{8,9},{9,13},{12,1},{13,5},{2,10},{3,14},... | collective-permute-start | bytes 294920 | tf_op jit(solution)/shard_map/ppermute | solution.py:411
  127.6 7.8 %collective-permute-start.43 = (bf16[256,128]{1,0:T(8,128)(2,1)S(1)}, bf16[256,128]{1,0:T(8,128)(2,1)S(1)}, u32[]{:S(2)}, u32[]{:S(2)}) collective-permute-start(bf16[256,128]{1,0:T(8,128)(2,1)S(1)} %get-tuple-element.35), channel_id=1, source_target_pairs={{0,4},{4,8},{8,12},{12,0},{1,5},{5,9},{9,13},{13,1},{2,6},{6,10},{... | collective-permute-start | bytes 196616 | tf_op jit(solution)/shard_map/ppermute | solution.py:29
  127.7 8.5 %collective-permute-start.44 = (bf16[256,128]{1,0:T(8,128)(2,1)S(1)}, bf16[256,128]{1,0:T(8,128)(2,1)S(1)}, u32[]{:S(2)}, u32[]{:S(2)}) collective-permute-start(bf16[256,128]{1,0:T(8,128)(2,1)S(1)} %get-tuple-element.34), channel_id=1, source_target_pairs={{0,8},{4,12},{8,0},{12,4},{1,9},{5,13},{9,1},{13,5},{2,10},{6,14},... | collective-permute-start | bytes 196616 | tf_op jit(solution)/shard_map/ppermute | solution.py:29
  130.2 7.2 %collective-permute-start.45 = (bf16[256,128]{1,0:T(8,128)(2,1)S(1)}, bf16[256,128]{1,0:T(8,128)(2,1)S(1)}, u32[]{:S(2)}, u32[]{:S(2)}) collective-permute-start(bf16[256,128]{1,0:T(8,128)(2,1)S(1)} %get-tuple-element.33), channel_id=1, source_target_pairs={{0,12},{4,0},{8,4},{12,8},{1,13},{5,1},{9,5},{13,9},{2,14},{6,2},{... | collective-permute-start | bytes 196616 | tf_op jit(solution)/shard_map/ppermute | solution.py:29
  131.5 6.7 %collective-permute-start.53 = (bf16[128,384]{1,0:T(8,128)(2,1)S(1)}, bf16[128,384]{1,0:T(8,128)(2,1)S(1)}, u32[]{:S(2)}, u32[]{:S(2)}) collective-permute-start(bf16[128,384]{1,0:T(8,128)(2,1)S(1)} %get-tuple-element.15), channel_id=1, source_target_pairs={{0,12},{1,0},{4,4},{5,8},{8,13},{9,1},{12,5},{13,9},{2,14},{3,2},{... | collective-permute-start | bytes 294920 | tf_op jit(solution)/shard_map/ppermute | solution.py:411
  134.0 5.0 %collective-permute-start.46 = (bf16[256,128]{1,0:T(8,128)(2,1)S(1)}, bf16[256,128]{1,0:T(8,128)(2,1)S(1)}, u32[]{:S(2)}, u32[]{:S(2)}) collective-permute-start(bf16[256,128]{1,0:T(8,128)(2,1)S(1)} %get-tuple-element.36.refs_0_), channel_id=1, source_target_pairs={{0,2},{2,0},{1,3},{3,1},{4,6},{6,4},{5,7},{7,5},{8,10},{10,8},{9,1... | collective-permute-start | bytes 196616 | tf_op jit(solution)/shard_map/ppermute | solution.py:20
  135.4 5.1 %collective-permute-start.47 = (bf16[256,128]{1,0:T(8,128)(2,1)S(1)}, bf16[256,128]{1,0:T(8,128)(2,1)S(1)}, u32[]{:S(2)}, u32[]{:S(2)}) collective-permute-start(bf16[256,128]{1,0:T(8,128)(2,1)S(1)} %collective-permute-done.43.refs_1_), channel_id=1, source_target_pairs={{0,2},{2,0},{1,3},{3,1},{4,6},{6,4},{5,7},{7,5},{8,10},{10,8},{9,1... | collective-permute-start | bytes 196616 | tf_op jit(solution)/shard_map/ppermute | solution.py:20
  136.1 5.7 %collective-permute-start.48 = (bf16[256,128]{1,0:T(8,128)(2,1)S(1)}, bf16[256,128]{1,0:T(8,128)(2,1)S(1)}, u32[]{:S(2)}, u32[]{:S(2)}) collective-permute-start(bf16[256,128]{1,0:T(8,128)(2,1)S(1)} %collective-permute-done.44.refs_2_), channel_id=1, source_target_pairs={{0,2},{2,0},{1,3},{3,1},{4,6},{6,4},{5,7},{7,5},{8,10},{10,8},{9,1... | collective-permute-start | bytes 196616 | tf_op jit(solution)/shard_map/ppermute | solution.py:20
  137.4 5.1 %collective-permute-start.49 = (bf16[256,128]{1,0:T(8,128)(2,1)S(1)}, bf16[256,128]{1,0:T(8,128)(2,1)S(1)}, u32[]{:S(2)}, u32[]{:S(2)}) collective-permute-start(bf16[256,128]{1,0:T(8,128)(2,1)S(1)} %collective-permute-done.45.refs_3_), channel_id=1, source_target_pairs={{0,2},{2,0},{1,3},{3,1},{4,6},{6,4},{5,7},{7,5},{8,10},{10,8},{9,1... | collective-permute-start | bytes 196616 | tf_op jit(solution)/shard_map/ppermute | solution.py:20
  (12 other events, 64.4 us)

commit v2 on v0

--- a/solution.py
+++ b/solution.py
@@ -1,13 +1,465 @@
+import functools
 import math
 
 import jax
 import jax.numpy as jnp
 from jax import lax
+from jax.experimental import pallas as pl
+from jax.experimental.pallas import tpu as pltpu
 from jax.sharding import PartitionSpec as P
 
 HEAD = 128
 LAYERS = 3
 BINS_DEV = 512
+F32 = jnp.float32
+BF16 = jnp.bfloat16
+VMEM_LIMIT = 16 * 1024 * 1024
+SPLIT = 4
+
+
+def swap(x, axis):
+    return lax.ppermute(x, axis, [(0, 1), (1, 0)])
+
+
+def swap_both(x):
+    return lax.ppermute(x, ("mp", "sub"), [(i, 3 - i) for i in range(4)])
+
+
+def rotate(x, by):
+    n = lax.axis_size("seq")
+    return lax.ppermute(x, "seq", [(i, (i + by) % n) for i in range(n)])
+
+
+def gather_parts(*pieces, under=None):
+    across = [swap(x, "mp") for x in pieces]
+    if under is not None:
+        across = lax.optimization_barrier((across, under))[0]
+    near = [swap(x, "sub") for x in pieces]
+    return (*pieces, *near, *across, *[swap(x, "sub") for x in across])
+
+
+def dot(a, b):
+    return jnp.dot(a, b, preferred_element_type=F32)
+
+
+def at(start, size):
+    return pl.ds(pl.multiple_of(start, size), size)
+
+
+SUB, SEQ = 4, 5
+
+
+def fill_hidden(scalars, parts, gains, layer, hidden, order=None):
+    count = len(parts) // 4
+    rows, width = parts[0].shape
+    quarter = rows * count // 4
+    tile = 16
+    columns = [at(scalars[p] * width, width) for p in range(4)]
+    gain = [gains[layer : layer + 1, c] for c in columns]
+    for r in range(0, rows * count, tile):
+        here = slice(r % rows, r % rows + tile)
+        wide = [parts[p * count + r // rows][here, :].astype(F32) for p in range(4)]
+        squares = wide[0] * wide[0]
+        for x in wide[1:]:
+            squares = squares + x * x
+        mean = jnp.sum(squares, axis=1, keepdims=True) / (4 * width)
+        scale = lax.rsqrt(mean + 1e-06)
+        if order is None:
+            target = pl.ds(r, tile)
+        else:
+            target = at(order[r // quarter] * quarter + r % quarter, tile)
+        for p, x in enumerate(wide):
+            hidden[target, columns[p]] = jax.nn.gelu(x * scale * gain[p]).astype(BF16)
+
+
+def turn(scalars, by):
+    return lax.rem(scalars[SEQ] + by, 4)
+
+
+def bring(copies):
+    copies = [pltpu.make_async_copy(*copy) for copy in copies]
+    for copy in copies:
+        copy.start()
+    for copy in copies:
+        copy.wait()
+
+
+def load_taps_kernel(layer, scalars, w, out, sems):
+    size = out.shape[1] // SPLIT
+    copies = []
+    for tap in range(3):
+        for i in range(SPLIT):
+            rows = pl.ds(i * size, size)
+            copies.append((w.at[layer, tap, rows], out.at[tap, rows], sems.at[tap, i]))
+    bring(copies)
+
+
+def load_projections_kernel(scalars, w_q, w_k, w_v, out, sems):
+    size = out.shape[1] // SPLIT
+    copies = []
+    for m, w in enumerate((w_q, w_k, w_v)):
+        for i in range(SPLIT):
+            rows = pl.ds(i * size, size)
+            copies.append((w.at[rows], out.at[m, rows], sems.at[m, i]))
+    bring(copies)
+
+
+def cut_kernel(scalars, x, edge, middle, sems):
+    b = edge.shape[0] // 2
+    bring(
+        [
+            (x.at[pl.ds(0, b)], edge.at[pl.ds(0, b)], sems.at[0]),
+            (x.at[pl.ds(3 * b, b)], edge.at[pl.ds(b, b)], sems.at[1]),
+            (x.at[pl.ds(b, 2 * b)], middle, sems.at[2]),
+        ]
+    )
+
+
+def first_edge_kernel(scalars, p0, p1, p2, p3, gains, w, acc, up, down, hidden):
+    fill_hidden(scalars, (p0, p1, p2, p3), gains, 0, hidden)
+    b = up.shape[0]
+    middle = p0[...].astype(F32) + dot(hidden[...], w[1])
+    before = dot(hidden[...], w[0])
+    after = dot(hidden[...], w[2])
+    up[...] = before[b:].astype(BF16)
+    down[...] = after[:b].astype(BF16)
+    acc[0] = middle[:b]
+    acc[1] = before[:b]
+    acc[2] = after[b:]
+    acc[3] = middle[b:]
+
+
+def first_middle_kernel(
+    scalars, p0, p1, p2, p3, gains, w, acc, partial, hidden
+):
+    fill_hidden(scalars, (p0, p1, p2, p3), gains, 0, hidden)
+    b = acc.shape[1]
+    middle = p0[...].astype(F32) + dot(hidden[...], w[1])
+    before = dot(hidden[...], w[0])
+    after = dot(hidden[...], w[2])
+    partial[0] = acc[0] + after[:b]
+    partial[1] = acc[1] + middle[:b] + after[b:]
+    partial[2] = acc[2] + middle[b:] + before[:b]
+    partial[3] = acc[3] + before[b:]
+
+
+def deal_kernel(scalars, partial, lower, upper, *refs):
+    outs, stream = refs[:4], refs[4]
+    stream[0] = (partial[0] + lower[...].astype(F32)).astype(BF16)
+    stream[1] = partial[1].astype(BF16)
+    stream[2] = partial[2].astype(BF16)
+    stream[3] = (partial[3] + upper[...].astype(F32)).astype(BF16)
+    for s, out in enumerate(outs):
+        out[...] = stream[turn(scalars, s)]
+
+
+def local_taps(hidden, acc, w, shift):
+    rows = hidden.shape[0]
+    acc[...] = dot(hidden[...], w[1])
+    acc[shift:, :] += dot(hidden[: rows - shift, :], w[0])
+    acc[: rows - shift, :] += dot(hidden[shift:, :], w[2])
+
+
+def second_kernel(scalars, *refs):
+    parts = refs[:8]
+    gains, w, low, high, hidden, acc, kept = refs[8:]
+    half = low.shape[0]
+    b = half // 2
+    order = [turn(scalars, 4 - s) for s in range(4)]
+    fill_hidden(scalars, parts, gains, 1, hidden, order)
+    for s in range(4):
+        kept[order[s]] = parts[s // 2][(s % 2) * b : (s % 2 + 1) * b, :]
+    local_taps(hidden, acc, w, b)
+    for k in range(4):
+        out = low if k < 2 else high
+        made = kept[k].astype(F32) + acc[k * b : (k + 1) * b, :]
+        out[(k % 2) * b : (k % 2 + 1) * b, :] = made.astype(BF16)
+
+
+def third_kernel(scalars, *refs):
+    parts = refs[:8]
+    gains, w = refs[8:10]
+    mine, theirs = refs[10:12]
+    outs = refs[12:16]
+    hidden, acc, made = refs[16:]
+    half = parts[0].shape[0]
+    b = half // 2
+    fill_hidden(scalars, parts, gains, 2, hidden)
+    local_taps(hidden, acc, w, half)
+    for k in range(4):
+        own = parts[k // 2][(k % 2) * b : (k % 2 + 1) * b, :].astype(F32)
+        made[k] = (own + acc[k * b : (k + 1) * b, :]).astype(BF16)
+    sub = scalars[SUB]
+    for c in range(2):
+        rows = slice(c * b, (c + 1) * b)
+        mine[rows, :] = made[2 * c + sub]
+        theirs[rows, :] = made[2 * c + 1 - sub]
+    for s, out in enumerate(outs):
+        out[...] = made[turn(scalars, s)]
+
+
+def sort_kernel(scalars, *refs):
+    arrived, keep, give, ordered = refs[:4], *refs[4:]
+    b = arrived[0].shape[0]
+    for s in range(4):
+        ordered[turn(scalars, 4 - s)] = arrived[s][...]
+    for a in range(2):
+        rows = slice(a * b, (a + 1) * b)
+        keep[rows, :] = ordered[2 * scalars[SUB] + a]
+        give[rows, :] = ordered[2 * (1 - scalars[SUB]) + a]
+
+
+def project_kernel(scalars, p0, p1, p2, p3, w, o0, o1, o2, o3, rows, made):
+    width = p0.shape[1]
+    for p, part in enumerate((p0, p1, p2, p3)):
+        rows[:, at(scalars[p] * width, width)] = part[...]
+    for i in range(3):
+        product = dot(rows[...], w[i]).astype(BF16)
+        for h in range(4):
+            made[h, :, i * HEAD : (i + 1) * HEAD] = product[:, h * HEAD : (h + 1) * HEAD]
+    for s, out in enumerate((o0, o1, o2, o3)):
+        out[...] = made[turn(scalars, s)]
+
+
+def attend_kernel(scalars, *refs):
+    own, other, outs = refs[:4], refs[4:8], refs[8:12]
+    queries, keys, values = refs[12:]
+    rows = own[0].shape[0]
+    b = rows // 2
+    sub = scalars[SUB]
+    for s in range(4):
+        for c in range(2):
+            queries[c, sub, s] = own[s][c * b : (c + 1) * b, :HEAD]
+            queries[c, 1 - sub, s] = other[s][c * b : (c + 1) * b, :HEAD]
+        for o, ref in enumerate((own[s], other[s])):
+            here = pl.ds((s * 2 + o) * rows, rows)
+            keys[here, :] = ref[:, HEAD : 2 * HEAD]
+            values[here, :] = ref[:, 2 * HEAD :]
+    factor = math.log2(math.e) / math.sqrt(HEAD)
+    for s, out in enumerate(outs):
+        k = turn(scalars, s)
+        for a in range(2):
+            source = lax.rem(scalars[SEQ] - 2 * sub - a + 4, 4)
+            asked = queries[k // 2, lax.rem(k, 2), source]
+            scores = lax.dot_general(
+                asked, keys[...], (((1,), (1,)), ((), ())), preferred_element_type=F32
+            )
+            top = jnp.max(scores, axis=1, keepdims=True)
+            expw = jnp.exp2((scores - top) * factor)
+            denom = jnp.sum(expw, axis=1, keepdims=True)
+            numer = dot(expw.astype(BF16), values[...])
+            out[a * b : (a + 1) * b, :] = (numer / denom).astype(BF16)
+
+
+def finish_kernel(scalars, *refs):
+    own, other = refs[:4], refs[4:8]
+    keep, got, w_own, w_near, w_far, out, mixed, residual = refs[8:]
+    sub = scalars[SUB]
+    width = keep.shape[1]
+    half = 4 * HEAD
+    for s in range(4):
+        head = turn(scalars, 4 - s)
+        mixed[:, at(head * HEAD, HEAD)] = own[s][...]
+        place = lax.rem(head + 2 * (1 - sub) + 2, 4)
+        mixed[:, at(half + place * HEAD, HEAD)] = other[s][...]
+    residual[:, at(sub * width, width)] = keep[...]
+    residual[:, at((1 - sub) * width, width)] = got[...]
+    shares = dot(mixed[:, :half], w_own[...])
+    shares = shares + dot(mixed[:, half : half + 2 * HEAD], w_near[...])
+    shares = shares + dot(mixed[:, half + 2 * HEAD :], w_far[...])
+    out[...] = (residual[...].astype(F32) + shares).astype(BF16)
+
+
+def whole(x):
+    zeros = (0,) * len(x.shape)
+    return pl.BlockSpec(x.shape, lambda *_: zeros)
+
+
+def struct(shape, dtype=BF16):
+    return jax.ShapeDtypeStruct(shape, dtype)
+
+
+def call(kernel, scalars, args, outs, scratch, flops, far=(), limit=VMEM_LIMIT):
+    moved = sum(math.prod(a.shape) * a.dtype.itemsize for a in (*args, *outs))
+    return pl.pallas_call(
+        kernel,
+        out_shape=outs,
+        grid_spec=pltpu.PrefetchScalarGridSpec(
+            num_scalar_prefetch=1,
+            grid=(1,),
+            in_specs=[
+                pl.BlockSpec(memory_space=pl.ANY) if i in far else whole(a)
+                for i, a in enumerate(args)
+            ],
+            out_specs=[whole(o) for o in outs],
+            scratch_shapes=scratch,
+        ),
+        compiler_params=pltpu.CompilerParams(
+            dimension_semantics=("arbitrary",), vmem_limit_bytes=limit
+        ),
+        cost_estimate=pl.CostEstimate(flops=flops, transcendentals=0, bytes_accessed=moved),
+        name=getattr(kernel, "func", kernel).__name__,
+    )(scalars, *args)
+
+
+def after(x, *earlier):
+    return lax.optimization_barrier((x, *earlier))[0]
+
+
+def per_device_fast(seq_in, conv_gain, conv_weight, w_q, w_k, w_v, w_o):
+    rows, width = seq_in.shape
+    channels = 4 * width
+    n = 4
+    b = rows // n
+    half = rows // 2
+    z, mp, sub = (lax.axis_index(a) for a in ("seq", "mp", "sub"))
+    place = mp * 2 + sub
+    scalars = jnp.stack([place, place ^ 1, place ^ 2, place ^ 3, sub, z]).astype(jnp.int32)
+    hidden = pltpu.VMEM((half, channels), BF16)
+    hidden_all = pltpu.VMEM((rows, channels), BF16)
+    summed = pltpu.VMEM((rows, width), F32)
+    blocks = pltpu.VMEM((n, b, width), BF16)
+    block = struct((b, width))
+    flops = 2 * half * channels * 3 * width
+    out_width = w_o.shape[1] // 2
+    sems = pltpu.SemaphoreType.DMA((3, SPLIT))
+
+    def load_taps(layer):
+        (w,) = call(
+            functools.partial(load_taps_kernel, layer),
+            scalars,
+            (conv_weight,),
+            [struct(conv_weight.shape[1:])],
+            [sems],
+            0,
+            far=(0,),
+        )
+        return w
+
+    edge, middle = call(
+        cut_kernel,
+        scalars,
+        (seq_in,),
+        [struct((half, width))] * 2,
+        [pltpu.SemaphoreType.DMA((3,))],
+        0,
+        far=(0,),
+    )
+    taps = (conv_gain, load_taps(0))
+    edge_across = after(swap(edge, "mp"), taps[1])
+    middle_across = swap(middle, "mp")
+    middle_near = swap(middle, "sub")
+    acc, up, down = call(
+        first_edge_kernel,
+        scalars,
+        (edge, swap(edge, "sub"), edge_across, swap(edge_across, "sub"), *taps),
+        [struct((n, b, width), F32), struct((b, width)), struct((b, width))],
+        [hidden],
+        flops,
+    )
+    lower = lax.ppermute(up, "seq", [(i, i + 1) for i in range(n - 1)])
+    upper = lax.ppermute(down, "seq", [(i + 1, i) for i in range(n - 1)])
+    middle_across = after(middle_across, acc)
+    (partial,) = call(
+        first_middle_kernel,
+        scalars,
+        (middle, middle_near, middle_across, swap(middle_across, "sub"), *taps, acc),
+        [struct((n, b, width), F32)],
+        [hidden],
+        flops,
+    )
+    dealt = call(
+        deal_kernel,
+        scalars,
+        (partial, lower, upper),
+        [block] * n,
+        [blocks],
+        0,
+    )
+    dealt = [dealt[0]] + [rotate(dealt[s], s) for s in range(1, n)]
+
+    taps = (conv_gain, load_taps(1))
+    early = after(jnp.concatenate(dealt[:2], axis=0), taps[1])
+    late = jnp.concatenate(dealt[2:], axis=0)
+    next_taps = load_taps(2)
+    low, high = call(
+        second_kernel,
+        scalars,
+        (*gather_parts(early, late, under=next_taps), *taps),
+        [struct((half, width))] * 2,
+        [hidden_all, summed, blocks],
+        flops * 2,
+    )
+    (w_qkv,) = call(
+        load_projections_kernel,
+        scalars,
+        (w_q, w_k, w_v),
+        [struct((3, *w_q.shape))],
+        [sems],
+        0,
+        far=(0, 1, 2),
+    )
+    mine, theirs, *back = call(
+        third_kernel,
+        scalars,
+        (*gather_parts(low, high, under=w_qkv), conv_gain, next_taps),
+        [struct((half, width))] * 2 + [block] * n,
+        [hidden_all, summed, blocks],
+        flops * 2,
+    )
+
+    back = [back[0]] + [rotate(back[s], s) for s in range(1, n)]
+    keep, give = call(
+        sort_kernel, scalars, back, [struct((half, width))] * 2, [blocks], 0
+    )
+
+    parts = (mine, swap(theirs, "sub"), swap(mine, "mp"), swap_both(theirs))
+    parts, keep = lax.optimization_barrier((parts, keep))
+    projected = call(
+        project_kernel,
+        scalars,
+        (*parts, w_qkv),
+        [struct((half, 3 * HEAD))] * n,
+        [pltpu.VMEM((half, channels), BF16), pltpu.VMEM((n, half, 3 * HEAD), BF16)],
+        2 * half * channels * 3 * n * HEAD,
+    )
+    received = [projected[0]] + [rotate(projected[s], s) for s in range(1, n)]
+    got = swap(give, "sub")
+    last = projected[0]
+
+    w_o = after(w_o, last)
+    half_rows = w_o.shape[0] // 2
+    asked = lax.dynamic_slice(
+        w_o, (sub * half_rows, (1 - mp) * out_width), (half_rows, out_width)
+    )
+    w_own = lax.dynamic_slice_in_dim(w_o, mp * out_width, out_width, 1)
+    w_near = swap(asked, "mp")
+    w_far = swap(w_near, "sub")
+
+    swapped = [swap(x, "sub") for x in received]
+    keys = pltpu.VMEM((8 * half, HEAD), BF16)
+    attended = call(
+        attend_kernel,
+        scalars,
+        (*received, *swapped),
+        [struct((half, HEAD))] * n,
+        [pltpu.VMEM((2, 2, n, b, HEAD), BF16), keys, keys],
+        4 * half * 4 * 8 * half * HEAD,
+    )
+    keep, got, w_near, w_far = lax.optimization_barrier(
+        (keep, got, w_near, w_far, attended[0])
+    )[:4]
+    heads = [attended[0]] + [rotate(attended[s], s) for s in range(1, n)]
+    others = [swap(x, "mp") for x in heads]
+    (out,) = call(
+        finish_kernel,
+        scalars,
+        (*heads, *others, keep, got, w_own, w_near, w_far),
+        [struct((half, out_width))],
+        [pltpu.VMEM((half, 8 * HEAD), BF16), pltpu.VMEM((half, out_width), BF16)],
+        2 * half * 8 * HEAD * out_width,
+    )
+    return out
 
 
 def passed_along(x, axis, by):
@@ -109,8 +561,10 @@
         P(None, "mp"),
         P("mp", None),
     )
+    sizes = dict(mesh.shape)
+    dealt = sizes["seq"] == 4 and sizes["mp"] == 2 and sizes["sub"] == 2
     return jax.shard_map(
-        per_device,
+        per_device_fast if dealt else per_device,
         mesh=mesh,
         in_specs=placed,
         out_specs=P(("groups", "seq", "sub"), "mp"),

time: 253 us -> 131 us (0.52)
  waiting for transfers between devices: 157 us -> 45.9 us
  matrix products: 34.3 us -> 0 us
  Pallas kernels: 0 us -> 32.2 us
  starting transfers between devices: 19.2 us -> 42.8 us
  between operations: 13.7 us -> 0.31 us
  other arithmetic: 9.91 us -> 0.02 us
  blocking collectives: 9.14 us -> 0 us
    all_gather x6 -> x0, waiting for transfers between devices: 98.6 us -> none  [the longest x3 60.7 us: tower_section(): gathered = lax.all_gather(stream_shard, ('mp', 'sub'), axis=1, tiled=True)]
    dot_general x9 -> x0, matrix products: 34.3 us -> none  [the longest x3 16.9 us: tower_section(): jnp.einsum('rc,jco->jro', hidden, weight_taps, preferred_element_type=jnp...]
    pallas_call x0 -> x14, Pallas kernels: none -> 32.2 us  [call(): pl.pallas_call(kernel, out_shape=outs, grid_spec=pltpu.PrefetchScalarGrid...]
    ppermute x6 -> x46, starting transfers between devices: 15.1 us -> 42.8 us  [the longest x12 19.1 us: rotate(): return lax.ppermute(x, 'seq', [(i, (i + by) % n) for i in range(n)])]
    all_to_all x1 -> x0, waiting for transfers between devices: 19.9 us -> none  [per_device(): lax.all_to_all(w_o, 'mp', split_axis=1, concat_axis=0, tiled=True)]
    all_gather x1 -> x0, blocking collectives: 9.14 us -> none  [per_device(): every_head = lax.all_gather(attended, 'mp', axis=1, tiled=True)]
    ppermute x6 -> x46, waiting for transfers between devices: 37.6 us -> 45.9 us  [the longest x12 26.3 us: rotate(): return lax.ppermute(x, 'seq', [(i, (i + by) % n) for i in range(n)])]
    reduce_sum x4 -> x0, other arithmetic: 6.99 us -> none  [the longest x3 5.37 us: tower_section(): jnp.mean(widened * widened, axis=1, keepdims=True) + 1e-06]
  transfers between devices with their start and end apart: 13 -> 46, of which waited for: 12 -> 24; matrix products, arithmetic and copies ran while one was open for 6% -> 0% of each run, Pallas kernels for 0% -> 14%
where the time goes in v2:
time: 131 us
  waiting for transfers between devices  45.9 us (35%)
  starting transfers between devices  42.8 us (33%)
  Pallas kernels  32.2 us (25%)
  local copies, waits for them, and re-layouts  9.75 us (7%)
    pallas_call x14, Pallas kernels, call(): pl.pallas_call(kernel, out_shape=outs, grid_spec=pltpu.PrefetchScalarGrid...  32.2 us
    ppermute x12, waiting for transfers between devices, rotate(): return lax.ppermute(x, 'seq', [(i, (i + by) % n) for i in range(n)])  26.3 us
    ppermute x12, starting transfers between devices, rotate(): return lax.ppermute(x, 'seq', [(i, (i + by) % n) for i in range(n)])  19.1 us
    ppermute x31, starting transfers between devices, swap(): return lax.ppermute(x, axis, [(0, 1), (1, 0)])  18.1 us
    ppermute x31, waiting for transfers between devices, swap(): return lax.ppermute(x, axis, [(0, 1), (1, 0)])  16.9 us
    unnamed x25, local copies, waits for them, and re-layouts  9.56 us
    ppermute x1, starting transfers between devices, per_device_fast(): lower = lax.ppermute(up, 'seq', [(i, i + 1) for i in range(n - 1)])  3.47 us
    ppermute x1, waiting for transfers between devices, per_device_fast(): upper = lax.ppermute(down, 'seq', [(i + 1, i) for i in range(n - 1)])  2.74 us
  transfers between devices with their start and end apart: 46, of which 24 were waited for; matrix products, arithmetic and copies ran while one was open for 0% of the time, Pallas kernels for 14%

profile of v2, /device:TPU:0, one launch (start us, length us, event | category | flops | bytes accessed | tf_op | source)
XLA Modules:
  0.0 131.0 jit_solution(11314226933256231247)
XLA Ops:
  1.1 1.1 cut_kernel.1
  2.2 3.0 %collective-permute-start.3 = (bf16[256,384]{1,0:T(8,128)(2,1)S(1)}, bf16[256,384]{1,0:T(8,128)(2,1)S(1)}, u32[]{:S(2)}, u32[]{:S(2)}) collective-permute-start(bf16[256,384]{1,0:T(8,128)(2,1)S(1)} %get-tuple-element.50.p0), channel_id=1, source_target_pairs={{0,2},{2,0},{1,3},{3,1},{4,6},{6,4},{5,7},{7,5},{8,10},{10,8},{9,1... | collective-permute-start | bytes 589832 | tf_op jit(solution)/shard_map/ppermute | solution.py:21
  5.2 4.0 %copy-done = bf16[3,3,1536,384]{3,2,1,0:T(8,128)(2,1)S(1)} copy-done((bf16[3,3,1536,384]{3,2,1,0:T(8,128)(2,1)S(1)}, bf16[3,3,1536,384]{3,2,1,0:T(8,128)(2,1)}, u32[]{:S(2)}) %copy-start) | copy-done | bytes 10616856
  9.2 1.4 %load_taps_kernel.3.w = bf16[3,1536,384]{2,1,0:T(8,128)(2,1)S(1)} custom-call(s32[6]{0:T(128)S(1)} %stack.27.scalars, bf16[3,3,1536,384]{3,2,1,0:T(8,128)(2,1)S(1)} %copy-done), custom_call_target="tpu_custom_call" | custom-call | bytes 14155776 | tf_op jit(solution)/shard_map/load_taps_kernel/pallas_call | solution.py:284
  12.2 2.7 %first_edge_kernel.1 = (f32[4,128,384]{2,1,0:T(8,128)S(1)}, bf16[128,384]{1,0:T(8,128)(2,1)S(1)}, bf16[128,384]{1,0:T(8,128)(2,1)S(1)}) custom-call(s32[6]{0:T(128)S(1)} %stack.27.scalars, bf16[256,384]{1,0:T(8,128)(2,1)S(1)} %get-tuple-element.50.p0, bf16[256,384]{1,0:T(8,128)(2,1)S(1)} %collective-permute-done.2.p1, ...), custom_call_target="tpu_custom_call" | custom-call | flops 905969664 | bytes 5326848 | tf_op jit(solution)/shard_map/first_edge_kernel/pallas_call | solution.py:284
  15.0 3.1 %collective-permute-done.1.p2 = bf16[256,384]{1,0:T(8,128)(2,1)S(1)} collective-permute-done((bf16[256,384]{1,0:T(8,128)(2,1)S(1)}, bf16[256,384]{1,0:T(8,128)(2,1)S(1)}, u32[]{:S(2)}, u32[]{:S(2)}) %collective-permute-start.1) | collective-permute-done | bytes 196640 | tf_op jit(solution)/shard_map/ppermute | solution.py:21
  18.1 3.5 %collective-permute-start.6 = (bf16[128,384]{1,0:T(8,128)(2,1)S(1)}, bf16[128,384]{1,0:T(8,128)(2,1)S(1)}, u32[]{:S(2)}, u32[]{:S(2)}) collective-permute-start(bf16[128,384]{1,0:T(8,128)(2,1)S(1)} %get-tuple-element.54), channel_id=1, source_target_pairs={{0,4},{4,8},{8,12},{1,5},{5,9},{9,13},{2,6},{6,10},{10,14},{3,7},{... | collective-permute-start | bytes 294920 | tf_op jit(solution)/shard_map/ppermute | solution.py:360
  21.6 1.3 collective-permute-start.7
  22.9 2.7 %first_middle_kernel.1.partial = f32[4,128,384]{2,1,0:T(8,128)S(1)} custom-call(s32[6]{0:T(128)S(1)} %stack.27.scalars, bf16[256,384]{1,0:T(8,128)(2,1)S(1)} %get-tuple-element.49.p0, bf16[256,384]{1,0:T(8,128)(2,1)S(1)} %collective-permute-done.p1, bf16[256,384]{1,0:T(8,128)(2,1)S(1)} %collective-permute-done.1.p2, ...), custom_call_target="tpu_custom_call" | custom-call | flops 905969664 | bytes 5916672 | tf_op jit(solution)/shard_map/first_middle_kernel/pallas_call | solution.py:284
  25.6 2.7 %collective-permute-done.7.upper = bf16[128,384]{1,0:T(8,128)(2,1)S(1)} collective-permute-done((bf16[128,384]{1,0:T(8,128)(2,1)S(1)}, bf16[128,384]{1,0:T(8,128)(2,1)S(1)}, u32[]{:S(2)}, u32[]{:S(2)}) %collective-permute-start.7) | collective-permute-done | bytes 98336 | tf_op jit(solution)/shard_map/ppermute | solution.py:361
  29.0 2.7 %collective-permute-start.9 = (bf16[128,384]{1,0:T(8,128)(2,1)S(1)}, bf16[128,384]{1,0:T(8,128)(2,1)S(1)}, u32[]{:S(2)}, u32[]{:S(2)}) collective-permute-start(bf16[128,384]{1,0:T(8,128)(2,1)S(1)} %get-tuple-element.59), channel_id=1, source_target_pairs={{0,8},{4,12},{8,0},{12,4},{1,9},{5,13},{9,1},{13,5},{2,10},{6,14},... | collective-permute-start | bytes 294920 | tf_op jit(solution)/shard_map/ppermute | solution.py:30
  31.7 1.4 %load_taps_kernel.4.refs_9_ = bf16[3,1536,384]{2,1,0:T(8,128)(2,1)S(1)} custom-call(s32[6]{0:T(128)S(1)} %stack.27.scalars, bf16[3,3,1536,384]{3,2,1,0:T(8,128)(2,1)S(1)} %bitcast.7), custom_call_target="tpu_custom_call" | custom-call | bytes 14155776 | tf_op jit(solution)/shard_map/load_taps_kernel/pallas_call | solution.py:284
  33.1 1.4 %collective-permute-start.10 = (bf16[128,384]{1,0:T(8,128)(2,1)S(1)}, bf16[128,384]{1,0:T(8,128)(2,1)S(1)}, u32[]{:S(2)}, u32[]{:S(2)}) collective-permute-start(bf16[128,384]{1,0:T(8,128)(2,1)S(1)} %get-tuple-element.60), channel_id=1, source_target_pairs={{0,12},{4,0},{8,4},{12,8},{1,13},{5,1},{9,5},{13,9},{2,14},{6,2},{... | collective-permute-start | bytes 294920 | tf_op jit(solution)/shard_map/ppermute | solution.py:30
  35.2 1.5 %collective-permute-done.9 = bf16[128,384]{1,0:T(8,128)(2,1)S(1)} collective-permute-done((bf16[128,384]{1,0:T(8,128)(2,1)S(1)}, bf16[128,384]{1,0:T(8,128)(2,1)S(1)}, u32[]{:S(2)}, u32[]{:S(2)}) %collective-permute-start.9) | collective-permute-done | bytes 98336 | tf_op jit(solution)/shard_map/ppermute | solution.py:30
  36.7 1.1 collective-permute-done.10
  37.8 1.1 collective-permute-start.14
  38.9 2.0 %collective-permute-done.8 = bf16[128,384]{1,0:T(8,128)(2,1)S(1)} collective-permute-done((bf16[128,384]{1,0:T(8,128)(2,1)S(1)}, bf16[128,384]{1,0:T(8,128)(2,1)S(1)}, u32[]{:S(2)}, u32[]{:S(2)}) %collective-permute-start.8) | collective-permute-done | bytes 98336 | tf_op jit(solution)/shard_map/ppermute | solution.py:30
  40.9 1.1 collective-permute-start.13
  42.1 1.4 %load_taps_kernel.5.refs_9_ = bf16[3,1536,384]{2,1,0:T(8,128)(2,1)S(1)} custom-call(s32[6]{0:T(128)S(1)} %stack.27.scalars, bf16[3,3,1536,384]{3,2,1,0:T(8,128)(2,1)S(1)} %bitcast.7), custom_call_target="tpu_custom_call" | custom-call | bytes 14155776 | tf_op jit(solution)/shard_map/load_taps_kernel/pallas_call | solution.py:284
  44.1 1.5 %collective-permute-done.14.refs_5_ = bf16[256,384]{1,0:T(8,128)(2,1)S(1)} collective-permute-done((bf16[256,384]{1,0:T(8,128)(2,1)S(1)}, bf16[256,384]{1,0:T(8,128)(2,1)S(1)}, u32[]{:S(2)}, u32[]{:S(2)}) %collective-permute-start.14) | collective-permute-done | bytes 196640 | tf_op jit(solution)/shard_map/ppermute | solution.py:21
  45.6 2.1 %collective-permute-done.13.refs_4_ = bf16[256,384]{1,0:T(8,128)(2,1)S(1)} collective-permute-done((bf16[256,384]{1,0:T(8,128)(2,1)S(1)}, bf16[256,384]{1,0:T(8,128)(2,1)S(1)}, u32[]{:S(2)}, u32[]{:S(2)}) %collective-permute-start.13) | collective-permute-done | bytes 196640 | tf_op jit(solution)/shard_map/ppermute | solution.py:21
  49.4 4.3 %second_kernel.1 = (bf16[256,384]{1,0:T(8,128)(2,1)S(1)}, bf16[256,384]{1,0:T(8,128)(2,1)S(1)}) custom-call(s32[6]{0:T(128)S(1)} %stack.27.scalars, bf16[256,384]{1,0:T(8,128)(2,1)S(1)} %pad_maximum_fusion.refs_0_, bf16[256,384]{1,0:T(8,128)(2,1)S(1)} %constant_dynamic-update-slice_fusion.refs_1_, bf16[256,384]{1,0:T(8,128)(2,1)S(1)} %collective-permute-done.11.refs_2_, ...), custom_call_target="tpu_custom_call" | custom-call | flops 1811939328 | bytes 5523456 | tf_op jit(solution)/shard_map/second_kernel/pallas_call | solution.py:284
  53.8 1.1 collective-permute-start.19
  55.9 2.9 %load_projections_kernel.1.w = bf16[3,1536,512]{2,1,0:T(8,128)(2,1)S(1)} custom-call(s32[6]{0:T(128)S(1)} %stack.27.scalars, bf16[1536,512]{1,0:T(8,128)(2,1)S(1)} %copy-done.3, bf16[1536,512]{1,0:T(8,128)(2,1)S(1)} %copy-done.4, bf16[1536,512]{1,0:T(8,128)(2,1)S(1)} %copy-done.5), custom_call_target="tpu_custom_call" | custom-call | bytes 9437184 | tf_op jit(solution)/shard_map/load_projections_kernel/pallas_call | solution.py:284
  58.8 2.2 %copy-done.1 = bf16[3,1536,512]{2,1,0:T(8,128)(2,1)} copy-done((bf16[3,1536,512]{2,1,0:T(8,128)(2,1)}, bf16[3,1536,512]{2,1,0:T(8,128)(2,1)S(1)}, u32[]{:S(2)}) %copy-start.1) | copy-done | bytes 4718616
  61.6 3.5 %collective-permute-done.20.refs_5_ = bf16[256,384]{1,0:T(8,128)(2,1)S(1)} collective-permute-done((bf16[256,384]{1,0:T(8,128)(2,1)S(1)}, bf16[256,384]{1,0:T(8,128)(2,1)S(1)}, u32[]{:S(2)}, u32[]{:S(2)}) %collective-permute-start.20) | collective-permute-done | bytes 196640 | tf_op jit(solution)/shard_map/ppermute | solution.py:21
  66.8 4.1 %third_kernel.1 = (bf16[256,384]{1,0:T(8,128)(2,1)S(1)}, bf16[256,384]{1,0:T(8,128)(2,1)S(1)}, bf16[128,384]{1,0:T(8,128)(2,1)S(1)}, bf16[128,384]{1,0:T(8,128)(...) custom-call(s32[6]{0:T(128)S(1)} %stack.27.scalars, ...), custom_call_target="tpu_custom_call" | custom-call | flops 1811939328 | bytes 5916672 | tf_op jit(solution)/shard_map/third_kernel/pallas_call | solution.py:284
  70.9 1.9 %collective-permute-start.26 = (bf16[128,384]{1,0:T(8,128)(2,1)S(1)}, bf16[128,384]{1,0:T(8,128)(2,1)S(1)}, u32[]{:S(2)}, u32[]{:S(2)}) collective-permute-start(bf16[128,384]{1,0:T(8,128)(2,1)S(1)} %get-tuple-element.70), channel_id=1, source_target_pairs={{0,4},{4,8},{8,12},{12,0},{1,5},{5,9},{9,13},{13,1},{2,6},{6,10},{... | collective-permute-start | bytes 294920 | tf_op jit(solution)/shard_map/ppermute | solution.py:30
  72.8 1.1 collective-permute-start.24
  74.7 1.1 collective-permute-start.27
  75.8 1.9 %collective-permute-done.26.refs_1_ = bf16[128,384]{1,0:T(8,128)(2,1)S(1)} collective-permute-done((bf16[128,384]{1,0:T(8,128)(2,1)S(1)}, bf16[128,384]{1,0:T(8,128)(2,1)S(1)}, u32[]{:S(2)}, u32[]{:S(2)}) %collective-permute-start.26) | collective-permute-done | bytes 98336 | tf_op jit(solution)/shard_map/ppermute | solution.py:30
  78.3 4.2 %collective-permute-done.27.refs_2_ = bf16[128,384]{1,0:T(8,128)(2,1)S(1)} collective-permute-done((bf16[128,384]{1,0:T(8,128)(2,1)S(1)}, bf16[128,384]{1,0:T(8,128)(2,1)S(1)}, u32[]{:S(2)}, u32[]{:S(2)}) %collective-permute-start.27) | collective-permute-done | bytes 98336 | tf_op jit(solution)/shard_map/ppermute | solution.py:30
  82.5 1.2 collective-permute-done.28.refs_3_
  84.4 2.3 %copy-done.2 = bf16[3,1536,512]{2,1,0:T(8,128)(2,1)S(1)} copy-done((bf16[3,1536,512]{2,1,0:T(8,128)(2,1)S(1)}, bf16[3,1536,512]{2,1,0:T(8,128)(2,1)}, u32[]{:S(2)}) %copy-start.2) | copy-done | bytes 4718616
  86.8 2.2 %project_kernel.1 = (bf16[256,384]{1,0:T(8,128)(2,1)S(1)}, bf16[256,384]{1,0:T(8,128)(2,1)S(1)}, bf16[256,384]{1,0:T(8,128)(2,1)S(1)}, bf16[256,384]{1,0:T(8,128)(2,1)S(1)}) custom-call(s32[6]{0:T(128)S(1)} %stack.27.scalars, bf16[256,384]{1,0:T(8,128)(2,1)S(1)} %get-tuple-element.74.p0, bf16[256,384]{1,0:T(8,128)(2,1)S(1)} %collective-permute-done.23.p1, ...), custom_call_target="tpu_custom_call" | custom-call | flops 1207959552 | bytes 6291456 | tf_op jit(solution)/shard_map/project_kernel/pallas_call | solution.py:284
  89.1 1.1 collective-permute-start.44
  90.2 1.4 %collective-permute-start.29 = (bf16[256,384]{1,0:T(8,128)(2,1)S(1)}, bf16[256,384]{1,0:T(8,128)(2,1)S(1)}, u32[]{:S(2)}, u32[]{:S(2)}) collective-permute-start(bf16[256,384]{1,0:T(8,128)(2,1)S(1)} %get-tuple-element.79), channel_id=1, source_target_pairs={{0,4},{4,8},{8,12},{12,0},{1,5},{5,9},{9,13},{13,1},{2,6},{6,10},{... | collective-permute-start | bytes 589832 | tf_op jit(solution)/shard_map/ppermute | solution.py:30
  91.5 2.2 %collective-permute-start.30 = (bf16[256,384]{1,0:T(8,128)(2,1)S(1)}, bf16[256,384]{1,0:T(8,128)(2,1)S(1)}, u32[]{:S(2)}, u32[]{:S(2)}) collective-permute-start(bf16[256,384]{1,0:T(8,128)(2,1)S(1)} %get-tuple-element.80), channel_id=1, source_target_pairs={{0,8},{4,12},{8,0},{12,4},{1,9},{5,13},{9,1},{13,5},{2,10},{6,14},... | collective-permute-start | bytes 589832 | tf_op jit(solution)/shard_map/ppermute | solution.py:30
  94.0 5.9 %collective-permute-done.29.refs_1_ = bf16[256,384]{1,0:T(8,128)(2,1)S(1)} collective-permute-done((bf16[256,384]{1,0:T(8,128)(2,1)S(1)}, bf16[256,384]{1,0:T(8,128)(2,1)S(1)}, u32[]{:S(2)}, u32[]{:S(2)}) %collective-permute-start.29) | collective-permute-done | bytes 196640 | tf_op jit(solution)/shard_map/ppermute | solution.py:30
  99.9 6.9 %collective-permute-done.30.refs_2_ = bf16[256,384]{1,0:T(8,128)(2,1)S(1)} collective-permute-done((bf16[256,384]{1,0:T(8,128)(2,1)S(1)}, bf16[256,384]{1,0:T(8,128)(2,1)S(1)}, u32[]{:S(2)}, u32[]{:S(2)}) %collective-permute-start.30) | collective-permute-done | bytes 196640 | tf_op jit(solution)/shard_map/ppermute | solution.py:30
  108.5 4.7 %attend_kernel.1 = (bf16[256,128]{1,0:T(8,128)(2,1)S(1)}, bf16[256,128]{1,0:T(8,128)(2,1)S(1)}, bf16[256,128]{1,0:T(8,128)(2,1)S(1)}, bf16[256,128]{1,0:T(8,128)(2,1)S(1)}) custom-call(s32[6]{0:T(128)S(1)} %stack.27.scalars, bf16[256,384]{1,0:T(8,128)(2,1)S(1)} %get-tuple-element.78.refs_0_, bf16[256,384]{1,0:T(8,128)(2,1)S(1)} %collective-permute-done.29.refs_1_, ...), custom_call_target="tpu_custom_call" | custom-call | flops 1073741824 | bytes 1835008 | tf_op jit(solution)/shard_map/attend_kernel/pallas_call | solution.py:284
  113.2 4.5 %collective-permute-start.36 = (bf16[256,128]{1,0:T(8,128)(2,1)S(1)}, bf16[256,128]{1,0:T(8,128)(2,1)S(1)}, u32[]{:S(2)}, u32[]{:S(2)}) collective-permute-start(bf16[256,128]{1,0:T(8,128)(2,1)S(1)} %get-tuple-element.83), channel_id=1, source_target_pairs={{0,4},{4,8},{8,12},{12,0},{1,5},{5,9},{9,13},{13,1},{2,6},{6,10},{... | collective-permute-start | bytes 196616 | tf_op jit(solution)/shard_map/ppermute | solution.py:30
  118.5 1.7 %collective-permute-start.38 = (bf16[256,128]{1,0:T(8,128)(2,1)S(1)}, bf16[256,128]{1,0:T(8,128)(2,1)S(1)}, u32[]{:S(2)}, u32[]{:S(2)}) collective-permute-start(bf16[256,128]{1,0:T(8,128)(2,1)S(1)} %get-tuple-element.85), channel_id=1, source_target_pairs={{0,12},{4,0},{8,4},{12,8},{1,13},{5,1},{9,5},{13,9},{2,14},{6,2},{... | collective-permute-start | bytes 196616 | tf_op jit(solution)/shard_map/ppermute | solution.py:30
  121.1 1.0 collective-permute-start.40
  122.2 1.6 %collective-permute-done.37.refs_2_ = bf16[256,128]{1,0:T(8,128)(2,1)S(1)} collective-permute-done((bf16[256,128]{1,0:T(8,128)(2,1)S(1)}, bf16[256,128]{1,0:T(8,128)(2,1)S(1)}, u32[]{:S(2)}, u32[]{:S(2)}) %collective-permute-start.37) | collective-permute-done | bytes 65568 | tf_op jit(solution)/shard_map/ppermute | solution.py:30
  124.8 1.0 collective-permute-start.42
  125.9 2.5 %collective-permute-done.41.refs_6_ = bf16[256,128]{1,0:T(8,128)(2,1)S(1)} collective-permute-done((bf16[256,128]{1,0:T(8,128)(2,1)S(1)}, bf16[256,128]{1,0:T(8,128)(2,1)S(1)}, u32[]{:S(2)}, u32[]{:S(2)}) %collective-permute-start.41) | collective-permute-done | bytes 65568 | tf_op jit(solution)/shard_map/ppermute | solution.py:21
  129.1 2.0 %finish_kernel.1 = bf16[256,768]{1,0:T(8,128)(2,1)} custom-call(s32[6]{0:T(128)S(1)} %stack.27.scalars, bf16[256,128]{1,0:T(8,128)(2,1)S(1)} %get-tuple-element.82.refs_0_, bf16[256,128]{1,0:T(8,128)(2,1)S(1)} %collective-permute-done.36.refs_1_, bf16[256,128]{1,0:T(8,128)(2,1)S(1)} %collective-permute-done.37.refs_2_, ...), custom_call_target="tpu_custom_call" | custom-call | flops 402653184 | bytes 2883584 | tf_op jit(solution)/shard_map/finish_kernel/pallas_call | solution.py:284
  (89 shorter events, 17.4 us)
Async XLA Ops:
  2.2 8.4 %collective-permute-start.3 = (bf16[256,384]{1,0:T(8,128)(2,1)S(1)}, bf16[256,384]{1,0:T(8,128)(2,1)S(1)}, u32[]{:S(2)}, u32[]{:S(2)}) collective-permute-start(bf16[256,384]{1,0:T(8,128)(2,1)S(1)} %get-tuple-element.50.p0), channel_id=1, source_target_pairs={{0,2},{2,0},{1,3},{3,1},{4,6},{6,4},{5,7},{7,5},{8,10},{10,8},{9,1... | collective-permute-start | bytes 589832 | tf_op jit(solution)/shard_map/ppermute | solution.py:21
  5.2 6.9 %collective-permute-start.2 = (bf16[256,384]{1,0:T(8,128)(2,1)S(1)}, bf16[256,384]{1,0:T(8,128)(2,1)S(1)}, u32[]{:S(2)}, u32[]{:S(2)}) collective-permute-start(bf16[256,384]{1,0:T(8,128)(2,1)S(1)} %get-tuple-element.50.p0), channel_id=1, source_target_pairs={{0,1},{1,0},{2,3},{3,2},{4,5},{5,4},{6,7},{7,6},{8,9},{9,8},{10,11... | collective-permute-start | bytes 589832 | tf_op jit(solution)/shard_map/ppermute | solution.py:21
  9.2 22.5 %slice-start = ((s8[10616832]{0:T(1024)(128)(4,1)}), s8[4194304]{0:T(1024)(128)(4,1)S(1)}, s32[]{:S(2)}) async-start(s8[10616832]{0:T(1024)(128)(4,1)} %bitcast.6), calls=%async_computation | async-start | bytes 8388608
  9.2 22.5 %slice-start.1 = ((s8[10616832]{0:T(1024)(128)(4,1)}), s8[4194304]{0:T(1024)(128)(4,1)S(1)}, s32[]{:S(2)}) async-start(s8[10616832]{0:T(1024)(128)(4,1)} %bitcast.6), calls=%async_computation.1 | async-start | bytes 8388608
  10.6 1.6 %collective-permute-start.4 = (bf16[256,384]{1,0:T(8,128)(2,1)S(1)}, bf16[256,384]{1,0:T(8,128)(2,1)S(1)}, u32[]{:S(2)}, u32[]{:S(2)}) collective-permute-start(bf16[256,384]{1,0:T(8,128)(2,1)S(1)} %collective-permute-done.3.p2), channel_id=1, source_target_pairs={{0,1},{1,0},{2,3},{3,2},{4,5},{5,4},{6,7},{7,6},{8,9},{9,8},{10,11... | collective-permute-start | bytes 589832 | tf_op jit(solution)/shard_map/ppermute | solution.py:21
  11.2 6.9 %collective-permute-start.1 = (bf16[256,384]{1,0:T(8,128)(2,1)S(1)}, bf16[256,384]{1,0:T(8,128)(2,1)S(1)}, u32[]{:S(2)}, u32[]{:S(2)}) collective-permute-start(bf16[256,384]{1,0:T(8,128)(2,1)S(1)} %get-tuple-element.49.p0), channel_id=1, source_target_pairs={{0,2},{2,0},{1,3},{3,1},{4,6},{6,4},{5,7},{7,5},{8,10},{10,8},{9,1... | collective-permute-start | bytes 589832 | tf_op jit(solution)/shard_map/ppermute | solution.py:21
  11.8 11.0 %collective-permute-start = (bf16[256,384]{1,0:T(8,128)(2,1)S(1)}, bf16[256,384]{1,0:T(8,128)(2,1)S(1)}, u32[]{:S(2)}, u32[]{:S(2)}) collective-permute-start(bf16[256,384]{1,0:T(8,128)(2,1)S(1)} %get-tuple-element.49.p0), channel_id=1, source_target_pairs={{0,1},{1,0},{2,3},{3,2},{4,5},{5,4},{6,7},{7,6},{8,9},{9,8},{10,11... | collective-permute-start | bytes 589832 | tf_op jit(solution)/shard_map/ppermute | solution.py:21
  18.1 4.8 %collective-permute-start.5 = (bf16[256,384]{1,0:T(8,128)(2,1)S(1)}, bf16[256,384]{1,0:T(8,128)(2,1)S(1)}, u32[]{:S(2)}, u32[]{:S(2)}) collective-permute-start(bf16[256,384]{1,0:T(8,128)(2,1)S(1)} %collective-permute-done.1.p2), channel_id=1, source_target_pairs={{0,1},{1,0},{2,3},{3,2},{4,5},{5,4},{6,7},{7,6},{8,9},{9,8},{10,11... | collective-permute-start | bytes 589832 | tf_op jit(solution)/shard_map/ppermute | solution.py:21
  18.1 7.6 %collective-permute-start.6 = (bf16[128,384]{1,0:T(8,128)(2,1)S(1)}, bf16[128,384]{1,0:T(8,128)(2,1)S(1)}, u32[]{:S(2)}, u32[]{:S(2)}) collective-permute-start(bf16[128,384]{1,0:T(8,128)(2,1)S(1)} %get-tuple-element.54), channel_id=1, source_target_pairs={{0,4},{4,8},{8,12},{1,5},{5,9},{9,13},{2,6},{6,10},{10,14},{3,7},{... | collective-permute-start | bytes 294920 | tf_op jit(solution)/shard_map/ppermute | solution.py:360
  21.6 6.8 %collective-permute-start.7 = (bf16[128,384]{1,0:T(8,128)(2,1)S(1)}, bf16[128,384]{1,0:T(8,128)(2,1)S(1)}, u32[]{:S(2)}, u32[]{:S(2)}) collective-permute-start(bf16[128,384]{1,0:T(8,128)(2,1)S(1)} %get-tuple-element.55), channel_id=1, source_target_pairs={{4,0},{8,4},{12,8},{5,1},{9,5},{13,9},{6,2},{10,6},{14,10},{7,3},{... | collective-permute-start | bytes 294920 | tf_op jit(solution)/shard_map/ppermute | solution.py:361
  29.0 7.7 %collective-permute-start.9 = (bf16[128,384]{1,0:T(8,128)(2,1)S(1)}, bf16[128,384]{1,0:T(8,128)(2,1)S(1)}, u32[]{:S(2)}, u32[]{:S(2)}) collective-permute-start(bf16[128,384]{1,0:T(8,128)(2,1)S(1)} %get-tuple-element.59), channel_id=1, source_target_pairs={{0,8},{4,12},{8,0},{12,4},{1,9},{5,13},{9,1},{13,5},{2,10},{6,14},... | collective-permute-start | bytes 294920 | tf_op jit(solution)/shard_map/ppermute | solution.py:30
  33.1 4.7 %collective-permute-start.10 = (bf16[128,384]{1,0:T(8,128)(2,1)S(1)}, bf16[128,384]{1,0:T(8,128)(2,1)S(1)}, u32[]{:S(2)}, u32[]{:S(2)}) collective-permute-start(bf16[128,384]{1,0:T(8,128)(2,1)S(1)} %get-tuple-element.60), channel_id=1, source_target_pairs={{0,12},{4,0},{8,4},{12,8},{1,13},{5,1},{9,5},{13,9},{2,14},{6,2},{... | collective-permute-start | bytes 294920 | tf_op jit(solution)/shard_map/ppermute | solution.py:30
  34.5 6.4 %collective-permute-start.8 = (bf16[128,384]{1,0:T(8,128)(2,1)S(1)}, bf16[128,384]{1,0:T(8,128)(2,1)S(1)}, u32[]{:S(2)}, u32[]{:S(2)}) collective-permute-start(bf16[128,384]{1,0:T(8,128)(2,1)S(1)} %get-tuple-element.57), channel_id=1, source_target_pairs={{0,4},{4,8},{8,12},{12,0},{1,5},{5,9},{9,13},{13,1},{2,6},{6,10},{... | collective-permute-start | bytes 294920 | tf_op jit(solution)/shard_map/ppermute | solution.py:30
  37.8 7.8 %collective-permute-start.14 = (bf16[256,384]{1,0:T(8,128)(2,1)S(1)}, bf16[256,384]{1,0:T(8,128)(2,1)S(1)}, u32[]{:S(2)}, u32[]{:S(2)}) collective-permute-start(bf16[256,384]{1,0:T(8,128)(2,1)S(1)} %constant_dynamic-update-slice_fusion.refs_1_), channel_id=1, source_target_pairs={{0,2},{2,0},{1,3},{3,1},{4,6},{6,4},{5,7},{7,5},{8,10},{10,8},{9,1... | collective-permute-start | bytes 589832 | tf_op jit(solution)/shard_map/ppermute | solution.py:21
  40.9 6.8 %collective-permute-start.13 = (bf16[256,384]{1,0:T(8,128)(2,1)S(1)}, bf16[256,384]{1,0:T(8,128)(2,1)S(1)}, u32[]{:S(2)}, u32[]{:S(2)}) collective-permute-start(bf16[256,384]{1,0:T(8,128)(2,1)S(1)} %pad_maximum_fusion.refs_0_), channel_id=1, source_target_pairs={{0,2},{2,0},{1,3},{3,1},{4,6},{6,4},{5,7},{7,5},{8,10},{10,8},{9,1... | collective-permute-start | bytes 589832 | tf_op jit(solution)/shard_map/ppermute | solution.py:21
  43.5 4.7 %collective-permute-start.12 = (bf16[256,384]{1,0:T(8,128)(2,1)S(1)}, bf16[256,384]{1,0:T(8,128)(2,1)S(1)}, u32[]{:S(2)}, u32[]{:S(2)}) collective-permute-start(bf16[256,384]{1,0:T(8,128)(2,1)S(1)} %constant_dynamic-update-slice_fusion.refs_1_), channel_id=1, source_target_pairs={{0,1},{1,0},{2,3},{3,2},{4,5},{5,4},{6,7},{7,6},{8,9},{9,8},{10,11... | collective-permute-start | bytes 589832 | tf_op jit(solution)/shard_map/ppermute | solution.py:21
  43.6 4.7 %collective-permute-start.11 = (bf16[256,384]{1,0:T(8,128)(2,1)S(1)}, bf16[256,384]{1,0:T(8,128)(2,1)S(1)}, u32[]{:S(2)}, u32[]{:S(2)}) collective-permute-start(bf16[256,384]{1,0:T(8,128)(2,1)S(1)} %pad_maximum_fusion.refs_0_), channel_id=1, source_target_pairs={{0,1},{1,0},{2,3},{3,2},{4,5},{5,4},{6,7},{7,6},{8,9},{9,8},{10,11... | collective-permute-start | bytes 589832 | tf_op jit(solution)/shard_map/ppermute | solution.py:21
  47.7 1.4 %collective-permute-start.15 = (bf16[256,384]{1,0:T(8,128)(2,1)S(1)}, bf16[256,384]{1,0:T(8,128)(2,1)S(1)}, u32[]{:S(2)}, u32[]{:S(2)}) collective-permute-start(bf16[256,384]{1,0:T(8,128)(2,1)S(1)} %collective-permute-done.13.refs_4_), channel_id=1, source_target_pairs={{0,1},{1,0},{2,3},{3,2},{4,5},{5,4},{6,7},{7,6},{8,9},{9,8},{10,11... | collective-permute-start | bytes 589832 | tf_op jit(solution)/shard_map/ppermute | solution.py:21
  47.7 1.7 %collective-permute-start.16 = (bf16[256,384]{1,0:T(8,128)(2,1)S(1)}, bf16[256,384]{1,0:T(8,128)(2,1)S(1)}, u32[]{:S(2)}, u32[]{:S(2)}) collective-permute-start(bf16[256,384]{1,0:T(8,128)(2,1)S(1)} %collective-permute-done.14.refs_5_), channel_id=1, source_target_pairs={{0,1},{1,0},{2,3},{3,2},{4,5},{5,4},{6,7},{7,6},{8,9},{9,8},{10,11... | collective-permute-start | bytes 589832 | tf_op jit(solution)/shard_map/ppermute | solution.py:21
  53.8 7.8 %collective-permute-start.19 = (bf16[256,384]{1,0:T(8,128)(2,1)S(1)}, bf16[256,384]{1,0:T(8,128)(2,1)S(1)}, u32[]{:S(2)}, u32[]{:S(2)}) collective-permute-start(bf16[256,384]{1,0:T(8,128)(2,1)S(1)} %get-tuple-element.63.refs_0_), channel_id=1, source_target_pairs={{0,2},{2,0},{1,3},{3,1},{4,6},{6,4},{5,7},{7,5},{8,10},{10,8},{9,1... | collective-permute-start | bytes 589832 | tf_op jit(solution)/shard_map/ppermute | solution.py:21
  54.9 10.2 %collective-permute-start.20 = (bf16[256,384]{1,0:T(8,128)(2,1)S(1)}, bf16[256,384]{1,0:T(8,128)(2,1)S(1)}, u32[]{:S(2)}, u32[]{:S(2)}) collective-permute-start(bf16[256,384]{1,0:T(8,128)(2,1)S(1)} %get-tuple-element.64.refs_1_), channel_id=1, source_target_pairs={{0,2},{2,0},{1,3},{3,1},{4,6},{6,4},{5,7},{7,5},{8,10},{10,8},{9,1... | collective-permute-start | bytes 589832 | tf_op jit(solution)/shard_map/ppermute | solution.py:21
  60.9 4.6 %collective-permute-start.17 = (bf16[256,384]{1,0:T(8,128)(2,1)S(1)}, bf16[256,384]{1,0:T(8,128)(2,1)S(1)}, u32[]{:S(2)}, u32[]{:S(2)}) collective-permute-start(bf16[256,384]{1,0:T(8,128)(2,1)S(1)} %get-tuple-element.63.refs_0_), channel_id=1, source_target_pairs={{0,1},{1,0},{2,3},{3,2},{4,5},{5,4},{6,7},{7,6},{8,9},{9,8},{10,11... | collective-permute-start | bytes 589832 | tf_op jit(solution)/shard_map/ppermute | solution.py:21
  60.9 4.6 %collective-permute-start.18 = (bf16[256,384]{1,0:T(8,128)(2,1)S(1)}, bf16[256,384]{1,0:T(8,128)(2,1)S(1)}, u32[]{:S(2)}, u32[]{:S(2)}) collective-permute-start(bf16[256,384]{1,0:T(8,128)(2,1)S(1)} %get-tuple-element.64.refs_1_), channel_id=1, source_target_pairs={{0,1},{1,0},{2,3},{3,2},{4,5},{5,4},{6,7},{7,6},{8,9},{9,8},{10,11... | collective-permute-start | bytes 589832 | tf_op jit(solution)/shard_map/ppermute | solution.py:21
  65.1 1.4 %collective-permute-start.21 = (bf16[256,384]{1,0:T(8,128)(2,1)S(1)}, bf16[256,384]{1,0:T(8,128)(2,1)S(1)}, u32[]{:S(2)}, u32[]{:S(2)}) collective-permute-start(bf16[256,384]{1,0:T(8,128)(2,1)S(1)} %collective-permute-done.19.refs_4_), channel_id=1, source_target_pairs={{0,1},{1,0},{2,3},{3,2},{4,5},{5,4},{6,7},{7,6},{8,9},{9,8},{10,11... | collective-permute-start | bytes 589832 | tf_op jit(solution)/shard_map/ppermute | solution.py:21
  65.1 1.7 %collective-permute-start.22 = (bf16[256,384]{1,0:T(8,128)(2,1)S(1)}, bf16[256,384]{1,0:T(8,128)(2,1)S(1)}, u32[]{:S(2)}, u32[]{:S(2)}) collective-permute-start(bf16[256,384]{1,0:T(8,128)(2,1)S(1)} %collective-permute-done.20.refs_5_), channel_id=1, source_target_pairs={{0,1},{1,0},{2,3},{3,2},{4,5},{5,4},{6,7},{7,6},{8,9},{9,8},{10,11... | collective-permute-start | bytes 589832 | tf_op jit(solution)/shard_map/ppermute | solution.py:21
  70.9 6.8 %collective-permute-start.26 = (bf16[128,384]{1,0:T(8,128)(2,1)S(1)}, bf16[128,384]{1,0:T(8,128)(2,1)S(1)}, u32[]{:S(2)}, u32[]{:S(2)}) collective-permute-start(bf16[128,384]{1,0:T(8,128)(2,1)S(1)} %get-tuple-element.70), channel_id=1, source_target_pairs={{0,4},{4,8},{8,12},{12,0},{1,5},{5,9},{9,13},{13,1},{2,6},{6,10},{... | collective-permute-start | bytes 294920 | tf_op jit(solution)/shard_map/ppermute | solution.py:30
  72.8 11.6 %collective-permute-start.23 = (bf16[256,384]{1,0:T(8,128)(2,1)S(1)}, bf16[256,384]{1,0:T(8,128)(2,1)S(1)}, u32[]{:S(2)}, u32[]{:S(2)}) collective-permute-start(bf16[256,384]{1,0:T(8,128)(2,1)S(1)} %get-tuple-element.68), channel_id=1, source_target_pairs={{0,1},{1,0},{2,3},{3,2},{4,5},{5,4},{6,7},{7,6},{8,9},{9,8},{10,11... | collective-permute-start | bytes 589832 | tf_op jit(solution)/shard_map/ppermute | solution.py:21
  72.8 11.6 %collective-permute-start.24 = (bf16[256,384]{1,0:T(8,128)(2,1)S(1)}, bf16[256,384]{1,0:T(8,128)(2,1)S(1)}, u32[]{:S(2)}, u32[]{:S(2)}) collective-permute-start(bf16[256,384]{1,0:T(8,128)(2,1)S(1)} %get-tuple-element.74.p0), channel_id=1, source_target_pairs={{0,2},{2,0},{1,3},{3,1},{4,6},{6,4},{5,7},{7,5},{8,10},{10,8},{9,1... | collective-permute-start | bytes 589832 | tf_op jit(solution)/shard_map/ppermute | solution.py:21
  73.9 10.5 %collective-permute-start.25 = (bf16[256,384]{1,0:T(8,128)(2,1)S(1)}, bf16[256,384]{1,0:T(8,128)(2,1)S(1)}, u32[]{:S(2)}, u32[]{:S(2)}) collective-permute-start(bf16[256,384]{1,0:T(8,128)(2,1)S(1)} %get-tuple-element.68), channel_id=1, source_target_pairs={{0,3},{1,2},{2,1},{3,0},{4,7},{5,6},{6,5},{7,4},{8,11},{9,10},{10,... | collective-permute-start | bytes 589832 | tf_op jit(solution)/shard_map/ppermute | solution.py:25
  74.7 7.8 %collective-permute-start.27 = (bf16[128,384]{1,0:T(8,128)(2,1)S(1)}, bf16[128,384]{1,0:T(8,128)(2,1)S(1)}, u32[]{:S(2)}, u32[]{:S(2)}) collective-permute-start(bf16[128,384]{1,0:T(8,128)(2,1)S(1)} %get-tuple-element.71), channel_id=1, source_target_pairs={{0,8},{4,12},{8,0},{12,4},{1,9},{5,13},{9,1},{13,5},{2,10},{6,14},... | collective-permute-start | bytes 294920 | tf_op jit(solution)/shard_map/ppermute | solution.py:30
  77.7 6.1 %collective-permute-start.28 = (bf16[128,384]{1,0:T(8,128)(2,1)S(1)}, bf16[128,384]{1,0:T(8,128)(2,1)S(1)}, u32[]{:S(2)}, u32[]{:S(2)}) collective-permute-start(bf16[128,384]{1,0:T(8,128)(2,1)S(1)} %get-tuple-element.72), channel_id=1, source_target_pairs={{0,12},{4,0},{8,4},{12,8},{1,13},{5,1},{9,5},{13,9},{2,14},{6,2},{... | collective-permute-start | bytes 294920 | tf_op jit(solution)/shard_map/ppermute | solution.py:30
  89.1 18.2 %collective-permute-start.44 = (bf16[256,768]{1,0:T(8,128)(2,1)S(1)}, bf16[256,768]{1,0:T(8,128)(2,1)S(1)}, u32[]{:S(2)}, u32[]{:S(2)}) collective-permute-start(bf16[256,768]{1,0:T(8,128)(2,1)S(1)} %dynamic_slice.6), channel_id=1, source_target_pairs={{0,2},{2,0},{1,3},{3,1},{4,6},{6,4},{5,7},{7,5},{8,10},{10,8},{9,1... | collective-permute-start | bytes 1179656 | tf_op jit(solution)/shard_map/ppermute | solution.py:21
  90.2 9.7 %collective-permute-start.29 = (bf16[256,384]{1,0:T(8,128)(2,1)S(1)}, bf16[256,384]{1,0:T(8,128)(2,1)S(1)}, u32[]{:S(2)}, u32[]{:S(2)}) collective-permute-start(bf16[256,384]{1,0:T(8,128)(2,1)S(1)} %get-tuple-element.79), channel_id=1, source_target_pairs={{0,4},{4,8},{8,12},{12,0},{1,5},{5,9},{9,13},{13,1},{2,6},{6,10},{... | collective-permute-start | bytes 589832 | tf_op jit(solution)/shard_map/ppermute | solution.py:30
  91.5 15.2 %collective-permute-start.30 = (bf16[256,384]{1,0:T(8,128)(2,1)S(1)}, bf16[256,384]{1,0:T(8,128)(2,1)S(1)}, u32[]{:S(2)}, u32[]{:S(2)}) collective-permute-start(bf16[256,384]{1,0:T(8,128)(2,1)S(1)} %get-tuple-element.80), channel_id=1, source_target_pairs={{0,8},{4,12},{8,0},{12,4},{1,9},{5,13},{9,1},{13,5},{2,10},{6,14},... | collective-permute-start | bytes 589832 | tf_op jit(solution)/shard_map/ppermute | solution.py:30
  93.7 13.1 %collective-permute-start.31 = (bf16[256,384]{1,0:T(8,128)(2,1)S(1)}, bf16[256,384]{1,0:T(8,128)(2,1)S(1)}, u32[]{:S(2)}, u32[]{:S(2)}) collective-permute-start(bf16[256,384]{1,0:T(8,128)(2,1)S(1)} %get-tuple-element.81), channel_id=1, source_target_pairs={{0,12},{4,0},{8,4},{12,8},{1,13},{5,1},{9,5},{13,9},{2,14},{6,2},{... | collective-permute-start | bytes 589832 | tf_op jit(solution)/shard_map/ppermute | solution.py:30
  94.0 13.4 %collective-permute-start.32 = (bf16[256,384]{1,0:T(8,128)(2,1)S(1)}, bf16[256,384]{1,0:T(8,128)(2,1)S(1)}, u32[]{:S(2)}, u32[]{:S(2)}) collective-permute-start(bf16[256,384]{1,0:T(8,128)(2,1)S(1)} %get-tuple-element.78.refs_0_), channel_id=1, source_target_pairs={{0,1},{1,0},{2,3},{3,2},{4,5},{5,4},{6,7},{7,6},{8,9},{9,8},{10,11... | collective-permute-start | bytes 589832 | tf_op jit(solution)/shard_map/ppermute | solution.py:21
  99.9 7.9 %collective-permute-start.33 = (bf16[256,384]{1,0:T(8,128)(2,1)S(1)}, bf16[256,384]{1,0:T(8,128)(2,1)S(1)}, u32[]{:S(2)}, u32[]{:S(2)}) collective-permute-start(bf16[256,384]{1,0:T(8,128)(2,1)S(1)} %collective-permute-done.29.refs_1_), channel_id=1, source_target_pairs={{0,1},{1,0},{2,3},{3,2},{4,5},{5,4},{6,7},{7,6},{8,9},{9,8},{10,11... | collective-permute-start | bytes 589832 | tf_op jit(solution)/shard_map/ppermute | solution.py:21
  106.8 1.4 %collective-permute-start.34 = (bf16[256,384]{1,0:T(8,128)(2,1)S(1)}, bf16[256,384]{1,0:T(8,128)(2,1)S(1)}, u32[]{:S(2)}, u32[]{:S(2)}) collective-permute-start(bf16[256,384]{1,0:T(8,128)(2,1)S(1)} %collective-permute-done.30.refs_2_), channel_id=1, source_target_pairs={{0,1},{1,0},{2,3},{3,2},{4,5},{5,4},{6,7},{7,6},{8,9},{9,8},{10,11... | collective-permute-start | bytes 589832 | tf_op jit(solution)/shard_map/ppermute | solution.py:21
  106.8 1.7 %collective-permute-start.35 = (bf16[256,384]{1,0:T(8,128)(2,1)S(1)}, bf16[256,384]{1,0:T(8,128)(2,1)S(1)}, u32[]{:S(2)}, u32[]{:S(2)}) collective-permute-start(bf16[256,384]{1,0:T(8,128)(2,1)S(1)} %collective-permute-done.31.refs_3_), channel_id=1, source_target_pairs={{0,1},{1,0},{2,3},{3,2},{4,5},{5,4},{6,7},{7,6},{8,9},{9,8},{10,11... | collective-permute-start | bytes 589832 | tf_op jit(solution)/shard_map/ppermute | solution.py:21
  107.3 18.6 %collective-permute-start.45 = (bf16[256,768]{1,0:T(8,128)(2,1)S(1)}, bf16[256,768]{1,0:T(8,128)(2,1)S(1)}, u32[]{:S(2)}, u32[]{:S(2)}) collective-permute-start(bf16[256,768]{1,0:T(8,128)(2,1)S(1)} %collective-permute-done.44.refs_11_), channel_id=1, source_target_pairs={{0,1},{1,0},{2,3},{3,2},{4,5},{5,4},{6,7},{7,6},{8,9},{9,8},{10,11... | collective-permute-start | bytes 1179656 | tf_op jit(solution)/shard_map/ppermute | solution.py:21
  107.4 12.8 %collective-permute-start.43 = (bf16[256,384]{1,0:T(8,128)(2,1)S(1)}, bf16[256,384]{1,0:T(8,128)(2,1)S(1)}, u32[]{:S(2)}, u32[]{:S(2)}) collective-permute-start(bf16[256,384]{1,0:T(8,128)(2,1)S(1)} %get-tuple-element.87), channel_id=1, source_target_pairs={{0,1},{1,0},{2,3},{3,2},{4,5},{5,4},{6,7},{7,6},{8,9},{9,8},{10,11... | collective-permute-start | bytes 589832 | tf_op jit(solution)/shard_map/ppermute | solution.py:21
  113.2 7.9 %collective-permute-start.36 = (bf16[256,128]{1,0:T(8,128)(2,1)S(1)}, bf16[256,128]{1,0:T(8,128)(2,1)S(1)}, u32[]{:S(2)}, u32[]{:S(2)}) collective-permute-start(bf16[256,128]{1,0:T(8,128)(2,1)S(1)} %get-tuple-element.83), channel_id=1, source_target_pairs={{0,4},{4,8},{8,12},{12,0},{1,5},{5,9},{9,13},{13,1},{2,6},{6,10},{... | collective-permute-start | bytes 196616 | tf_op jit(solution)/shard_map/ppermute | solution.py:30
  117.7 6.1 %collective-permute-start.37 = (bf16[256,128]{1,0:T(8,128)(2,1)S(1)}, bf16[256,128]{1,0:T(8,128)(2,1)S(1)}, u32[]{:S(2)}, u32[]{:S(2)}) collective-permute-start(bf16[256,128]{1,0:T(8,128)(2,1)S(1)} %get-tuple-element.84), channel_id=1, source_target_pairs={{0,8},{4,12},{8,0},{12,4},{1,9},{5,13},{9,1},{13,5},{2,10},{6,14},... | collective-permute-start | bytes 196616 | tf_op jit(solution)/shard_map/ppermute | solution.py:30
  118.5 6.3 %collective-permute-start.38 = (bf16[256,128]{1,0:T(8,128)(2,1)S(1)}, bf16[256,128]{1,0:T(8,128)(2,1)S(1)}, u32[]{:S(2)}, u32[]{:S(2)}) collective-permute-start(bf16[256,128]{1,0:T(8,128)(2,1)S(1)} %get-tuple-element.85), channel_id=1, source_target_pairs={{0,12},{4,0},{8,4},{12,8},{1,13},{5,1},{9,5},{13,9},{2,14},{6,2},{... | collective-permute-start | bytes 196616 | tf_op jit(solution)/shard_map/ppermute | solution.py:30
  120.1 5.7 %collective-permute-start.39 = (bf16[256,128]{1,0:T(8,128)(2,1)S(1)}, bf16[256,128]{1,0:T(8,128)(2,1)S(1)}, u32[]{:S(2)}, u32[]{:S(2)}) collective-permute-start(bf16[256,128]{1,0:T(8,128)(2,1)S(1)} %get-tuple-element.82.refs_0_), channel_id=1, source_target_pairs={{0,2},{2,0},{1,3},{3,1},{4,6},{6,4},{5,7},{7,5},{8,10},{10,8},{9,1... | collective-permute-start | bytes 196616 | tf_op jit(solution)/shard_map/ppermute | solution.py:21
  121.1 4.7 %collective-permute-start.40 = (bf16[256,128]{1,0:T(8,128)(2,1)S(1)}, bf16[256,128]{1,0:T(8,128)(2,1)S(1)}, u32[]{:S(2)}, u32[]{:S(2)}) collective-permute-start(bf16[256,128]{1,0:T(8,128)(2,1)S(1)} %collective-permute-done.36.refs_1_), channel_id=1, source_target_pairs={{0,2},{2,0},{1,3},{3,1},{4,6},{6,4},{5,7},{7,5},{8,10},{10,8},{9,1... | collective-permute-start | bytes 196616 | tf_op jit(solution)/shard_map/ppermute | solution.py:21
  123.8 4.6 %collective-permute-start.41 = (bf16[256,128]{1,0:T(8,128)(2,1)S(1)}, bf16[256,128]{1,0:T(8,128)(2,1)S(1)}, u32[]{:S(2)}, u32[]{:S(2)}) collective-permute-start(bf16[256,128]{1,0:T(8,128)(2,1)S(1)} %collective-permute-done.37.refs_2_), channel_id=1, source_target_pairs={{0,2},{2,0},{1,3},{3,1},{4,6},{6,4},{5,7},{7,5},{8,10},{10,8},{9,1... | collective-permute-start | bytes 196616 | tf_op jit(solution)/shard_map/ppermute | solution.py:21
  124.8 4.3 %collective-permute-start.42 = (bf16[256,128]{1,0:T(8,128)(2,1)S(1)}, bf16[256,128]{1,0:T(8,128)(2,1)S(1)}, u32[]{:S(2)}, u32[]{:S(2)}) collective-permute-start(bf16[256,128]{1,0:T(8,128)(2,1)S(1)} %collective-permute-done.38.refs_3_), channel_id=1, source_target_pairs={{0,2},{2,0},{1,3},{3,1},{4,6},{6,4},{5,7},{7,5},{8,10},{10,8},{9,1... | collective-permute-start | bytes 196616 | tf_op jit(solution)/shard_map/ppermute | solution.py:21
  (10 other events, 92.5 us)

commit v3 on v2

--- a/solution.py
+++ b/solution.py
@@ -46,7 +46,7 @@
     return pl.ds(pl.multiple_of(start, size), size)
 
 
-SUB, SEQ = 4, 5
+SUB, SEQ, MP = 4, 5, 6
 
 
 def fill_hidden(scalars, parts, gains, layer, hidden, order=None):
@@ -84,9 +84,9 @@
         copy.wait()
 
 
-def load_taps_kernel(layer, scalars, w, out, sems):
+def load_taps_kernel(layer, scalars, w, gains, out, gains_out, sems):
     size = out.shape[1] // SPLIT
-    copies = []
+    copies = [(gains, gains_out, sems.at[3, 0])]
     for tap in range(3):
         for i in range(SPLIT):
             rows = pl.ds(i * size, size)
@@ -94,13 +94,18 @@
     bring(copies)
 
 
-def load_projections_kernel(scalars, w_q, w_k, w_v, out, sems):
+def load_projections_kernel(scalars, w_q, w_k, w_v, w_o, out, own, asked, sems):
     size = out.shape[1] // SPLIT
     copies = []
     for m, w in enumerate((w_q, w_k, w_v)):
         for i in range(SPLIT):
             rows = pl.ds(i * size, size)
             copies.append((w.at[rows], out.at[m, rows], sems.at[m, i]))
+    half, width = asked.shape
+    mp = scalars[MP]
+    copies.append((w_o.at[:, at(mp * width, width)], own, sems.at[3, 0]))
+    rows = at(scalars[SUB] * half, half)
+    copies.append((w_o.at[rows, at((1 - mp) * width, width)], asked, sems.at[3, 1]))
     bring(copies)
 
 
@@ -115,14 +120,16 @@
     )
 
 
-def first_edge_kernel(scalars, p0, p1, p2, p3, gains, w, acc, up, down, hidden):
+def first_edge_kernel(scalars, p0, p1, p2, p3, gains, w, acc, outer, inner, hidden):
     fill_hidden(scalars, (p0, p1, p2, p3), gains, 0, hidden)
-    b = up.shape[0]
+    b = outer.shape[0]
     middle = p0[...].astype(F32) + dot(hidden[...], w[1])
     before = dot(hidden[...], w[0])
     after = dot(hidden[...], w[2])
-    up[...] = before[b:].astype(BF16)
-    down[...] = after[:b].astype(BF16)
+    odd = lax.rem(scalars[SEQ], 2) == 1
+    up, down = before[b:], after[:b]
+    outer[...] = jnp.where(odd, down, up).astype(BF16)
+    inner[...] = jnp.where(odd, up, down).astype(BF16)
     acc[0] = middle[:b]
     acc[1] = before[:b]
     acc[2] = after[b:]
@@ -143,12 +150,16 @@
     partial[3] = acc[3] + before[b:]
 
 
-def deal_kernel(scalars, partial, lower, upper, *refs):
+def deal_kernel(scalars, partial, outer, inner, *refs):
     outs, stream = refs[:4], refs[4]
-    stream[0] = (partial[0] + lower[...].astype(F32)).astype(BF16)
+    odd = lax.rem(scalars[SEQ], 2) == 1
+    from_outer, from_inner = outer[...].astype(F32), inner[...].astype(F32)
+    lower = jnp.where(odd, from_outer, from_inner)
+    upper = jnp.where(odd, from_inner, from_outer)
+    stream[0] = (partial[0] + lower).astype(BF16)
     stream[1] = partial[1].astype(BF16)
     stream[2] = partial[2].astype(BF16)
-    stream[3] = (partial[3] + upper[...].astype(F32)).astype(BF16)
+    stream[3] = (partial[3] + upper).astype(BF16)
     for s, out in enumerate(outs):
         out[...] = stream[turn(scalars, s)]
 
@@ -198,17 +209,6 @@
         out[...] = made[turn(scalars, s)]
 
 
-def sort_kernel(scalars, *refs):
-    arrived, keep, give, ordered = refs[:4], *refs[4:]
-    b = arrived[0].shape[0]
-    for s in range(4):
-        ordered[turn(scalars, 4 - s)] = arrived[s][...]
-    for a in range(2):
-        rows = slice(a * b, (a + 1) * b)
-        keep[rows, :] = ordered[2 * scalars[SUB] + a]
-        give[rows, :] = ordered[2 * (1 - scalars[SUB]) + a]
-
-
 def project_kernel(scalars, p0, p1, p2, p3, w, o0, o1, o2, o3, rows, made):
     width = p0.shape[1]
     for p, part in enumerate((p0, p1, p2, p3)):
@@ -222,11 +222,17 @@
 
 
 def attend_kernel(scalars, *refs):
-    own, other, outs = refs[:4], refs[4:8], refs[8:12]
-    queries, keys, values = refs[12:]
+    own, other, arrived, outs = refs[:4], refs[4:8], refs[8:12], refs[12:16]
+    keep, give, queries, keys, values, ordered = refs[16:]
+    b = own[0].shape[0] // 2
+    sub = scalars[SUB]
+    for s in range(4):
+        ordered[turn(scalars, 4 - s)] = arrived[s][...]
+    for a in range(2):
+        rows = slice(a * b, (a + 1) * b)
+        keep[rows, :] = ordered[2 * sub + a]
+        give[rows, :] = ordered[2 * (1 - sub) + a]
     rows = own[0].shape[0]
-    b = rows // 2
-    sub = scalars[SUB]
     for s in range(4):
         for c in range(2):
             queries[c, sub, s] = own[s][c * b : (c + 1) * b, :HEAD]
@@ -288,7 +294,7 @@
             num_scalar_prefetch=1,
             grid=(1,),
             in_specs=[
-                pl.BlockSpec(memory_space=pl.ANY) if i in far else whole(a)
+                pl.BlockSpec(memory_space=pltpu.HBM) if i in far else whole(a)
                 for i, a in enumerate(args)
             ],
             out_specs=[whole(o) for o in outs],
@@ -307,6 +313,10 @@
 
 
 def per_device_fast(seq_in, conv_gain, conv_weight, w_q, w_k, w_v, w_o):
+    seq_in, conv_gain, conv_weight, w_q, w_k, w_v, w_o = (
+        pltpu.with_memory_space_constraint(w, pltpu.HBM)
+        for w in (seq_in, conv_gain, conv_weight, w_q, w_k, w_v, w_o)
+    )
     rows, width = seq_in.shape
     channels = 4 * width
     n = 4
@@ -314,7 +324,7 @@
     half = rows // 2
     z, mp, sub = (lax.axis_index(a) for a in ("seq", "mp", "sub"))
     place = mp * 2 + sub
-    scalars = jnp.stack([place, place ^ 1, place ^ 2, place ^ 3, sub, z]).astype(jnp.int32)
+    scalars = jnp.stack([place, place ^ 1, place ^ 2, place ^ 3, sub, z, mp]).astype(jnp.int32)
     hidden = pltpu.VMEM((half, channels), BF16)
     hidden_all = pltpu.VMEM((rows, channels), BF16)
     summed = pltpu.VMEM((rows, width), F32)
@@ -322,19 +332,19 @@
     block = struct((b, width))
     flops = 2 * half * channels * 3 * width
     out_width = w_o.shape[1] // 2
-    sems = pltpu.SemaphoreType.DMA((3, SPLIT))
+    sems = pltpu.SemaphoreType.DMA((4, SPLIT))
 
     def load_taps(layer):
-        (w,) = call(
+        w, gains = call(
             functools.partial(load_taps_kernel, layer),
             scalars,
-            (conv_weight,),
-            [struct(conv_weight.shape[1:])],
+            (conv_weight, conv_gain),
+            [struct(conv_weight.shape[1:]), struct(conv_gain.shape, F32)],
             [sems],
             0,
-            far=(0,),
+            far=(0, 1),
         )
-        return w
+        return gains, w
 
     edge, middle = call(
         cut_kernel,
@@ -345,21 +355,19 @@
         0,
         far=(0,),
     )
-    taps = (conv_gain, load_taps(0))
-    edge_across = after(swap(edge, "mp"), taps[1])
-    middle_across = swap(middle, "mp")
-    middle_near = swap(middle, "sub")
-    acc, up, down = call(
+    taps = load_taps(0)
+    edge_across, middle_across = after(swap(edge, "mp"), taps[1]), swap(middle, "mp")
+    acc, outer, inner = call(
         first_edge_kernel,
         scalars,
         (edge, swap(edge, "sub"), edge_across, swap(edge_across, "sub"), *taps),
-        [struct((n, b, width), F32), struct((b, width)), struct((b, width))],
+        [struct((n, b, width), F32), block, block],
         [hidden],
         flops,
     )
-    lower = lax.ppermute(up, "seq", [(i, i + 1) for i in range(n - 1)])
-    upper = lax.ppermute(down, "seq", [(i + 1, i) for i in range(n - 1)])
-    middle_across = after(middle_across, acc)
+    outer = lax.ppermute(outer, "seq", [(i, i ^ 1) for i in range(n)])
+    inner = lax.ppermute(inner, "seq", [(1, 2), (2, 1)])
+    middle_near = swap(middle, "sub")
     (partial,) = call(
         first_middle_kernel,
         scalars,
@@ -371,50 +379,51 @@
     dealt = call(
         deal_kernel,
         scalars,
-        (partial, lower, upper),
+        (partial, outer, inner),
         [block] * n,
         [blocks],
         0,
     )
     dealt = [dealt[0]] + [rotate(dealt[s], s) for s in range(1, n)]
 
-    taps = (conv_gain, load_taps(1))
-    early = after(jnp.concatenate(dealt[:2], axis=0), taps[1])
+    taps = load_taps(1)
+    early = jnp.concatenate(dealt[:2], axis=0)
     late = jnp.concatenate(dealt[2:], axis=0)
-    next_taps = load_taps(2)
     low, high = call(
         second_kernel,
         scalars,
-        (*gather_parts(early, late, under=next_taps), *taps),
+        (*gather_parts(early, late, under=taps[1]), *taps),
         [struct((half, width))] * 2,
         [hidden_all, summed, blocks],
         flops * 2,
     )
-    (w_qkv,) = call(
+    w_qkv, w_own, asked = call(
         load_projections_kernel,
         scalars,
-        (w_q, w_k, w_v),
-        [struct((3, *w_q.shape))],
+        (w_q, w_k, w_v, w_o),
+        [
+            struct((3, *w_q.shape)),
+            struct((w_o.shape[0], out_width)),
+            struct((w_o.shape[0] // 2, out_width)),
+        ],
         [sems],
         0,
-        far=(0, 1, 2),
-    )
+        far=(0, 1, 2, 3),
+    )
+    taps = load_taps(2)
     mine, theirs, *back = call(
         third_kernel,
         scalars,
-        (*gather_parts(low, high, under=w_qkv), conv_gain, next_taps),
+        (*gather_parts(low, high, under=(taps[1], w_qkv)), *taps),
         [struct((half, width))] * 2 + [block] * n,
         [hidden_all, summed, blocks],
         flops * 2,
     )
 
+    near = swap(theirs, "sub")
+    back = [after(x, near) for x in back]
     back = [back[0]] + [rotate(back[s], s) for s in range(1, n)]
-    keep, give = call(
-        sort_kernel, scalars, back, [struct((half, width))] * 2, [blocks], 0
-    )
-
-    parts = (mine, swap(theirs, "sub"), swap(mine, "mp"), swap_both(theirs))
-    parts, keep = lax.optimization_barrier((parts, keep))
+    parts = (mine, near, swap(mine, "mp"), swap_both(theirs))
     projected = call(
         project_kernel,
         scalars,
@@ -423,32 +432,23 @@
         [pltpu.VMEM((half, channels), BF16), pltpu.VMEM((n, half, 3 * HEAD), BF16)],
         2 * half * channels * 3 * n * HEAD,
     )
+    projected, back = lax.optimization_barrier((projected, back))
     received = [projected[0]] + [rotate(projected[s], s) for s in range(1, n)]
-    got = swap(give, "sub")
-    last = projected[0]
-
-    w_o = after(w_o, last)
-    half_rows = w_o.shape[0] // 2
-    asked = lax.dynamic_slice(
-        w_o, (sub * half_rows, (1 - mp) * out_width), (half_rows, out_width)
-    )
-    w_own = lax.dynamic_slice_in_dim(w_o, mp * out_width, out_width, 1)
+    asked = after(asked, back[1])
     w_near = swap(asked, "mp")
     w_far = swap(w_near, "sub")
 
     swapped = [swap(x, "sub") for x in received]
     keys = pltpu.VMEM((8 * half, HEAD), BF16)
-    attended = call(
+    *attended, keep, give = call(
         attend_kernel,
         scalars,
-        (*received, *swapped),
-        [struct((half, HEAD))] * n,
-        [pltpu.VMEM((2, 2, n, b, HEAD), BF16), keys, keys],
+        (*received, *swapped, *back),
+        [struct((half, HEAD))] * n + [struct((half, width))] * 2,
+        [pltpu.VMEM((2, 2, n, b, HEAD), BF16), keys, keys, blocks],
         4 * half * 4 * 8 * half * HEAD,
     )
-    keep, got, w_near, w_far = lax.optimization_barrier(
-        (keep, got, w_near, w_far, attended[0])
-    )[:4]
+    got = swap(give, "sub")
     heads = [attended[0]] + [rotate(attended[s], s) for s in range(1, n)]
     others = [swap(x, "mp") for x in heads]
     (out,) = call(

time: 131 us -> 128 us (0.977)
  local copies, waits for them, and re-layouts: 9.75 us -> 0.14 us
  Pallas kernels: 32.2 us -> 36.4 us
  starting transfers between devices: 42.8 us -> 46.9 us
  waiting for transfers between devices: 45.9 us -> 44.2 us
    unnamed x25 -> x2, local copies, waits for them, and re-layouts: 9.56 us -> 0.02 us
    ppermute x12, starting transfers between devices: 19.1 us -> 27.3 us  [rotate(): return lax.ppermute(x, 'seq', [(i, (i + by) % n) for i in range(n)])]
    pallas_call x14 -> x13, Pallas kernels: 32.2 us -> 36.4 us  [call(): pl.pallas_call(kernel, out_shape=outs, grid_spec=pltpu.PrefetchScalarGrid...]
    ppermute x12, waiting for transfers between devices: 26.3 us -> 22.4 us  [rotate(): return lax.ppermute(x, 'seq', [(i, (i + by) % n) for i in range(n)])]
    ppermute x2, waiting for transfers between devices: 2.74 us -> 0.01 us  [the longest x1 0.01 us: per_device_fast(): outer = lax.ppermute(outer, 'seq', [(i, i ^ 1) for i in range(n)])]
    ppermute x1, waiting for transfers between devices: 0.01 us -> 2.66 us  [swap_both(): return lax.ppermute(x, ('mp', 'sub'), [(i, 3 - i) for i in range(4)])]
    ppermute x31, waiting for transfers between devices: 16.9 us -> 19.1 us  [swap(): return lax.ppermute(x, axis, [(0, 1), (1, 0)])]
    ppermute x2, starting transfers between devices: 4.77 us -> 2.55 us  [the longest x1 1.89 us: per_device_fast(): outer = lax.ppermute(outer, 'seq', [(i, i ^ 1) for i in range(n)])]
  transfers between devices with their start and end apart: 46 -> 46, of which waited for: 24 -> 21; matrix products, arithmetic and copies ran while one was open for 0% -> 0% of each run, Pallas kernels for 14% -> 19%
where the time goes in v3:
time: 128 us
  starting transfers between devices  46.9 us (37%)
  waiting for transfers between devices  44.2 us (35%)
  Pallas kernels  36.4 us (28%)
    pallas_call x13, Pallas kernels, call(): pl.pallas_call(kernel, out_shape=outs, grid_spec=pltpu.PrefetchScalarGrid...  36.4 us
    ppermute x12, starting transfers between devices, rotate(): return lax.ppermute(x, 'seq', [(i, (i + by) % n) for i in range(n)])  27.3 us
    ppermute x12, waiting for transfers between devices, rotate(): return lax.ppermute(x, 'seq', [(i, (i + by) % n) for i in range(n)])  22.4 us
    ppermute x31, waiting for transfers between devices, swap(): return lax.ppermute(x, axis, [(0, 1), (1, 0)])  19.1 us
    ppermute x31, starting transfers between devices, swap(): return lax.ppermute(x, axis, [(0, 1), (1, 0)])  17 us
    ppermute x1, waiting for transfers between devices, swap_both(): return lax.ppermute(x, ('mp', 'sub'), [(i, 3 - i) for i in range(4)])  2.66 us
  transfers between devices with their start and end apart: 46, of which 21 were waited for; matrix products, arithmetic and copies ran while one was open for 0% of the time, Pallas kernels for 19%

profile of v3, /device:TPU:0, one launch (start us, length us, event | category | flops | bytes accessed | tf_op | source)
XLA Modules:
  0.0 127.8 jit_solution(2681364470351776414)
XLA Ops:
  0.1 1.6 %cut_kernel.1 = (bf16[256,384]{1,0:T(8,128)(2,1)S(1)}, bf16[256,384]{1,0:T(8,128)(2,1)S(1)}) custom-call(s32[7]{0:T(128)S(1)} %stack.31.scalars, bf16[512,384]{1,0:T(8,128)(2,1)} %x.1), custom_call_target="tpu_custom_call" | custom-call | bytes 786432 | tf_op jit(solution)/shard_map/cut_kernel/pallas_call | solution.py:290
  1.7 3.0 %collective-permute-start.4 = (bf16[256,384]{1,0:T(8,128)(2,1)S(1)}, bf16[256,384]{1,0:T(8,128)(2,1)S(1)}, u32[]{:S(2)}, u32[]{:S(2)}) collective-permute-start(bf16[256,384]{1,0:T(8,128)(2,1)S(1)} %get-tuple-element.62.p0), channel_id=1, source_target_pairs={{0,2},{2,0},{1,3},{3,1},{4,6},{6,4},{5,7},{7,5},{8,10},{10,8},{9,1... | collective-permute-start | bytes 589832 | tf_op jit(solution)/shard_map/ppermute | solution.py:21
  4.8 2.6 %load_taps_kernel.3 = (bf16[3,1536,384]{2,1,0:T(8,128)(2,1)S(1)}, f32[3,1536]{1,0:T(4,128)S(1)}) custom-call(s32[7]{0:T(128)S(1)} %stack.31.scalars, bf16[3,3,1536,384]{3,2,1,0:T(8,128)(2,1)} %w.5, f32[3,1536]{1,0:T(4,128)} %gains.5), custom_call_target="tpu_custom_call" | custom-call | bytes 14192640 | tf_op jit(solution)/shard_map/load_taps_kernel/pallas_call | solution.py:290
  7.4 3.0 %collective-permute-done.4.p2 = bf16[256,384]{1,0:T(8,128)(2,1)S(1)} collective-permute-done((bf16[256,384]{1,0:T(8,128)(2,1)S(1)}, bf16[256,384]{1,0:T(8,128)(2,1)S(1)}, u32[]{:S(2)}, u32[]{:S(2)}) %collective-permute-start.4) | collective-permute-done | bytes 196640 | tf_op jit(solution)/shard_map/ppermute | solution.py:21
  10.9 2.9 %collective-permute-done.1.p2 = bf16[256,384]{1,0:T(8,128)(2,1)S(1)} collective-permute-done((bf16[256,384]{1,0:T(8,128)(2,1)S(1)}, bf16[256,384]{1,0:T(8,128)(2,1)S(1)}, u32[]{:S(2)}, u32[]{:S(2)}) %collective-permute-start.1) | collective-permute-done | bytes 196640 | tf_op jit(solution)/shard_map/ppermute | solution.py:21
  13.8 2.7 %first_edge_kernel.1 = (f32[4,128,384]{2,1,0:T(8,128)S(1)}, bf16[128,384]{1,0:T(8,128)(2,1)S(1)}, bf16[128,384]{1,0:T(8,128)(2,1)S(1)}) custom-call(s32[7]{0:T(128)S(1)} %stack.31.scalars, bf16[256,384]{1,0:T(8,128)(2,1)S(1)} %get-tuple-element.62.p0, bf16[256,384]{1,0:T(8,128)(2,1)S(1)} %collective-permute-done.3.p1, ...), custom_call_target="tpu_custom_call" | custom-call | flops 905969664 | bytes 5326848 | tf_op jit(solution)/shard_map/first_edge_kernel/pallas_call | solution.py:290
  16.6 1.9 %collective-permute-start.6 = (bf16[128,384]{1,0:T(8,128)(2,1)S(1)}, bf16[128,384]{1,0:T(8,128)(2,1)S(1)}, u32[]{:S(2)}, u32[]{:S(2)}) collective-permute-start(bf16[128,384]{1,0:T(8,128)(2,1)S(1)} %get-tuple-element.65), channel_id=1, source_target_pairs={{0,4},{4,0},{8,12},{12,8},{1,5},{5,1},{9,13},{13,9},{2,6},{6,2},{1... | collective-permute-start | bytes 294920 | tf_op jit(solution)/shard_map/ppermute | solution.py:368
  19.1 2.8 %first_middle_kernel.1.partial = f32[4,128,384]{2,1,0:T(8,128)S(1)} custom-call(s32[7]{0:T(128)S(1)} %stack.31.scalars, bf16[256,384]{1,0:T(8,128)(2,1)S(1)} %get-tuple-element.59.p0, bf16[256,384]{1,0:T(8,128)(2,1)S(1)} %collective-permute-done.p1, bf16[256,384]{1,0:T(8,128)(2,1)S(1)} %collective-permute-done.1.p2, ...), custom_call_target="tpu_custom_call" | custom-call | flops 905969664 | bytes 5916672 | tf_op jit(solution)/shard_map/first_middle_kernel/pallas_call | solution.py:290
  21.9 0.7 deal_kernel.1
  22.6 4.8 %collective-permute-start.8 = (bf16[128,384]{1,0:T(8,128)(2,1)S(1)}, bf16[128,384]{1,0:T(8,128)(2,1)S(1)}, u32[]{:S(2)}, u32[]{:S(2)}) collective-permute-start(bf16[128,384]{1,0:T(8,128)(2,1)S(1)} %get-tuple-element.68), channel_id=1, source_target_pairs={{0,4},{4,8},{8,12},{12,0},{1,5},{5,9},{9,13},{13,1},{2,6},{6,10},{... | collective-permute-start | bytes 294920 | tf_op jit(solution)/shard_map/ppermute | solution.py:30
  27.4 1.2 collective-permute-start.9
  28.7 2.8 %collective-permute-start.10 = (bf16[128,384]{1,0:T(8,128)(2,1)S(1)}, bf16[128,384]{1,0:T(8,128)(2,1)S(1)}, u32[]{:S(2)}, u32[]{:S(2)}) collective-permute-start(bf16[128,384]{1,0:T(8,128)(2,1)S(1)} %get-tuple-element.70), channel_id=1, source_target_pairs={{0,12},{4,0},{8,4},{12,8},{1,13},{5,1},{9,5},{13,9},{2,14},{6,2},{... | collective-permute-start | bytes 294920 | tf_op jit(solution)/shard_map/ppermute | solution.py:30
  31.5 4.1 %collective-permute-done.9 = bf16[128,384]{1,0:T(8,128)(2,1)S(1)} collective-permute-done((bf16[128,384]{1,0:T(8,128)(2,1)S(1)}, bf16[128,384]{1,0:T(8,128)(2,1)S(1)}, u32[]{:S(2)}, u32[]{:S(2)}) %collective-permute-start.9) | collective-permute-done | bytes 98336 | tf_op jit(solution)/shard_map/ppermute | solution.py:30
  35.6 1.6 %collective-permute-start.14 = (bf16[256,384]{1,0:T(8,128)(2,1)S(1)}, bf16[256,384]{1,0:T(8,128)(2,1)S(1)}, u32[]{:S(2)}, u32[]{:S(2)}) collective-permute-start(bf16[256,384]{1,0:T(8,128)(2,1)S(1)} %constant_dynamic-update-slice_fusion.2.refs_1_), channel_id=1, source_target_pairs={{0,2},{2,0},{1,3},{3,1},{4,6},{6,4},{5,7},{7,5},{8,10},{10,8},{9,1... | collective-permute-start | bytes 589832 | tf_op jit(solution)/shard_map/ppermute | solution.py:21
  37.8 2.6 %load_taps_kernel.4 = (bf16[3,1536,384]{2,1,0:T(8,128)(2,1)S(1)}, f32[3,1536]{1,0:T(4,128)S(1)}) custom-call(s32[7]{0:T(128)S(1)} %stack.31.scalars, bf16[3,3,1536,384]{3,2,1,0:T(8,128)(2,1)} %w.5, f32[3,1536]{1,0:T(4,128)} %gains.5), custom_call_target="tpu_custom_call" | custom-call | bytes 14192640 | tf_op jit(solution)/shard_map/load_taps_kernel/pallas_call | solution.py:290
  41.0 0.7 collective-permute-done.14.refs_5_
  41.7 2.1 %collective-permute-done.13.refs_4_ = bf16[256,384]{1,0:T(8,128)(2,1)S(1)} collective-permute-done((bf16[256,384]{1,0:T(8,128)(2,1)S(1)}, bf16[256,384]{1,0:T(8,128)(2,1)S(1)}, u32[]{:S(2)}, u32[]{:S(2)}) %collective-permute-start.13) | collective-permute-done | bytes 196640 | tf_op jit(solution)/shard_map/ppermute | solution.py:21
  44.3 0.9 collective-permute-done.15.refs_6_
  45.5 4.3 %second_kernel.1 = (bf16[256,384]{1,0:T(8,128)(2,1)S(1)}, bf16[256,384]{1,0:T(8,128)(2,1)S(1)}) custom-call(s32[7]{0:T(128)S(1)} %stack.31.scalars, bf16[256,384]{1,0:T(8,128)(2,1)S(1)} %constant_dynamic-update-slice_fusion.refs_0_, bf16[256,384]{1,0:T(8,128)(2,1)S(1)} %constant_dynamic-update-slice_fusion.2.refs_1_, ...), custom_call_target="tpu_custom_call" | custom-call | flops 1811939328 | bytes 5523456 | tf_op jit(solution)/shard_map/second_kernel/pallas_call | solution.py:290
  49.8 1.6 %collective-permute-start.19 = (bf16[256,384]{1,0:T(8,128)(2,1)S(1)}, bf16[256,384]{1,0:T(8,128)(2,1)S(1)}, u32[]{:S(2)}, u32[]{:S(2)}) collective-permute-start(bf16[256,384]{1,0:T(8,128)(2,1)S(1)} %get-tuple-element.75.refs_0_), channel_id=1, source_target_pairs={{0,2},{2,0},{1,3},{3,1},{4,6},{6,4},{5,7},{7,5},{8,10},{10,8},{9,1... | collective-permute-start | bytes 589832 | tf_op jit(solution)/shard_map/ppermute | solution.py:21
  51.9 2.6 %load_taps_kernel.5 = (bf16[3,1536,384]{2,1,0:T(8,128)(2,1)S(1)}, f32[3,1536]{1,0:T(4,128)S(1)}) custom-call(s32[7]{0:T(128)S(1)} %stack.31.scalars, bf16[3,3,1536,384]{3,2,1,0:T(8,128)(2,1)} %w.5, f32[3,1536]{1,0:T(4,128)} %gains.5), custom_call_target="tpu_custom_call" | custom-call | bytes 14192640 | tf_op jit(solution)/shard_map/load_taps_kernel/pallas_call | solution.py:290
  54.6 3.3 %load_projections_kernel.1 = (bf16[3,1536,512]{2,1,0:T(8,128)(2,1)S(1)}, bf16[512,768]{1,0:T(8,128)(2,1)S(1)}, bf16[256,768]{1,0:T(8,128)(2,1)S(1)}) custom-call(s32[7]{0:T(128)S(1)} %stack.31.scalars, bf16[1536,512]{1,0:T(8,128)(2,1)} %w_q.1, bf16[1536,512]{1,0:T(8,128)(2,1)} %w_k.1, bf16[1536,512]{1,0:T(8,128)(2,1)} %w_v.1, bf16[512,1536]{1,0:T(8,128)(2,1)} %w_o.1), custom_call_target="tpu_custom_call" | custom-call | bytes 12189696 | tf_op jit(solution)/shard_map/load_projections_kernel/pallas_call | solution.py:290
  58.5 2.7 %collective-permute-done.20.refs_5_ = bf16[256,384]{1,0:T(8,128)(2,1)S(1)} collective-permute-done((bf16[256,384]{1,0:T(8,128)(2,1)S(1)}, bf16[256,384]{1,0:T(8,128)(2,1)S(1)}, u32[]{:S(2)}, u32[]{:S(2)}) %collective-permute-start.20) | collective-permute-done | bytes 196640 | tf_op jit(solution)/shard_map/ppermute | solution.py:21
  61.7 0.9 collective-permute-done.21.refs_6_
  62.9 4.0 %third_kernel.1 = (bf16[256,384]{1,0:T(8,128)(2,1)S(1)}, bf16[256,384]{1,0:T(8,128)(2,1)S(1)}, bf16[128,384]{1,0:T(8,128)(2,1)S(1)}, bf16[128,384]{1,0:T(8,128)(...) custom-call(s32[7]{0:T(128)S(1)} %stack.31.scalars, ...), custom_call_target="tpu_custom_call" | custom-call | flops 1811939328 | bytes 5916672 | tf_op jit(solution)/shard_map/third_kernel/pallas_call | solution.py:290
  67.2 1.5 %collective-permute-start.24 = (bf16[256,384]{1,0:T(8,128)(2,1)S(1)}, bf16[256,384]{1,0:T(8,128)(2,1)S(1)}, u32[]{:S(2)}, u32[]{:S(2)}) collective-permute-start(bf16[256,384]{1,0:T(8,128)(2,1)S(1)} %get-tuple-element.82.p0), channel_id=1, source_target_pairs={{0,2},{2,0},{1,3},{3,1},{4,6},{6,4},{5,7},{7,5},{8,10},{10,8},{9,1... | collective-permute-start | bytes 589832 | tf_op jit(solution)/shard_map/ppermute | solution.py:21
  68.8 3.6 %collective-permute-start.26 = (bf16[128,384]{1,0:T(8,128)(2,1)S(1)}, bf16[128,384]{1,0:T(8,128)(2,1)S(1)}, u32[]{:S(2)}, u32[]{:S(2)}) collective-permute-start(bf16[128,384]{1,0:T(8,128)(2,1)S(1)} %get-tuple-element.91), channel_id=1, source_target_pairs={{0,4},{4,8},{8,12},{12,0},{1,5},{5,9},{9,13},{13,1},{2,6},{6,10},{... | collective-permute-start | bytes 294920 | tf_op jit(solution)/shard_map/ppermute | solution.py:30
  72.5 2.7 %collective-permute-start.27 = (bf16[128,384]{1,0:T(8,128)(2,1)S(1)}, bf16[128,384]{1,0:T(8,128)(2,1)S(1)}, u32[]{:S(2)}, u32[]{:S(2)}) collective-permute-start(bf16[128,384]{1,0:T(8,128)(2,1)S(1)} %get-tuple-element.93), channel_id=1, source_target_pairs={{0,8},{4,12},{8,0},{12,4},{1,9},{5,13},{9,1},{13,5},{2,10},{6,14},... | collective-permute-start | bytes 294920 | tf_op jit(solution)/shard_map/ppermute | solution.py:30
  75.2 2.7 %collective-permute-done.25.p3 = bf16[256,384]{1,0:T(8,128)(2,1)S(1)} collective-permute-done((bf16[256,384]{1,0:T(8,128)(2,1)S(1)}, bf16[256,384]{1,0:T(8,128)(2,1)S(1)}, u32[]{:S(2)}, u32[]{:S(2)}) %collective-permute-start.25) | collective-permute-done | bytes 196640 | tf_op jit(solution)/shard_map/ppermute | solution.py:25
  77.9 2.2 %project_kernel.1 = (bf16[256,384]{1,0:T(8,128)(2,1)S(1)}, bf16[256,384]{1,0:T(8,128)(2,1)S(1)}, bf16[256,384]{1,0:T(8,128)(2,1)S(1)}, bf16[256,384]{1,0:T(8,128)(2,1)S(1)}) custom-call(s32[7]{0:T(128)S(1)} %stack.31.scalars, bf16[256,384]{1,0:T(8,128)(2,1)S(1)} %get-tuple-element.82.p0, bf16[256,384]{1,0:T(8,128)(2,1)S(1)} %collective-permute-done.23.p1, ...), custom_call_target="tpu_custom_call" | custom-call | flops 1207959552 | bytes 6291456 | tf_op jit(solution)/shard_map/project_kernel/pallas_call | solution.py:290
  80.1 2.3 %collective-permute-done.27.refs_10_ = bf16[128,384]{1,0:T(8,128)(2,1)S(1)} collective-permute-done((bf16[128,384]{1,0:T(8,128)(2,1)S(1)}, bf16[128,384]{1,0:T(8,128)(2,1)S(1)}, u32[]{:S(2)}, u32[]{:S(2)}) %collective-permute-start.27) | collective-permute-done | bytes 98336 | tf_op jit(solution)/shard_map/ppermute | solution.py:30
  82.4 1.5 %collective-permute-start.44 = (bf16[256,768]{1,0:T(8,128)(2,1)S(1)}, bf16[256,768]{1,0:T(8,128)(2,1)S(1)}, u32[]{:S(2)}, u32[]{:S(2)}) collective-permute-start(bf16[256,768]{1,0:T(8,128)(2,1)S(1)} %get-tuple-element.112), channel_id=1, source_target_pairs={{0,2},{2,0},{1,3},{3,1},{4,6},{6,4},{5,7},{7,5},{8,10},{10,8},{9,1... | collective-permute-start | bytes 1179656 | tf_op jit(solution)/shard_map/ppermute | solution.py:21
  83.9 2.6 %collective-permute-start.29 = (bf16[256,384]{1,0:T(8,128)(2,1)S(1)}, bf16[256,384]{1,0:T(8,128)(2,1)S(1)}, u32[]{:S(2)}, u32[]{:S(2)}) collective-permute-start(bf16[256,384]{1,0:T(8,128)(2,1)S(1)} %get-tuple-element.97), channel_id=1, source_target_pairs={{0,4},{4,8},{8,12},{12,0},{1,5},{5,9},{9,13},{13,1},{2,6},{6,10},{... | collective-permute-start | bytes 589832 | tf_op jit(solution)/shard_map/ppermute | solution.py:30
  86.5 1.6 %collective-permute-start.30 = (bf16[256,384]{1,0:T(8,128)(2,1)S(1)}, bf16[256,384]{1,0:T(8,128)(2,1)S(1)}, u32[]{:S(2)}, u32[]{:S(2)}) collective-permute-start(bf16[256,384]{1,0:T(8,128)(2,1)S(1)} %get-tuple-element.98), channel_id=1, source_target_pairs={{0,8},{4,12},{8,0},{12,4},{1,9},{5,13},{9,1},{13,5},{2,10},{6,14},... | collective-permute-start | bytes 589832 | tf_op jit(solution)/shard_map/ppermute | solution.py:30
  88.0 0.8 collective-permute-start.31
  88.8 4.7 %collective-permute-done.29.refs_1_ = bf16[256,384]{1,0:T(8,128)(2,1)S(1)} collective-permute-done((bf16[256,384]{1,0:T(8,128)(2,1)S(1)}, bf16[256,384]{1,0:T(8,128)(2,1)S(1)}, u32[]{:S(2)}, u32[]{:S(2)}) %collective-permute-start.29) | collective-permute-done | bytes 196640 | tf_op jit(solution)/shard_map/ppermute | solution.py:30
  93.5 8.1 %collective-permute-done.30.refs_2_ = bf16[256,384]{1,0:T(8,128)(2,1)S(1)} collective-permute-done((bf16[256,384]{1,0:T(8,128)(2,1)S(1)}, bf16[256,384]{1,0:T(8,128)(2,1)S(1)}, u32[]{:S(2)}, u32[]{:S(2)}) %collective-permute-start.30) | collective-permute-done | bytes 196640 | tf_op jit(solution)/shard_map/ppermute | solution.py:30
  102.2 0.8 collective-permute-done.34.refs_6_
  103.3 4.8 %attend_kernel.1 = (bf16[256,128]{1,0:T(8,128)(2,1)S(1)}, bf16[256,128]{1,0:T(8,128)(2,1)S(1)}, bf16[256,128]{1,0:T(8,128)(2,1)S(1)}, bf16[256,128]{1,0:T(8,128)...) custom-call(s32[7]{0:T(128)S(1)} %stack.31.scalars, ...), custom_call_target="tpu_custom_call" | custom-call | flops 1073741824 | bytes 2621440 | tf_op jit(solution)/shard_map/attend_kernel/pallas_call | solution.py:290
  108.1 4.5 %collective-permute-start.36 = (bf16[256,128]{1,0:T(8,128)(2,1)S(1)}, bf16[256,128]{1,0:T(8,128)(2,1)S(1)}, u32[]{:S(2)}, u32[]{:S(2)}) collective-permute-start(bf16[256,128]{1,0:T(8,128)(2,1)S(1)} %get-tuple-element.105), channel_id=1, source_target_pairs={{0,4},{4,8},{8,12},{12,0},{1,5},{5,9},{9,13},{13,1},{2,6},{6,10},{... | collective-permute-start | bytes 196616 | tf_op jit(solution)/shard_map/ppermute | solution.py:30
  112.6 0.9 collective-permute-start.37
  113.5 1.7 %collective-permute-start.38 = (bf16[256,128]{1,0:T(8,128)(2,1)S(1)}, bf16[256,128]{1,0:T(8,128)(2,1)S(1)}, u32[]{:S(2)}, u32[]{:S(2)}) collective-permute-start(bf16[256,128]{1,0:T(8,128)(2,1)S(1)} %get-tuple-element.107), channel_id=1, source_target_pairs={{0,12},{4,0},{8,4},{12,8},{1,13},{5,1},{9,5},{13,9},{2,14},{6,2},{... | collective-permute-start | bytes 196616 | tf_op jit(solution)/shard_map/ppermute | solution.py:30
  115.9 3.1 %collective-permute-done.37.refs_2_ = bf16[256,128]{1,0:T(8,128)(2,1)S(1)} collective-permute-done((bf16[256,128]{1,0:T(8,128)(2,1)S(1)}, bf16[256,128]{1,0:T(8,128)(2,1)S(1)}, u32[]{:S(2)}, u32[]{:S(2)}) %collective-permute-start.37) | collective-permute-done | bytes 65568 | tf_op jit(solution)/shard_map/ppermute | solution.py:30
  119.6 1.5 %collective-permute-start.41 = (bf16[256,128]{1,0:T(8,128)(2,1)S(1)}, bf16[256,128]{1,0:T(8,128)(2,1)S(1)}, u32[]{:S(2)}, u32[]{:S(2)}) collective-permute-start(bf16[256,128]{1,0:T(8,128)(2,1)S(1)} %collective-permute-done.37.refs_2_), channel_id=1, source_target_pairs={{0,2},{2,0},{1,3},{3,1},{4,6},{6,4},{5,7},{7,5},{8,10},{10,8},{9,1... | collective-permute-start | bytes 196616 | tf_op jit(solution)/shard_map/ppermute | solution.py:21
  121.6 2.4 %collective-permute-done.40.refs_5_ = bf16[256,128]{1,0:T(8,128)(2,1)S(1)} collective-permute-done((bf16[256,128]{1,0:T(8,128)(2,1)S(1)}, bf16[256,128]{1,0:T(8,128)(2,1)S(1)}, u32[]{:S(2)}, u32[]{:S(2)}) %collective-permute-start.40) | collective-permute-done | bytes 65568 | tf_op jit(solution)/shard_map/ppermute | solution.py:21
  124.0 1.2 collective-permute-done.41.refs_6_
  125.1 0.7 collective-permute-done.42.refs_7_
  125.8 2.0 %finish_kernel.1 = bf16[256,768]{1,0:T(8,128)(2,1)} custom-call(s32[7]{0:T(128)S(1)} %stack.31.scalars, bf16[256,128]{1,0:T(8,128)(2,1)S(1)} %get-tuple-element.104.refs_0_, bf16[256,128]{1,0:T(8,128)(2,1)S(1)} %collective-permute-done.36.refs_1_, bf16[256,128]{1,0:T(8,128)(2,1)S(1)} %collective-permute-done.37.refs_2_, ...), custom_call_target="tpu_custom_call" | custom-call | flops 402653184 | bytes 2883584 | tf_op jit(solution)/shard_map/finish_kernel/pallas_call | solution.py:290
  (62 shorter events, 8.5 us)
Async XLA Ops:
  1.7 8.7 %collective-permute-start.4 = (bf16[256,384]{1,0:T(8,128)(2,1)S(1)}, bf16[256,384]{1,0:T(8,128)(2,1)S(1)}, u32[]{:S(2)}, u32[]{:S(2)}) collective-permute-start(bf16[256,384]{1,0:T(8,128)(2,1)S(1)} %get-tuple-element.62.p0), channel_id=1, source_target_pairs={{0,2},{2,0},{1,3},{3,1},{4,6},{6,4},{5,7},{7,5},{8,10},{10,8},{9,1... | collective-permute-start | bytes 589832 | tf_op jit(solution)/shard_map/ppermute | solution.py:21
  4.7 9.1 %collective-permute-start.1 = (bf16[256,384]{1,0:T(8,128)(2,1)S(1)}, bf16[256,384]{1,0:T(8,128)(2,1)S(1)}, u32[]{:S(2)}, u32[]{:S(2)}) collective-permute-start(bf16[256,384]{1,0:T(8,128)(2,1)S(1)} %get-tuple-element.59.p0), channel_id=1, source_target_pairs={{0,2},{2,0},{1,3},{3,1},{4,6},{6,4},{5,7},{7,5},{8,10},{10,8},{9,1... | collective-permute-start | bytes 589832 | tf_op jit(solution)/shard_map/ppermute | solution.py:21
  4.8 9.0 %collective-permute-start.3 = (bf16[256,384]{1,0:T(8,128)(2,1)S(1)}, bf16[256,384]{1,0:T(8,128)(2,1)S(1)}, u32[]{:S(2)}, u32[]{:S(2)}) collective-permute-start(bf16[256,384]{1,0:T(8,128)(2,1)S(1)} %get-tuple-element.62.p0), channel_id=1, source_target_pairs={{0,1},{1,0},{2,3},{3,2},{4,5},{5,4},{6,7},{7,6},{8,9},{9,8},{10,11... | collective-permute-start | bytes 589832 | tf_op jit(solution)/shard_map/ppermute | solution.py:21
  10.4 3.4 %collective-permute-start.5 = (bf16[256,384]{1,0:T(8,128)(2,1)S(1)}, bf16[256,384]{1,0:T(8,128)(2,1)S(1)}, u32[]{:S(2)}, u32[]{:S(2)}) collective-permute-start(bf16[256,384]{1,0:T(8,128)(2,1)S(1)} %collective-permute-done.4.p2), channel_id=1, source_target_pairs={{0,1},{1,0},{2,3},{3,2},{4,5},{5,4},{6,7},{7,6},{8,9},{9,8},{10,11... | collective-permute-start | bytes 589832 | tf_op jit(solution)/shard_map/ppermute | solution.py:21
  10.4 8.7 %collective-permute-start = (bf16[256,384]{1,0:T(8,128)(2,1)S(1)}, bf16[256,384]{1,0:T(8,128)(2,1)S(1)}, u32[]{:S(2)}, u32[]{:S(2)}) collective-permute-start(bf16[256,384]{1,0:T(8,128)(2,1)S(1)} %get-tuple-element.59.p0), channel_id=1, source_target_pairs={{0,1},{1,0},{2,3},{3,2},{4,5},{5,4},{6,7},{7,6},{8,9},{9,8},{10,11... | collective-permute-start | bytes 589832 | tf_op jit(solution)/shard_map/ppermute | solution.py:21
  13.8 5.3 %collective-permute-start.2 = (bf16[256,384]{1,0:T(8,128)(2,1)S(1)}, bf16[256,384]{1,0:T(8,128)(2,1)S(1)}, u32[]{:S(2)}, u32[]{:S(2)}) collective-permute-start(bf16[256,384]{1,0:T(8,128)(2,1)S(1)} %collective-permute-done.1.p2), channel_id=1, source_target_pairs={{0,1},{1,0},{2,3},{3,2},{4,5},{5,4},{6,7},{7,6},{8,9},{9,8},{10,11... | collective-permute-start | bytes 589832 | tf_op jit(solution)/shard_map/ppermute | solution.py:21
  16.6 5.4 %collective-permute-start.6 = (bf16[128,384]{1,0:T(8,128)(2,1)S(1)}, bf16[128,384]{1,0:T(8,128)(2,1)S(1)}, u32[]{:S(2)}, u32[]{:S(2)}) collective-permute-start(bf16[128,384]{1,0:T(8,128)(2,1)S(1)} %get-tuple-element.65), channel_id=1, source_target_pairs={{0,4},{4,0},{8,12},{12,8},{1,5},{5,1},{9,13},{13,9},{2,6},{6,2},{1... | collective-permute-start | bytes 294920 | tf_op jit(solution)/shard_map/ppermute | solution.py:368
  18.5 3.5 %collective-permute-start.7 = (bf16[128,384]{1,0:T(8,128)(2,1)S(1)}, bf16[128,384]{1,0:T(8,128)(2,1)S(1)}, u32[]{:S(2)}, u32[]{:S(2)}) collective-permute-start(bf16[128,384]{1,0:T(8,128)(2,1)S(1)} %get-tuple-element.66), channel_id=1, source_target_pairs={{4,8},{8,4},{5,9},{9,5},{6,10},{10,6},{7,11},{11,7},{20,24},{24,20... | collective-permute-start | bytes 294920 | tf_op jit(solution)/shard_map/ppermute | solution.py:369
  22.6 14.6 %collective-permute-start.8 = (bf16[128,384]{1,0:T(8,128)(2,1)S(1)}, bf16[128,384]{1,0:T(8,128)(2,1)S(1)}, u32[]{:S(2)}, u32[]{:S(2)}) collective-permute-start(bf16[128,384]{1,0:T(8,128)(2,1)S(1)} %get-tuple-element.68), channel_id=1, source_target_pairs={{0,4},{4,8},{8,12},{12,0},{1,5},{5,9},{9,13},{13,1},{2,6},{6,10},{... | collective-permute-start | bytes 294920 | tf_op jit(solution)/shard_map/ppermute | solution.py:30
  27.4 8.2 %collective-permute-start.9 = (bf16[128,384]{1,0:T(8,128)(2,1)S(1)}, bf16[128,384]{1,0:T(8,128)(2,1)S(1)}, u32[]{:S(2)}, u32[]{:S(2)}) collective-permute-start(bf16[128,384]{1,0:T(8,128)(2,1)S(1)} %get-tuple-element.69), channel_id=1, source_target_pairs={{0,8},{4,12},{8,0},{12,4},{1,9},{5,13},{9,1},{13,5},{2,10},{6,14},... | collective-permute-start | bytes 294920 | tf_op jit(solution)/shard_map/ppermute | solution.py:30
  28.7 6.9 %collective-permute-start.10 = (bf16[128,384]{1,0:T(8,128)(2,1)S(1)}, bf16[128,384]{1,0:T(8,128)(2,1)S(1)}, u32[]{:S(2)}, u32[]{:S(2)}) collective-permute-start(bf16[128,384]{1,0:T(8,128)(2,1)S(1)} %get-tuple-element.70), channel_id=1, source_target_pairs={{0,12},{4,0},{8,4},{12,8},{1,13},{5,1},{9,5},{13,9},{2,14},{6,2},{... | collective-permute-start | bytes 294920 | tf_op jit(solution)/shard_map/ppermute | solution.py:30
  35.6 6.1 %collective-permute-start.14 = (bf16[256,384]{1,0:T(8,128)(2,1)S(1)}, bf16[256,384]{1,0:T(8,128)(2,1)S(1)}, u32[]{:S(2)}, u32[]{:S(2)}) collective-permute-start(bf16[256,384]{1,0:T(8,128)(2,1)S(1)} %constant_dynamic-update-slice_fusion.2.refs_1_), channel_id=1, source_target_pairs={{0,2},{2,0},{1,3},{3,1},{4,6},{6,4},{5,7},{7,5},{8,10},{10,8},{9,1... | collective-permute-start | bytes 589832 | tf_op jit(solution)/shard_map/ppermute | solution.py:21
  37.2 6.6 %collective-permute-start.13 = (bf16[256,384]{1,0:T(8,128)(2,1)S(1)}, bf16[256,384]{1,0:T(8,128)(2,1)S(1)}, u32[]{:S(2)}, u32[]{:S(2)}) collective-permute-start(bf16[256,384]{1,0:T(8,128)(2,1)S(1)} %constant_dynamic-update-slice_fusion.refs_0_), channel_id=1, source_target_pairs={{0,2},{2,0},{1,3},{3,1},{4,6},{6,4},{5,7},{7,5},{8,10},{10,8},{9,1... | collective-permute-start | bytes 589832 | tf_op jit(solution)/shard_map/ppermute | solution.py:21
  40.5 3.9 %collective-permute-start.12 = (bf16[256,384]{1,0:T(8,128)(2,1)S(1)}, bf16[256,384]{1,0:T(8,128)(2,1)S(1)}, u32[]{:S(2)}, u32[]{:S(2)}) collective-permute-start(bf16[256,384]{1,0:T(8,128)(2,1)S(1)} %constant_dynamic-update-slice_fusion.2.refs_1_), channel_id=1, source_target_pairs={{0,1},{1,0},{2,3},{3,2},{4,5},{5,4},{6,7},{7,6},{8,9},{9,8},{10,11... | collective-permute-start | bytes 589832 | tf_op jit(solution)/shard_map/ppermute | solution.py:21
  40.5 3.8 %collective-permute-start.11 = (bf16[256,384]{1,0:T(8,128)(2,1)S(1)}, bf16[256,384]{1,0:T(8,128)(2,1)S(1)}, u32[]{:S(2)}, u32[]{:S(2)}) collective-permute-start(bf16[256,384]{1,0:T(8,128)(2,1)S(1)} %constant_dynamic-update-slice_fusion.refs_0_), channel_id=1, source_target_pairs={{0,1},{1,0},{2,3},{3,2},{4,5},{5,4},{6,7},{7,6},{8,9},{9,8},{10,11... | collective-permute-start | bytes 589832 | tf_op jit(solution)/shard_map/ppermute | solution.py:21
  43.8 1.4 %collective-permute-start.15 = (bf16[256,384]{1,0:T(8,128)(2,1)S(1)}, bf16[256,384]{1,0:T(8,128)(2,1)S(1)}, u32[]{:S(2)}, u32[]{:S(2)}) collective-permute-start(bf16[256,384]{1,0:T(8,128)(2,1)S(1)} %collective-permute-done.13.refs_4_), channel_id=1, source_target_pairs={{0,1},{1,0},{2,3},{3,2},{4,5},{5,4},{6,7},{7,6},{8,9},{9,8},{10,11... | collective-permute-start | bytes 589832 | tf_op jit(solution)/shard_map/ppermute | solution.py:21
  43.8 1.7 %collective-permute-start.16 = (bf16[256,384]{1,0:T(8,128)(2,1)S(1)}, bf16[256,384]{1,0:T(8,128)(2,1)S(1)}, u32[]{:S(2)}, u32[]{:S(2)}) collective-permute-start(bf16[256,384]{1,0:T(8,128)(2,1)S(1)} %collective-permute-done.14.refs_5_), channel_id=1, source_target_pairs={{0,1},{1,0},{2,3},{3,2},{4,5},{5,4},{6,7},{7,6},{8,9},{9,8},{10,11... | collective-permute-start | bytes 589832 | tf_op jit(solution)/shard_map/ppermute | solution.py:21
  49.8 8.7 %collective-permute-start.19 = (bf16[256,384]{1,0:T(8,128)(2,1)S(1)}, bf16[256,384]{1,0:T(8,128)(2,1)S(1)}, u32[]{:S(2)}, u32[]{:S(2)}) collective-permute-start(bf16[256,384]{1,0:T(8,128)(2,1)S(1)} %get-tuple-element.75.refs_0_), channel_id=1, source_target_pairs={{0,2},{2,0},{1,3},{3,1},{4,6},{6,4},{5,7},{7,5},{8,10},{10,8},{9,1... | collective-permute-start | bytes 589832 | tf_op jit(solution)/shard_map/ppermute | solution.py:21
  51.4 9.8 %collective-permute-start.20 = (bf16[256,384]{1,0:T(8,128)(2,1)S(1)}, bf16[256,384]{1,0:T(8,128)(2,1)S(1)}, u32[]{:S(2)}, u32[]{:S(2)}) collective-permute-start(bf16[256,384]{1,0:T(8,128)(2,1)S(1)} %get-tuple-element.76.refs_1_), channel_id=1, source_target_pairs={{0,2},{2,0},{1,3},{3,1},{4,6},{6,4},{5,7},{7,5},{8,10},{10,8},{9,1... | collective-permute-start | bytes 589832 | tf_op jit(solution)/shard_map/ppermute | solution.py:21
  57.9 3.7 %collective-permute-start.17 = (bf16[256,384]{1,0:T(8,128)(2,1)S(1)}, bf16[256,384]{1,0:T(8,128)(2,1)S(1)}, u32[]{:S(2)}, u32[]{:S(2)}) collective-permute-start(bf16[256,384]{1,0:T(8,128)(2,1)S(1)} %get-tuple-element.75.refs_0_), channel_id=1, source_target_pairs={{0,1},{1,0},{2,3},{3,2},{4,5},{5,4},{6,7},{7,6},{8,9},{9,8},{10,11... | collective-permute-start | bytes 589832 | tf_op jit(solution)/shard_map/ppermute | solution.py:21
  58.0 3.7 %collective-permute-start.18 = (bf16[256,384]{1,0:T(8,128)(2,1)S(1)}, bf16[256,384]{1,0:T(8,128)(2,1)S(1)}, u32[]{:S(2)}, u32[]{:S(2)}) collective-permute-start(bf16[256,384]{1,0:T(8,128)(2,1)S(1)} %get-tuple-element.76.refs_1_), channel_id=1, source_target_pairs={{0,1},{1,0},{2,3},{3,2},{4,5},{5,4},{6,7},{7,6},{8,9},{9,8},{10,11... | collective-permute-start | bytes 589832 | tf_op jit(solution)/shard_map/ppermute | solution.py:21
  61.1 1.4 %collective-permute-start.21 = (bf16[256,384]{1,0:T(8,128)(2,1)S(1)}, bf16[256,384]{1,0:T(8,128)(2,1)S(1)}, u32[]{:S(2)}, u32[]{:S(2)}) collective-permute-start(bf16[256,384]{1,0:T(8,128)(2,1)S(1)} %collective-permute-done.19.refs_4_), channel_id=1, source_target_pairs={{0,1},{1,0},{2,3},{3,2},{4,5},{5,4},{6,7},{7,6},{8,9},{9,8},{10,11... | collective-permute-start | bytes 589832 | tf_op jit(solution)/shard_map/ppermute | solution.py:21
  61.1 1.7 %collective-permute-start.22 = (bf16[256,384]{1,0:T(8,128)(2,1)S(1)}, bf16[256,384]{1,0:T(8,128)(2,1)S(1)}, u32[]{:S(2)}, u32[]{:S(2)}) collective-permute-start(bf16[256,384]{1,0:T(8,128)(2,1)S(1)} %collective-permute-done.20.refs_5_), channel_id=1, source_target_pairs={{0,1},{1,0},{2,3},{3,2},{4,5},{5,4},{6,7},{7,6},{8,9},{9,8},{10,11... | collective-permute-start | bytes 589832 | tf_op jit(solution)/shard_map/ppermute | solution.py:21
  66.9 1.9 %collective-permute-start.23 = (bf16[256,384]{1,0:T(8,128)(2,1)S(1)}, bf16[256,384]{1,0:T(8,128)(2,1)S(1)}, u32[]{:S(2)}, u32[]{:S(2)}) collective-permute-start(bf16[256,384]{1,0:T(8,128)(2,1)S(1)} %get-tuple-element.83), channel_id=1, source_target_pairs={{0,1},{1,0},{2,3},{3,2},{4,5},{5,4},{6,7},{7,6},{8,9},{9,8},{10,11... | collective-permute-start | bytes 589832 | tf_op jit(solution)/shard_map/ppermute | solution.py:21
  67.2 8.0 %collective-permute-start.24 = (bf16[256,384]{1,0:T(8,128)(2,1)S(1)}, bf16[256,384]{1,0:T(8,128)(2,1)S(1)}, u32[]{:S(2)}, u32[]{:S(2)}) collective-permute-start(bf16[256,384]{1,0:T(8,128)(2,1)S(1)} %get-tuple-element.82.p0), channel_id=1, source_target_pairs={{0,2},{2,0},{1,3},{3,1},{4,6},{6,4},{5,7},{7,5},{8,10},{10,8},{9,1... | collective-permute-start | bytes 589832 | tf_op jit(solution)/shard_map/ppermute | solution.py:21
  68.7 9.2 %collective-permute-start.25 = (bf16[256,384]{1,0:T(8,128)(2,1)S(1)}, bf16[256,384]{1,0:T(8,128)(2,1)S(1)}, u32[]{:S(2)}, u32[]{:S(2)}) collective-permute-start(bf16[256,384]{1,0:T(8,128)(2,1)S(1)} %get-tuple-element.83), channel_id=1, source_target_pairs={{0,3},{1,2},{2,1},{3,0},{4,7},{5,6},{6,5},{7,4},{8,11},{9,10},{10,... | collective-permute-start | bytes 589832 | tf_op jit(solution)/shard_map/ppermute | solution.py:25
  68.8 11.2 %collective-permute-start.26 = (bf16[128,384]{1,0:T(8,128)(2,1)S(1)}, bf16[128,384]{1,0:T(8,128)(2,1)S(1)}, u32[]{:S(2)}, u32[]{:S(2)}) collective-permute-start(bf16[128,384]{1,0:T(8,128)(2,1)S(1)} %get-tuple-element.91), channel_id=1, source_target_pairs={{0,4},{4,8},{8,12},{12,0},{1,5},{5,9},{9,13},{13,1},{2,6},{6,10},{... | collective-permute-start | bytes 294920 | tf_op jit(solution)/shard_map/ppermute | solution.py:30
  72.5 9.9 %collective-permute-start.27 = (bf16[128,384]{1,0:T(8,128)(2,1)S(1)}, bf16[128,384]{1,0:T(8,128)(2,1)S(1)}, u32[]{:S(2)}, u32[]{:S(2)}) collective-permute-start(bf16[128,384]{1,0:T(8,128)(2,1)S(1)} %get-tuple-element.93), channel_id=1, source_target_pairs={{0,8},{4,12},{8,0},{12,4},{1,9},{5,13},{9,1},{13,5},{2,10},{6,14},... | collective-permute-start | bytes 294920 | tf_op jit(solution)/shard_map/ppermute | solution.py:30
  75.2 7.2 %collective-permute-start.28 = (bf16[128,384]{1,0:T(8,128)(2,1)S(1)}, bf16[128,384]{1,0:T(8,128)(2,1)S(1)}, u32[]{:S(2)}, u32[]{:S(2)}) collective-permute-start(bf16[128,384]{1,0:T(8,128)(2,1)S(1)} %get-tuple-element.95), channel_id=1, source_target_pairs={{0,12},{4,0},{8,4},{12,8},{1,13},{5,1},{9,5},{13,9},{2,14},{6,2},{... | collective-permute-start | bytes 294920 | tf_op jit(solution)/shard_map/ppermute | solution.py:30
  82.4 19.7 %collective-permute-start.44 = (bf16[256,768]{1,0:T(8,128)(2,1)S(1)}, bf16[256,768]{1,0:T(8,128)(2,1)S(1)}, u32[]{:S(2)}, u32[]{:S(2)}) collective-permute-start(bf16[256,768]{1,0:T(8,128)(2,1)S(1)} %get-tuple-element.112), channel_id=1, source_target_pairs={{0,2},{2,0},{1,3},{3,1},{4,6},{6,4},{5,7},{7,5},{8,10},{10,8},{9,1... | collective-permute-start | bytes 1179656 | tf_op jit(solution)/shard_map/ppermute | solution.py:21
  83.9 9.6 %collective-permute-start.29 = (bf16[256,384]{1,0:T(8,128)(2,1)S(1)}, bf16[256,384]{1,0:T(8,128)(2,1)S(1)}, u32[]{:S(2)}, u32[]{:S(2)}) collective-permute-start(bf16[256,384]{1,0:T(8,128)(2,1)S(1)} %get-tuple-element.97), channel_id=1, source_target_pairs={{0,4},{4,8},{8,12},{12,0},{1,5},{5,9},{9,13},{13,1},{2,6},{6,10},{... | collective-permute-start | bytes 589832 | tf_op jit(solution)/shard_map/ppermute | solution.py:30
  86.5 15.1 %collective-permute-start.30 = (bf16[256,384]{1,0:T(8,128)(2,1)S(1)}, bf16[256,384]{1,0:T(8,128)(2,1)S(1)}, u32[]{:S(2)}, u32[]{:S(2)}) collective-permute-start(bf16[256,384]{1,0:T(8,128)(2,1)S(1)} %get-tuple-element.98), channel_id=1, source_target_pairs={{0,8},{4,12},{8,0},{12,4},{1,9},{5,13},{9,1},{13,5},{2,10},{6,14},... | collective-permute-start | bytes 589832 | tf_op jit(solution)/shard_map/ppermute | solution.py:30
  88.0 13.6 %collective-permute-start.31 = (bf16[256,384]{1,0:T(8,128)(2,1)S(1)}, bf16[256,384]{1,0:T(8,128)(2,1)S(1)}, u32[]{:S(2)}, u32[]{:S(2)}) collective-permute-start(bf16[256,384]{1,0:T(8,128)(2,1)S(1)} %get-tuple-element.99), channel_id=1, source_target_pairs={{0,12},{4,0},{8,4},{12,8},{1,13},{5,1},{9,5},{13,9},{2,14},{6,2},{... | collective-permute-start | bytes 589832 | tf_op jit(solution)/shard_map/ppermute | solution.py:30
  88.8 13.3 %collective-permute-start.32 = (bf16[256,384]{1,0:T(8,128)(2,1)S(1)}, bf16[256,384]{1,0:T(8,128)(2,1)S(1)}, u32[]{:S(2)}, u32[]{:S(2)}) collective-permute-start(bf16[256,384]{1,0:T(8,128)(2,1)S(1)} %get-tuple-element.96.refs_0_), channel_id=1, source_target_pairs={{0,1},{1,0},{2,3},{3,2},{4,5},{5,4},{6,7},{7,6},{8,9},{9,8},{10,11... | collective-permute-start | bytes 589832 | tf_op jit(solution)/shard_map/ppermute | solution.py:21
  93.5 8.7 %collective-permute-start.33 = (bf16[256,384]{1,0:T(8,128)(2,1)S(1)}, bf16[256,384]{1,0:T(8,128)(2,1)S(1)}, u32[]{:S(2)}, u32[]{:S(2)}) collective-permute-start(bf16[256,384]{1,0:T(8,128)(2,1)S(1)} %collective-permute-done.29.refs_1_), channel_id=1, source_target_pairs={{0,1},{1,0},{2,3},{3,2},{4,5},{5,4},{6,7},{7,6},{8,9},{9,8},{10,11... | collective-permute-start | bytes 589832 | tf_op jit(solution)/shard_map/ppermute | solution.py:21
  101.6 1.4 %collective-permute-start.34 = (bf16[256,384]{1,0:T(8,128)(2,1)S(1)}, bf16[256,384]{1,0:T(8,128)(2,1)S(1)}, u32[]{:S(2)}, u32[]{:S(2)}) collective-permute-start(bf16[256,384]{1,0:T(8,128)(2,1)S(1)} %collective-permute-done.30.refs_2_), channel_id=1, source_target_pairs={{0,1},{1,0},{2,3},{3,2},{4,5},{5,4},{6,7},{7,6},{8,9},{9,8},{10,11... | collective-permute-start | bytes 589832 | tf_op jit(solution)/shard_map/ppermute | solution.py:21
  101.6 1.7 %collective-permute-start.35 = (bf16[256,384]{1,0:T(8,128)(2,1)S(1)}, bf16[256,384]{1,0:T(8,128)(2,1)S(1)}, u32[]{:S(2)}, u32[]{:S(2)}) collective-permute-start(bf16[256,384]{1,0:T(8,128)(2,1)S(1)} %collective-permute-done.31.refs_3_), channel_id=1, source_target_pairs={{0,1},{1,0},{2,3},{3,2},{4,5},{5,4},{6,7},{7,6},{8,9},{9,8},{10,11... | collective-permute-start | bytes 589832 | tf_op jit(solution)/shard_map/ppermute | solution.py:21
  102.1 23.8 %collective-permute-start.45 = (bf16[256,768]{1,0:T(8,128)(2,1)S(1)}, bf16[256,768]{1,0:T(8,128)(2,1)S(1)}, u32[]{:S(2)}, u32[]{:S(2)}) collective-permute-start(bf16[256,768]{1,0:T(8,128)(2,1)S(1)} %collective-permute-done.44.refs_11_), channel_id=1, source_target_pairs={{0,1},{1,0},{2,3},{3,2},{4,5},{5,4},{6,7},{7,6},{8,9},{9,8},{10,11... | collective-permute-start | bytes 1179656 | tf_op jit(solution)/shard_map/ppermute | solution.py:21
  108.1 7.3 %collective-permute-start.36 = (bf16[256,128]{1,0:T(8,128)(2,1)S(1)}, bf16[256,128]{1,0:T(8,128)(2,1)S(1)}, u32[]{:S(2)}, u32[]{:S(2)}) collective-permute-start(bf16[256,128]{1,0:T(8,128)(2,1)S(1)} %get-tuple-element.105), channel_id=1, source_target_pairs={{0,4},{4,8},{8,12},{12,0},{1,5},{5,9},{9,13},{13,1},{2,6},{6,10},{... | collective-permute-start | bytes 196616 | tf_op jit(solution)/shard_map/ppermute | solution.py:30
  112.6 13.3 %collective-permute-start.43 = (bf16[256,384]{1,0:T(8,128)(2,1)S(1)}, bf16[256,384]{1,0:T(8,128)(2,1)S(1)}, u32[]{:S(2)}, u32[]{:S(2)}) collective-permute-start(bf16[256,384]{1,0:T(8,128)(2,1)S(1)} %get-tuple-element.109), channel_id=1, source_target_pairs={{0,1},{1,0},{2,3},{3,2},{4,5},{5,4},{6,7},{7,6},{8,9},{9,8},{10,11... | collective-permute-start | bytes 589832 | tf_op jit(solution)/shard_map/ppermute | solution.py:21
  112.6 6.4 %collective-permute-start.37 = (bf16[256,128]{1,0:T(8,128)(2,1)S(1)}, bf16[256,128]{1,0:T(8,128)(2,1)S(1)}, u32[]{:S(2)}, u32[]{:S(2)}) collective-permute-start(bf16[256,128]{1,0:T(8,128)(2,1)S(1)} %get-tuple-element.106), channel_id=1, source_target_pairs={{0,8},{4,12},{8,0},{12,4},{1,9},{5,13},{9,1},{13,5},{2,10},{6,14},... | collective-permute-start | bytes 196616 | tf_op jit(solution)/shard_map/ppermute | solution.py:30
  113.5 6.1 %collective-permute-start.38 = (bf16[256,128]{1,0:T(8,128)(2,1)S(1)}, bf16[256,128]{1,0:T(8,128)(2,1)S(1)}, u32[]{:S(2)}, u32[]{:S(2)}) collective-permute-start(bf16[256,128]{1,0:T(8,128)(2,1)S(1)} %get-tuple-element.107), channel_id=1, source_target_pairs={{0,12},{4,0},{8,4},{12,8},{1,13},{5,1},{9,5},{13,9},{2,14},{6,2},{... | collective-permute-start | bytes 196616 | tf_op jit(solution)/shard_map/ppermute | solution.py:30
  115.4 5.6 %collective-permute-start.39 = (bf16[256,128]{1,0:T(8,128)(2,1)S(1)}, bf16[256,128]{1,0:T(8,128)(2,1)S(1)}, u32[]{:S(2)}, u32[]{:S(2)}) collective-permute-start(bf16[256,128]{1,0:T(8,128)(2,1)S(1)} %get-tuple-element.104.refs_0_), channel_id=1, source_target_pairs={{0,2},{2,0},{1,3},{3,1},{4,6},{6,4},{5,7},{7,5},{8,10},{10,8},{9,1... | collective-permute-start | bytes 196616 | tf_op jit(solution)/shard_map/ppermute | solution.py:21
  119.0 5.0 %collective-permute-start.40 = (bf16[256,128]{1,0:T(8,128)(2,1)S(1)}, bf16[256,128]{1,0:T(8,128)(2,1)S(1)}, u32[]{:S(2)}, u32[]{:S(2)}) collective-permute-start(bf16[256,128]{1,0:T(8,128)(2,1)S(1)} %collective-permute-done.36.refs_1_), channel_id=1, source_target_pairs={{0,2},{2,0},{1,3},{3,1},{4,6},{6,4},{5,7},{7,5},{8,10},{10,8},{9,1... | collective-permute-start | bytes 196616 | tf_op jit(solution)/shard_map/ppermute | solution.py:21
  119.6 5.6 %collective-permute-start.41 = (bf16[256,128]{1,0:T(8,128)(2,1)S(1)}, bf16[256,128]{1,0:T(8,128)(2,1)S(1)}, u32[]{:S(2)}, u32[]{:S(2)}) collective-permute-start(bf16[256,128]{1,0:T(8,128)(2,1)S(1)} %collective-permute-done.37.refs_2_), channel_id=1, source_target_pairs={{0,2},{2,0},{1,3},{3,1},{4,6},{6,4},{5,7},{7,5},{8,10},{10,8},{9,1... | collective-permute-start | bytes 196616 | tf_op jit(solution)/shard_map/ppermute | solution.py:21
  121.1 4.8 %collective-permute-start.42 = (bf16[256,128]{1,0:T(8,128)(2,1)S(1)}, bf16[256,128]{1,0:T(8,128)(2,1)S(1)}, u32[]{:S(2)}, u32[]{:S(2)}) collective-permute-start(bf16[256,128]{1,0:T(8,128)(2,1)S(1)} %collective-permute-done.38.refs_3_), channel_id=1, source_target_pairs={{0,2},{2,0},{1,3},{3,1},{4,6},{6,4},{5,7},{7,5},{8,10},{10,8},{9,1... | collective-permute-start | bytes 196616 | tf_op jit(solution)/shard_map/ppermute | solution.py:21

commit v4 on v3

--- a/solution.py
+++ b/solution.py
@@ -111,13 +111,14 @@
 
 def cut_kernel(scalars, x, edge, middle, sems):
     b = edge.shape[0] // 2
-    bring(
-        [
-            (x.at[pl.ds(0, b)], edge.at[pl.ds(0, b)], sems.at[0]),
-            (x.at[pl.ds(3 * b, b)], edge.at[pl.ds(b, b)], sems.at[1]),
-            (x.at[pl.ds(b, 2 * b)], middle, sems.at[2]),
-        ]
-    )
+    size = 2 * b // SPLIT
+    copies = []
+    for i in range(SPLIT):
+        rows = pl.ds(i * size, size)
+        start = i * size if i * size < b else i * size + 2 * b
+        copies.append((x.at[pl.ds(start, size)], edge.at[rows], sems.at[0, i]))
+        copies.append((x.at[pl.ds(b + i * size, size)], middle.at[rows], sems.at[1, i]))
+    bring(copies)
 
 
 def first_edge_kernel(scalars, p0, p1, p2, p3, gains, w, acc, outer, inner, hidden):
@@ -244,17 +245,21 @@
     factor = math.log2(math.e) / math.sqrt(HEAD)
     for s, out in enumerate(outs):
         k = turn(scalars, s)
-        for a in range(2):
-            source = lax.rem(scalars[SEQ] - 2 * sub - a + 4, 4)
-            asked = queries[k // 2, lax.rem(k, 2), source]
-            scores = lax.dot_general(
-                asked, keys[...], (((1,), (1,)), ((), ())), preferred_element_type=F32
-            )
-            top = jnp.max(scores, axis=1, keepdims=True)
-            expw = jnp.exp2((scores - top) * factor)
-            denom = jnp.sum(expw, axis=1, keepdims=True)
-            numer = dot(expw.astype(BF16), values[...])
-            out[a * b : (a + 1) * b, :] = (numer / denom).astype(BF16)
+        asked = jnp.concatenate(
+            [
+                queries[k // 2, lax.rem(k, 2), lax.rem(scalars[SEQ] - 2 * sub - a + 4, 4)]
+                for a in range(2)
+            ],
+            axis=0,
+        )
+        scores = lax.dot_general(
+            asked, keys[...], (((1,), (1,)), ((), ())), preferred_element_type=F32
+        )
+        top = jnp.max(scores, axis=1, keepdims=True)
+        expw = jnp.exp2((scores - top) * factor)
+        denom = jnp.sum(expw, axis=1, keepdims=True)
+        numer = dot(expw.astype(BF16), values[...])
+        out[...] = (numer / denom).astype(BF16)
 
 
 def finish_kernel(scalars, *refs):
@@ -351,7 +356,7 @@
         scalars,
         (seq_in,),
         [struct((half, width))] * 2,
-        [pltpu.SemaphoreType.DMA((3,))],
+        [sems],
         0,
         far=(0,),
     )
@@ -450,7 +455,9 @@
     )
     got = swap(give, "sub")
     heads = [attended[0]] + [rotate(attended[s], s) for s in range(1, n)]
-    others = [swap(x, "mp") for x in heads]
+    others = [swap(heads[0], "mp")]
+    heads[2] = after(heads[2], others[0])
+    others += [swap(x, "mp") for x in heads[1:]]
     (out,) = call(
         finish_kernel,
         scalars,

time: 128 us -> 128 us (level)
  starting transfers between devices: 46.9 us -> 50.4 us
  waiting for transfers between devices: 44.2 us -> 40.9 us
    ppermute x12, starting transfers between devices: 27.3 us -> 30.6 us  [rotate(): return lax.ppermute(x, 'seq', [(i, (i + by) % n) for i in range(n)])]
    ppermute x12, waiting for transfers between devices: 22.4 us -> 20.3 us  [rotate(): return lax.ppermute(x, 'seq', [(i, (i + by) % n) for i in range(n)])]
  transfers between devices with their start and end apart: 46 -> 46, of which waited for: 21 -> 20; matrix products, arithmetic and copies ran while one was open for 0% -> 0% of each run, Pallas kernels for 19% -> 18%
where the time goes in v4:
time: 128 us; the launch traced here: 127 us
  starting transfers between devices  50.4 us (39%)
  waiting for transfers between devices  40.9 us (32%)
  Pallas kernels  35.7 us (28%)
    pallas_call x13, Pallas kernels, call(): pl.pallas_call(kernel, out_shape=outs, grid_spec=pltpu.PrefetchScalarGrid...  35.7 us
    ppermute x12, starting transfers between devices, rotate(): return lax.ppermute(x, 'seq', [(i, (i + by) % n) for i in range(n)])  30.6 us
    ppermute x12, waiting for transfers between devices, rotate(): return lax.ppermute(x, 'seq', [(i, (i + by) % n) for i in range(n)])  20.3 us
    ppermute x31, waiting for transfers between devices, swap(): return lax.ppermute(x, axis, [(0, 1), (1, 0)])  18 us
    ppermute x31, starting transfers between devices, swap(): return lax.ppermute(x, axis, [(0, 1), (1, 0)])  17.2 us
    ppermute x1, waiting for transfers between devices, swap_both(): return lax.ppermute(x, ('mp', 'sub'), [(i, 3 - i) for i in range(4)])  2.66 us
  transfers between devices with their start and end apart: 46, of which 20 were waited for; matrix products, arithmetic and copies ran while one was open for 0% of the time, Pallas kernels for 18%

profile of v4, /device:TPU:0, one launch (start us, length us, event | category | flops | bytes accessed | tf_op | source)
XLA Modules:
  0.0 127.4 jit_solution(14666678184343612559)
XLA Ops:
  0.1 1.6 %cut_kernel.1 = (bf16[256,384]{1,0:T(8,128)(2,1)S(1)}, bf16[256,384]{1,0:T(8,128)(2,1)S(1)}) custom-call(s32[7]{0:T(128)S(1)} %stack.31.scalars, bf16[512,384]{1,0:T(8,128)(2,1)} %x.1), custom_call_target="tpu_custom_call" | custom-call | bytes 786432 | tf_op jit(solution)/shard_map/cut_kernel/pallas_call | solution.py:295
  1.7 3.0 %collective-permute-start.4 = (bf16[256,384]{1,0:T(8,128)(2,1)S(1)}, bf16[256,384]{1,0:T(8,128)(2,1)S(1)}, u32[]{:S(2)}, u32[]{:S(2)}) collective-permute-start(bf16[256,384]{1,0:T(8,128)(2,1)S(1)} %get-tuple-element.63.p0), channel_id=1, source_target_pairs={{0,2},{2,0},{1,3},{3,1},{4,6},{6,4},{5,7},{7,5},{8,10},{10,8},{9,1... | collective-permute-start | bytes 589832 | tf_op jit(solution)/shard_map/ppermute | solution.py:21
  4.8 2.6 %load_taps_kernel.3 = (bf16[3,1536,384]{2,1,0:T(8,128)(2,1)S(1)}, f32[3,1536]{1,0:T(4,128)S(1)}) custom-call(s32[7]{0:T(128)S(1)} %stack.31.scalars, bf16[3,3,1536,384]{3,2,1,0:T(8,128)(2,1)} %w.5, f32[3,1536]{1,0:T(4,128)} %gains.5), custom_call_target="tpu_custom_call" | custom-call | bytes 14192640 | tf_op jit(solution)/shard_map/load_taps_kernel/pallas_call | solution.py:295
  7.5 3.0 %collective-permute-done.4.p2 = bf16[256,384]{1,0:T(8,128)(2,1)S(1)} collective-permute-done((bf16[256,384]{1,0:T(8,128)(2,1)S(1)}, bf16[256,384]{1,0:T(8,128)(2,1)S(1)}, u32[]{:S(2)}, u32[]{:S(2)}) %collective-permute-start.4) | collective-permute-done | bytes 196640 | tf_op jit(solution)/shard_map/ppermute | solution.py:21
  11.0 2.9 %collective-permute-done.1.p2 = bf16[256,384]{1,0:T(8,128)(2,1)S(1)} collective-permute-done((bf16[256,384]{1,0:T(8,128)(2,1)S(1)}, bf16[256,384]{1,0:T(8,128)(2,1)S(1)}, u32[]{:S(2)}, u32[]{:S(2)}) %collective-permute-start.1) | collective-permute-done | bytes 196640 | tf_op jit(solution)/shard_map/ppermute | solution.py:21
  13.9 2.8 %first_edge_kernel.1 = (f32[4,128,384]{2,1,0:T(8,128)S(1)}, bf16[128,384]{1,0:T(8,128)(2,1)S(1)}, bf16[128,384]{1,0:T(8,128)(2,1)S(1)}) custom-call(s32[7]{0:T(128)S(1)} %stack.31.scalars, bf16[256,384]{1,0:T(8,128)(2,1)S(1)} %get-tuple-element.63.p0, bf16[256,384]{1,0:T(8,128)(2,1)S(1)} %collective-permute-done.3.p1, ...), custom_call_target="tpu_custom_call" | custom-call | flops 905969664 | bytes 5326848 | tf_op jit(solution)/shard_map/first_edge_kernel/pallas_call | solution.py:295
  16.6 1.9 %collective-permute-start.6 = (bf16[128,384]{1,0:T(8,128)(2,1)S(1)}, bf16[128,384]{1,0:T(8,128)(2,1)S(1)}, u32[]{:S(2)}, u32[]{:S(2)}) collective-permute-start(bf16[128,384]{1,0:T(8,128)(2,1)S(1)} %get-tuple-element.66), channel_id=1, source_target_pairs={{0,4},{4,0},{8,12},{12,8},{1,5},{5,1},{9,13},{13,9},{2,6},{6,2},{1... | collective-permute-start | bytes 294920 | tf_op jit(solution)/shard_map/ppermute | solution.py:373
  19.2 2.8 %first_middle_kernel.1.partial = f32[4,128,384]{2,1,0:T(8,128)S(1)} custom-call(s32[7]{0:T(128)S(1)} %stack.31.scalars, bf16[256,384]{1,0:T(8,128)(2,1)S(1)} %get-tuple-element.60.p0, bf16[256,384]{1,0:T(8,128)(2,1)S(1)} %collective-permute-done.p1, bf16[256,384]{1,0:T(8,128)(2,1)S(1)} %collective-permute-done.1.p2, ...), custom_call_target="tpu_custom_call" | custom-call | flops 905969664 | bytes 5916672 | tf_op jit(solution)/shard_map/first_middle_kernel/pallas_call | solution.py:295
  22.0 0.7 deal_kernel.1
  22.7 4.8 %collective-permute-start.8 = (bf16[128,384]{1,0:T(8,128)(2,1)S(1)}, bf16[128,384]{1,0:T(8,128)(2,1)S(1)}, u32[]{:S(2)}, u32[]{:S(2)}) collective-permute-start(bf16[128,384]{1,0:T(8,128)(2,1)S(1)} %get-tuple-element.69), channel_id=1, source_target_pairs={{0,4},{4,8},{8,12},{12,0},{1,5},{5,9},{9,13},{13,1},{2,6},{6,10},{... | collective-permute-start | bytes 294920 | tf_op jit(solution)/shard_map/ppermute | solution.py:30
  27.5 1.2 collective-permute-start.9
  28.7 2.8 %collective-permute-start.10 = (bf16[128,384]{1,0:T(8,128)(2,1)S(1)}, bf16[128,384]{1,0:T(8,128)(2,1)S(1)}, u32[]{:S(2)}, u32[]{:S(2)}) collective-permute-start(bf16[128,384]{1,0:T(8,128)(2,1)S(1)} %get-tuple-element.71), channel_id=1, source_target_pairs={{0,12},{4,0},{8,4},{12,8},{1,13},{5,1},{9,5},{13,9},{2,14},{6,2},{... | collective-permute-start | bytes 294920 | tf_op jit(solution)/shard_map/ppermute | solution.py:30
  31.6 4.1 %collective-permute-done.9 = bf16[128,384]{1,0:T(8,128)(2,1)S(1)} collective-permute-done((bf16[128,384]{1,0:T(8,128)(2,1)S(1)}, bf16[128,384]{1,0:T(8,128)(2,1)S(1)}, u32[]{:S(2)}, u32[]{:S(2)}) %collective-permute-start.9) | collective-permute-done | bytes 98336 | tf_op jit(solution)/shard_map/ppermute | solution.py:30
  35.7 1.6 %collective-permute-start.14 = (bf16[256,384]{1,0:T(8,128)(2,1)S(1)}, bf16[256,384]{1,0:T(8,128)(2,1)S(1)}, u32[]{:S(2)}, u32[]{:S(2)}) collective-permute-start(bf16[256,384]{1,0:T(8,128)(2,1)S(1)} %constant_dynamic-update-slice_fusion.2.refs_1_), channel_id=1, source_target_pairs={{0,2},{2,0},{1,3},{3,1},{4,6},{6,4},{5,7},{7,5},{8,10},{10,8},{9,1... | collective-permute-start | bytes 589832 | tf_op jit(solution)/shard_map/ppermute | solution.py:21
  37.9 2.6 %load_taps_kernel.4 = (bf16[3,1536,384]{2,1,0:T(8,128)(2,1)S(1)}, f32[3,1536]{1,0:T(4,128)S(1)}) custom-call(s32[7]{0:T(128)S(1)} %stack.31.scalars, bf16[3,3,1536,384]{3,2,1,0:T(8,128)(2,1)} %w.5, f32[3,1536]{1,0:T(4,128)} %gains.5), custom_call_target="tpu_custom_call" | custom-call | bytes 14192640 | tf_op jit(solution)/shard_map/load_taps_kernel/pallas_call | solution.py:295
  41.7 2.1 %collective-permute-done.13.refs_4_ = bf16[256,384]{1,0:T(8,128)(2,1)S(1)} collective-permute-done((bf16[256,384]{1,0:T(8,128)(2,1)S(1)}, bf16[256,384]{1,0:T(8,128)(2,1)S(1)}, u32[]{:S(2)}, u32[]{:S(2)}) %collective-permute-start.13) | collective-permute-done | bytes 196640 | tf_op jit(solution)/shard_map/ppermute | solution.py:21
  44.4 0.9 collective-permute-done.15.refs_6_
  45.6 4.3 %second_kernel.1 = (bf16[256,384]{1,0:T(8,128)(2,1)S(1)}, bf16[256,384]{1,0:T(8,128)(2,1)S(1)}) custom-call(s32[7]{0:T(128)S(1)} %stack.31.scalars, bf16[256,384]{1,0:T(8,128)(2,1)S(1)} %constant_dynamic-update-slice_fusion.refs_0_, bf16[256,384]{1,0:T(8,128)(2,1)S(1)} %constant_dynamic-update-slice_fusion.2.refs_1_, ...), custom_call_target="tpu_custom_call" | custom-call | flops 1811939328 | bytes 5523456 | tf_op jit(solution)/shard_map/second_kernel/pallas_call | solution.py:295
  49.9 1.6 %collective-permute-start.19 = (bf16[256,384]{1,0:T(8,128)(2,1)S(1)}, bf16[256,384]{1,0:T(8,128)(2,1)S(1)}, u32[]{:S(2)}, u32[]{:S(2)}) collective-permute-start(bf16[256,384]{1,0:T(8,128)(2,1)S(1)} %get-tuple-element.76.refs_0_), channel_id=1, source_target_pairs={{0,2},{2,0},{1,3},{3,1},{4,6},{6,4},{5,7},{7,5},{8,10},{10,8},{9,1... | collective-permute-start | bytes 589832 | tf_op jit(solution)/shard_map/ppermute | solution.py:21
  52.0 2.6 %load_taps_kernel.5 = (bf16[3,1536,384]{2,1,0:T(8,128)(2,1)S(1)}, f32[3,1536]{1,0:T(4,128)S(1)}) custom-call(s32[7]{0:T(128)S(1)} %stack.31.scalars, bf16[3,3,1536,384]{3,2,1,0:T(8,128)(2,1)} %w.5, f32[3,1536]{1,0:T(4,128)} %gains.5), custom_call_target="tpu_custom_call" | custom-call | bytes 14192640 | tf_op jit(solution)/shard_map/load_taps_kernel/pallas_call | solution.py:295
  54.6 3.3 %load_projections_kernel.1 = (bf16[3,1536,512]{2,1,0:T(8,128)(2,1)S(1)}, bf16[512,768]{1,0:T(8,128)(2,1)S(1)}, bf16[256,768]{1,0:T(8,128)(2,1)S(1)}) custom-call(s32[7]{0:T(128)S(1)} %stack.31.scalars, bf16[1536,512]{1,0:T(8,128)(2,1)} %w_q.1, bf16[1536,512]{1,0:T(8,128)(2,1)} %w_k.1, bf16[1536,512]{1,0:T(8,128)(2,1)} %w_v.1, bf16[512,1536]{1,0:T(8,128)(2,1)} %w_o.1), custom_call_target="tpu_custom_call" | custom-call | bytes 12189696 | tf_op jit(solution)/shard_map/load_projections_kernel/pallas_call | solution.py:295
  58.5 2.7 %collective-permute-done.20.refs_5_ = bf16[256,384]{1,0:T(8,128)(2,1)S(1)} collective-permute-done((bf16[256,384]{1,0:T(8,128)(2,1)S(1)}, bf16[256,384]{1,0:T(8,128)(2,1)S(1)}, u32[]{:S(2)}, u32[]{:S(2)}) %collective-permute-start.20) | collective-permute-done | bytes 196640 | tf_op jit(solution)/shard_map/ppermute | solution.py:21
  61.7 0.9 collective-permute-done.21.refs_6_
  62.9 4.0 %third_kernel.1 = (bf16[256,384]{1,0:T(8,128)(2,1)S(1)}, bf16[256,384]{1,0:T(8,128)(2,1)S(1)}, bf16[128,384]{1,0:T(8,128)(2,1)S(1)}, bf16[128,384]{1,0:T(8,128)(...) custom-call(s32[7]{0:T(128)S(1)} %stack.31.scalars, ...), custom_call_target="tpu_custom_call" | custom-call | flops 1811939328 | bytes 5916672 | tf_op jit(solution)/shard_map/third_kernel/pallas_call | solution.py:295
  67.3 1.5 %collective-permute-start.24 = (bf16[256,384]{1,0:T(8,128)(2,1)S(1)}, bf16[256,384]{1,0:T(8,128)(2,1)S(1)}, u32[]{:S(2)}, u32[]{:S(2)}) collective-permute-start(bf16[256,384]{1,0:T(8,128)(2,1)S(1)} %get-tuple-element.83.p0), channel_id=1, source_target_pairs={{0,2},{2,0},{1,3},{3,1},{4,6},{6,4},{5,7},{7,5},{8,10},{10,8},{9,1... | collective-permute-start | bytes 589832 | tf_op jit(solution)/shard_map/ppermute | solution.py:21
  68.9 3.6 %collective-permute-start.26 = (bf16[128,384]{1,0:T(8,128)(2,1)S(1)}, bf16[128,384]{1,0:T(8,128)(2,1)S(1)}, u32[]{:S(2)}, u32[]{:S(2)}) collective-permute-start(bf16[128,384]{1,0:T(8,128)(2,1)S(1)} %get-tuple-element.92), channel_id=1, source_target_pairs={{0,4},{4,8},{8,12},{12,0},{1,5},{5,9},{9,13},{13,1},{2,6},{6,10},{... | collective-permute-start | bytes 294920 | tf_op jit(solution)/shard_map/ppermute | solution.py:30
  72.5 2.7 %collective-permute-start.27 = (bf16[128,384]{1,0:T(8,128)(2,1)S(1)}, bf16[128,384]{1,0:T(8,128)(2,1)S(1)}, u32[]{:S(2)}, u32[]{:S(2)}) collective-permute-start(bf16[128,384]{1,0:T(8,128)(2,1)S(1)} %get-tuple-element.94), channel_id=1, source_target_pairs={{0,8},{4,12},{8,0},{12,4},{1,9},{5,13},{9,1},{13,5},{2,10},{6,14},... | collective-permute-start | bytes 294920 | tf_op jit(solution)/shard_map/ppermute | solution.py:30
  75.3 2.7 %collective-permute-done.25.p3 = bf16[256,384]{1,0:T(8,128)(2,1)S(1)} collective-permute-done((bf16[256,384]{1,0:T(8,128)(2,1)S(1)}, bf16[256,384]{1,0:T(8,128)(2,1)S(1)}, u32[]{:S(2)}, u32[]{:S(2)}) %collective-permute-start.25) | collective-permute-done | bytes 196640 | tf_op jit(solution)/shard_map/ppermute | solution.py:25
  77.9 2.2 %project_kernel.1 = (bf16[256,384]{1,0:T(8,128)(2,1)S(1)}, bf16[256,384]{1,0:T(8,128)(2,1)S(1)}, bf16[256,384]{1,0:T(8,128)(2,1)S(1)}, bf16[256,384]{1,0:T(8,128)(2,1)S(1)}) custom-call(s32[7]{0:T(128)S(1)} %stack.31.scalars, bf16[256,384]{1,0:T(8,128)(2,1)S(1)} %get-tuple-element.83.p0, bf16[256,384]{1,0:T(8,128)(2,1)S(1)} %collective-permute-done.23.p1, ...), custom_call_target="tpu_custom_call" | custom-call | flops 1207959552 | bytes 6291456 | tf_op jit(solution)/shard_map/project_kernel/pallas_call | solution.py:295
  80.1 2.3 %collective-permute-done.27.refs_10_ = bf16[128,384]{1,0:T(8,128)(2,1)S(1)} collective-permute-done((bf16[128,384]{1,0:T(8,128)(2,1)S(1)}, bf16[128,384]{1,0:T(8,128)(2,1)S(1)}, u32[]{:S(2)}, u32[]{:S(2)}) %collective-permute-start.27) | collective-permute-done | bytes 98336 | tf_op jit(solution)/shard_map/ppermute | solution.py:30
  82.4 1.5 %collective-permute-start.44 = (bf16[256,768]{1,0:T(8,128)(2,1)S(1)}, bf16[256,768]{1,0:T(8,128)(2,1)S(1)}, u32[]{:S(2)}, u32[]{:S(2)}) collective-permute-start(bf16[256,768]{1,0:T(8,128)(2,1)S(1)} %get-tuple-element.114), channel_id=1, source_target_pairs={{0,2},{2,0},{1,3},{3,1},{4,6},{6,4},{5,7},{7,5},{8,10},{10,8},{9,1... | collective-permute-start | bytes 1179656 | tf_op jit(solution)/shard_map/ppermute | solution.py:21
  83.9 2.6 %collective-permute-start.29 = (bf16[256,384]{1,0:T(8,128)(2,1)S(1)}, bf16[256,384]{1,0:T(8,128)(2,1)S(1)}, u32[]{:S(2)}, u32[]{:S(2)}) collective-permute-start(bf16[256,384]{1,0:T(8,128)(2,1)S(1)} %get-tuple-element.98), channel_id=1, source_target_pairs={{0,4},{4,8},{8,12},{12,0},{1,5},{5,9},{9,13},{13,1},{2,6},{6,10},{... | collective-permute-start | bytes 589832 | tf_op jit(solution)/shard_map/ppermute | solution.py:30
  86.5 1.6 %collective-permute-start.30 = (bf16[256,384]{1,0:T(8,128)(2,1)S(1)}, bf16[256,384]{1,0:T(8,128)(2,1)S(1)}, u32[]{:S(2)}, u32[]{:S(2)}) collective-permute-start(bf16[256,384]{1,0:T(8,128)(2,1)S(1)} %get-tuple-element.99), channel_id=1, source_target_pairs={{0,8},{4,12},{8,0},{12,4},{1,9},{5,13},{9,1},{13,5},{2,10},{6,14},... | collective-permute-start | bytes 589832 | tf_op jit(solution)/shard_map/ppermute | solution.py:30
  88.1 0.8 collective-permute-start.31
  88.9 4.7 %collective-permute-done.29.refs_1_ = bf16[256,384]{1,0:T(8,128)(2,1)S(1)} collective-permute-done((bf16[256,384]{1,0:T(8,128)(2,1)S(1)}, bf16[256,384]{1,0:T(8,128)(2,1)S(1)}, u32[]{:S(2)}, u32[]{:S(2)}) %collective-permute-start.29) | collective-permute-done | bytes 196640 | tf_op jit(solution)/shard_map/ppermute | solution.py:30
  93.6 8.1 %collective-permute-done.30.refs_2_ = bf16[256,384]{1,0:T(8,128)(2,1)S(1)} collective-permute-done((bf16[256,384]{1,0:T(8,128)(2,1)S(1)}, bf16[256,384]{1,0:T(8,128)(2,1)S(1)}, u32[]{:S(2)}, u32[]{:S(2)}) %collective-permute-start.30) | collective-permute-done | bytes 196640 | tf_op jit(solution)/shard_map/ppermute | solution.py:30
  102.2 0.8 collective-permute-done.34.refs_6_
  103.4 4.1 %attend_kernel.1 = (bf16[256,128]{1,0:T(8,128)(2,1)S(1)}, bf16[256,128]{1,0:T(8,128)(2,1)S(1)}, bf16[256,128]{1,0:T(8,128)(2,1)S(1)}, bf16[256,128]{1,0:T(8,128)...) custom-call(s32[7]{0:T(128)S(1)} %stack.31.scalars, ...), custom_call_target="tpu_custom_call" | custom-call | flops 1073741824 | bytes 2621440 | tf_op jit(solution)/shard_map/attend_kernel/pallas_call | solution.py:295
  107.5 3.4 %collective-permute-start.37 = (bf16[256,128]{1,0:T(8,128)(2,1)S(1)}, bf16[256,128]{1,0:T(8,128)(2,1)S(1)}, u32[]{:S(2)}, u32[]{:S(2)}) collective-permute-start(bf16[256,128]{1,0:T(8,128)(2,1)S(1)} %get-tuple-element.107), channel_id=1, source_target_pairs={{0,8},{4,12},{8,0},{12,4},{1,9},{5,13},{9,1},{13,5},{2,10},{6,14},... | collective-permute-start | bytes 196616 | tf_op jit(solution)/shard_map/ppermute | solution.py:30
  111.4 1.9 %collective-permute-start.36 = (bf16[256,128]{1,0:T(8,128)(2,1)S(1)}, bf16[256,128]{1,0:T(8,128)(2,1)S(1)}, u32[]{:S(2)}, u32[]{:S(2)}) collective-permute-start(bf16[256,128]{1,0:T(8,128)(2,1)S(1)} %get-tuple-element.106), channel_id=1, source_target_pairs={{0,4},{4,8},{8,12},{12,0},{1,5},{5,9},{9,13},{13,1},{2,6},{6,10},{... | collective-permute-start | bytes 196616 | tf_op jit(solution)/shard_map/ppermute | solution.py:30
  113.3 5.0 %collective-permute-start.39 = (bf16[256,128]{1,0:T(8,128)(2,1)S(1)}, bf16[256,128]{1,0:T(8,128)(2,1)S(1)}, u32[]{:S(2)}, u32[]{:S(2)}) collective-permute-start(bf16[256,128]{1,0:T(8,128)(2,1)S(1)} %get-tuple-element.109), channel_id=1, source_target_pairs={{0,12},{4,0},{8,4},{12,8},{1,13},{5,1},{9,5},{13,9},{2,14},{6,2},{... | collective-permute-start | bytes 196616 | tf_op jit(solution)/shard_map/ppermute | solution.py:30
  118.4 0.7 collective-permute-start.40
  119.1 1.2 collective-permute-done.39.refs_3_
  120.8 1.5 %collective-permute-start.41 = (bf16[256,128]{1,0:T(8,128)(2,1)S(1)}, bf16[256,128]{1,0:T(8,128)(2,1)S(1)}, u32[]{:S(2)}, u32[]{:S(2)}) collective-permute-start(bf16[256,128]{1,0:T(8,128)(2,1)S(1)} %collective-permute-done.37.refs_2_), channel_id=1, source_target_pairs={{0,2},{2,0},{1,3},{3,1},{4,6},{6,4},{5,7},{7,5},{8,10},{10,8},{9,1... | collective-permute-start | bytes 196616 | tf_op jit(solution)/shard_map/ppermute | solution.py:21
  122.3 1.0 collective-permute-done.40.refs_5_
  123.4 1.3 %collective-permute-done.42.refs_7_ = bf16[256,128]{1,0:T(8,128)(2,1)S(1)} collective-permute-done((bf16[256,128]{1,0:T(8,128)(2,1)S(1)}, bf16[256,128]{1,0:T(8,128)(2,1)S(1)}, u32[]{:S(2)}, u32[]{:S(2)}) %collective-permute-start.42) | collective-permute-done | bytes 65568 | tf_op jit(solution)/shard_map/ppermute | solution.py:21
  124.7 0.7 collective-permute-done.41.refs_6_
  125.4 2.0 %finish_kernel.1 = bf16[256,768]{1,0:T(8,128)(2,1)} custom-call(s32[7]{0:T(128)S(1)} %stack.31.scalars, bf16[256,128]{1,0:T(8,128)(2,1)S(1)} %get-tuple-element.105.refs_0_, bf16[256,128]{1,0:T(8,128)(2,1)S(1)} %collective-permute-done.36.refs_1_, bf16[256,128]{1,0:T(8,128)(2,1)S(1)} %collective-permute-done.37.refs_2_, ...), custom_call_target="tpu_custom_call" | custom-call | flops 402653184 | bytes 2883584 | tf_op jit(solution)/shard_map/finish_kernel/pallas_call | solution.py:295
  (62 shorter events, 8.3 us)
Async XLA Ops:
  1.7 8.7 %collective-permute-start.4 = (bf16[256,384]{1,0:T(8,128)(2,1)S(1)}, bf16[256,384]{1,0:T(8,128)(2,1)S(1)}, u32[]{:S(2)}, u32[]{:S(2)}) collective-permute-start(bf16[256,384]{1,0:T(8,128)(2,1)S(1)} %get-tuple-element.63.p0), channel_id=1, source_target_pairs={{0,2},{2,0},{1,3},{3,1},{4,6},{6,4},{5,7},{7,5},{8,10},{10,8},{9,1... | collective-permute-start | bytes 589832 | tf_op jit(solution)/shard_map/ppermute | solution.py:21
  4.7 9.1 %collective-permute-start.1 = (bf16[256,384]{1,0:T(8,128)(2,1)S(1)}, bf16[256,384]{1,0:T(8,128)(2,1)S(1)}, u32[]{:S(2)}, u32[]{:S(2)}) collective-permute-start(bf16[256,384]{1,0:T(8,128)(2,1)S(1)} %get-tuple-element.60.p0), channel_id=1, source_target_pairs={{0,2},{2,0},{1,3},{3,1},{4,6},{6,4},{5,7},{7,5},{8,10},{10,8},{9,1... | collective-permute-start | bytes 589832 | tf_op jit(solution)/shard_map/ppermute | solution.py:21
  4.8 9.0 %collective-permute-start.3 = (bf16[256,384]{1,0:T(8,128)(2,1)S(1)}, bf16[256,384]{1,0:T(8,128)(2,1)S(1)}, u32[]{:S(2)}, u32[]{:S(2)}) collective-permute-start(bf16[256,384]{1,0:T(8,128)(2,1)S(1)} %get-tuple-element.63.p0), channel_id=1, source_target_pairs={{0,1},{1,0},{2,3},{3,2},{4,5},{5,4},{6,7},{7,6},{8,9},{9,8},{10,11... | collective-permute-start | bytes 589832 | tf_op jit(solution)/shard_map/ppermute | solution.py:21
  10.5 3.4 %collective-permute-start.5 = (bf16[256,384]{1,0:T(8,128)(2,1)S(1)}, bf16[256,384]{1,0:T(8,128)(2,1)S(1)}, u32[]{:S(2)}, u32[]{:S(2)}) collective-permute-start(bf16[256,384]{1,0:T(8,128)(2,1)S(1)} %collective-permute-done.4.p2), channel_id=1, source_target_pairs={{0,1},{1,0},{2,3},{3,2},{4,5},{5,4},{6,7},{7,6},{8,9},{9,8},{10,11... | collective-permute-start | bytes 589832 | tf_op jit(solution)/shard_map/ppermute | solution.py:21
  10.5 8.7 %collective-permute-start = (bf16[256,384]{1,0:T(8,128)(2,1)S(1)}, bf16[256,384]{1,0:T(8,128)(2,1)S(1)}, u32[]{:S(2)}, u32[]{:S(2)}) collective-permute-start(bf16[256,384]{1,0:T(8,128)(2,1)S(1)} %get-tuple-element.60.p0), channel_id=1, source_target_pairs={{0,1},{1,0},{2,3},{3,2},{4,5},{5,4},{6,7},{7,6},{8,9},{9,8},{10,11... | collective-permute-start | bytes 589832 | tf_op jit(solution)/shard_map/ppermute | solution.py:21
  13.9 5.3 %collective-permute-start.2 = (bf16[256,384]{1,0:T(8,128)(2,1)S(1)}, bf16[256,384]{1,0:T(8,128)(2,1)S(1)}, u32[]{:S(2)}, u32[]{:S(2)}) collective-permute-start(bf16[256,384]{1,0:T(8,128)(2,1)S(1)} %collective-permute-done.1.p2), channel_id=1, source_target_pairs={{0,1},{1,0},{2,3},{3,2},{4,5},{5,4},{6,7},{7,6},{8,9},{9,8},{10,11... | collective-permute-start | bytes 589832 | tf_op jit(solution)/shard_map/ppermute | solution.py:21
  16.6 5.4 %collective-permute-start.6 = (bf16[128,384]{1,0:T(8,128)(2,1)S(1)}, bf16[128,384]{1,0:T(8,128)(2,1)S(1)}, u32[]{:S(2)}, u32[]{:S(2)}) collective-permute-start(bf16[128,384]{1,0:T(8,128)(2,1)S(1)} %get-tuple-element.66), channel_id=1, source_target_pairs={{0,4},{4,0},{8,12},{12,8},{1,5},{5,1},{9,13},{13,9},{2,6},{6,2},{1... | collective-permute-start | bytes 294920 | tf_op jit(solution)/shard_map/ppermute | solution.py:373
  18.5 3.5 %collective-permute-start.7 = (bf16[128,384]{1,0:T(8,128)(2,1)S(1)}, bf16[128,384]{1,0:T(8,128)(2,1)S(1)}, u32[]{:S(2)}, u32[]{:S(2)}) collective-permute-start(bf16[128,384]{1,0:T(8,128)(2,1)S(1)} %get-tuple-element.67), channel_id=1, source_target_pairs={{4,8},{8,4},{5,9},{9,5},{6,10},{10,6},{7,11},{11,7},{20,24},{24,20... | collective-permute-start | bytes 294920 | tf_op jit(solution)/shard_map/ppermute | solution.py:374
  22.7 14.6 %collective-permute-start.8 = (bf16[128,384]{1,0:T(8,128)(2,1)S(1)}, bf16[128,384]{1,0:T(8,128)(2,1)S(1)}, u32[]{:S(2)}, u32[]{:S(2)}) collective-permute-start(bf16[128,384]{1,0:T(8,128)(2,1)S(1)} %get-tuple-element.69), channel_id=1, source_target_pairs={{0,4},{4,8},{8,12},{12,0},{1,5},{5,9},{9,13},{13,1},{2,6},{6,10},{... | collective-permute-start | bytes 294920 | tf_op jit(solution)/shard_map/ppermute | solution.py:30
  27.5 8.2 %collective-permute-start.9 = (bf16[128,384]{1,0:T(8,128)(2,1)S(1)}, bf16[128,384]{1,0:T(8,128)(2,1)S(1)}, u32[]{:S(2)}, u32[]{:S(2)}) collective-permute-start(bf16[128,384]{1,0:T(8,128)(2,1)S(1)} %get-tuple-element.70), channel_id=1, source_target_pairs={{0,8},{4,12},{8,0},{12,4},{1,9},{5,13},{9,1},{13,5},{2,10},{6,14},... | collective-permute-start | bytes 294920 | tf_op jit(solution)/shard_map/ppermute | solution.py:30
  28.7 6.9 %collective-permute-start.10 = (bf16[128,384]{1,0:T(8,128)(2,1)S(1)}, bf16[128,384]{1,0:T(8,128)(2,1)S(1)}, u32[]{:S(2)}, u32[]{:S(2)}) collective-permute-start(bf16[128,384]{1,0:T(8,128)(2,1)S(1)} %get-tuple-element.71), channel_id=1, source_target_pairs={{0,12},{4,0},{8,4},{12,8},{1,13},{5,1},{9,5},{13,9},{2,14},{6,2},{... | collective-permute-start | bytes 294920 | tf_op jit(solution)/shard_map/ppermute | solution.py:30
  35.7 6.1 %collective-permute-start.14 = (bf16[256,384]{1,0:T(8,128)(2,1)S(1)}, bf16[256,384]{1,0:T(8,128)(2,1)S(1)}, u32[]{:S(2)}, u32[]{:S(2)}) collective-permute-start(bf16[256,384]{1,0:T(8,128)(2,1)S(1)} %constant_dynamic-update-slice_fusion.2.refs_1_), channel_id=1, source_target_pairs={{0,2},{2,0},{1,3},{3,1},{4,6},{6,4},{5,7},{7,5},{8,10},{10,8},{9,1... | collective-permute-start | bytes 589832 | tf_op jit(solution)/shard_map/ppermute | solution.py:21
  37.3 6.6 %collective-permute-start.13 = (bf16[256,384]{1,0:T(8,128)(2,1)S(1)}, bf16[256,384]{1,0:T(8,128)(2,1)S(1)}, u32[]{:S(2)}, u32[]{:S(2)}) collective-permute-start(bf16[256,384]{1,0:T(8,128)(2,1)S(1)} %constant_dynamic-update-slice_fusion.refs_0_), channel_id=1, source_target_pairs={{0,2},{2,0},{1,3},{3,1},{4,6},{6,4},{5,7},{7,5},{8,10},{10,8},{9,1... | collective-permute-start | bytes 589832 | tf_op jit(solution)/shard_map/ppermute | solution.py:21
  40.5 3.9 %collective-permute-start.12 = (bf16[256,384]{1,0:T(8,128)(2,1)S(1)}, bf16[256,384]{1,0:T(8,128)(2,1)S(1)}, u32[]{:S(2)}, u32[]{:S(2)}) collective-permute-start(bf16[256,384]{1,0:T(8,128)(2,1)S(1)} %constant_dynamic-update-slice_fusion.2.refs_1_), channel_id=1, source_target_pairs={{0,1},{1,0},{2,3},{3,2},{4,5},{5,4},{6,7},{7,6},{8,9},{9,8},{10,11... | collective-permute-start | bytes 589832 | tf_op jit(solution)/shard_map/ppermute | solution.py:21
  40.6 3.8 %collective-permute-start.11 = (bf16[256,384]{1,0:T(8,128)(2,1)S(1)}, bf16[256,384]{1,0:T(8,128)(2,1)S(1)}, u32[]{:S(2)}, u32[]{:S(2)}) collective-permute-start(bf16[256,384]{1,0:T(8,128)(2,1)S(1)} %constant_dynamic-update-slice_fusion.refs_0_), channel_id=1, source_target_pairs={{0,1},{1,0},{2,3},{3,2},{4,5},{5,4},{6,7},{7,6},{8,9},{9,8},{10,11... | collective-permute-start | bytes 589832 | tf_op jit(solution)/shard_map/ppermute | solution.py:21
  43.9 1.4 %collective-permute-start.15 = (bf16[256,384]{1,0:T(8,128)(2,1)S(1)}, bf16[256,384]{1,0:T(8,128)(2,1)S(1)}, u32[]{:S(2)}, u32[]{:S(2)}) collective-permute-start(bf16[256,384]{1,0:T(8,128)(2,1)S(1)} %collective-permute-done.13.refs_4_), channel_id=1, source_target_pairs={{0,1},{1,0},{2,3},{3,2},{4,5},{5,4},{6,7},{7,6},{8,9},{9,8},{10,11... | collective-permute-start | bytes 589832 | tf_op jit(solution)/shard_map/ppermute | solution.py:21
  43.9 1.7 %collective-permute-start.16 = (bf16[256,384]{1,0:T(8,128)(2,1)S(1)}, bf16[256,384]{1,0:T(8,128)(2,1)S(1)}, u32[]{:S(2)}, u32[]{:S(2)}) collective-permute-start(bf16[256,384]{1,0:T(8,128)(2,1)S(1)} %collective-permute-done.14.refs_5_), channel_id=1, source_target_pairs={{0,1},{1,0},{2,3},{3,2},{4,5},{5,4},{6,7},{7,6},{8,9},{9,8},{10,11... | collective-permute-start | bytes 589832 | tf_op jit(solution)/shard_map/ppermute | solution.py:21
  49.9 8.7 %collective-permute-start.19 = (bf16[256,384]{1,0:T(8,128)(2,1)S(1)}, bf16[256,384]{1,0:T(8,128)(2,1)S(1)}, u32[]{:S(2)}, u32[]{:S(2)}) collective-permute-start(bf16[256,384]{1,0:T(8,128)(2,1)S(1)} %get-tuple-element.76.refs_0_), channel_id=1, source_target_pairs={{0,2},{2,0},{1,3},{3,1},{4,6},{6,4},{5,7},{7,5},{8,10},{10,8},{9,1... | collective-permute-start | bytes 589832 | tf_op jit(solution)/shard_map/ppermute | solution.py:21
  51.5 9.7 %collective-permute-start.20 = (bf16[256,384]{1,0:T(8,128)(2,1)S(1)}, bf16[256,384]{1,0:T(8,128)(2,1)S(1)}, u32[]{:S(2)}, u32[]{:S(2)}) collective-permute-start(bf16[256,384]{1,0:T(8,128)(2,1)S(1)} %get-tuple-element.77.refs_1_), channel_id=1, source_target_pairs={{0,2},{2,0},{1,3},{3,1},{4,6},{6,4},{5,7},{7,5},{8,10},{10,8},{9,1... | collective-permute-start | bytes 589832 | tf_op jit(solution)/shard_map/ppermute | solution.py:21
  58.0 3.8 %collective-permute-start.17 = (bf16[256,384]{1,0:T(8,128)(2,1)S(1)}, bf16[256,384]{1,0:T(8,128)(2,1)S(1)}, u32[]{:S(2)}, u32[]{:S(2)}) collective-permute-start(bf16[256,384]{1,0:T(8,128)(2,1)S(1)} %get-tuple-element.76.refs_0_), channel_id=1, source_target_pairs={{0,1},{1,0},{2,3},{3,2},{4,5},{5,4},{6,7},{7,6},{8,9},{9,8},{10,11... | collective-permute-start | bytes 589832 | tf_op jit(solution)/shard_map/ppermute | solution.py:21
  58.0 3.7 %collective-permute-start.18 = (bf16[256,384]{1,0:T(8,128)(2,1)S(1)}, bf16[256,384]{1,0:T(8,128)(2,1)S(1)}, u32[]{:S(2)}, u32[]{:S(2)}) collective-permute-start(bf16[256,384]{1,0:T(8,128)(2,1)S(1)} %get-tuple-element.77.refs_1_), channel_id=1, source_target_pairs={{0,1},{1,0},{2,3},{3,2},{4,5},{5,4},{6,7},{7,6},{8,9},{9,8},{10,11... | collective-permute-start | bytes 589832 | tf_op jit(solution)/shard_map/ppermute | solution.py:21
  61.2 1.4 %collective-permute-start.21 = (bf16[256,384]{1,0:T(8,128)(2,1)S(1)}, bf16[256,384]{1,0:T(8,128)(2,1)S(1)}, u32[]{:S(2)}, u32[]{:S(2)}) collective-permute-start(bf16[256,384]{1,0:T(8,128)(2,1)S(1)} %collective-permute-done.19.refs_4_), channel_id=1, source_target_pairs={{0,1},{1,0},{2,3},{3,2},{4,5},{5,4},{6,7},{7,6},{8,9},{9,8},{10,11... | collective-permute-start | bytes 589832 | tf_op jit(solution)/shard_map/ppermute | solution.py:21
  61.2 1.7 %collective-permute-start.22 = (bf16[256,384]{1,0:T(8,128)(2,1)S(1)}, bf16[256,384]{1,0:T(8,128)(2,1)S(1)}, u32[]{:S(2)}, u32[]{:S(2)}) collective-permute-start(bf16[256,384]{1,0:T(8,128)(2,1)S(1)} %collective-permute-done.20.refs_5_), channel_id=1, source_target_pairs={{0,1},{1,0},{2,3},{3,2},{4,5},{5,4},{6,7},{7,6},{8,9},{9,8},{10,11... | collective-permute-start | bytes 589832 | tf_op jit(solution)/shard_map/ppermute | solution.py:21
  67.0 1.9 %collective-permute-start.23 = (bf16[256,384]{1,0:T(8,128)(2,1)S(1)}, bf16[256,384]{1,0:T(8,128)(2,1)S(1)}, u32[]{:S(2)}, u32[]{:S(2)}) collective-permute-start(bf16[256,384]{1,0:T(8,128)(2,1)S(1)} %get-tuple-element.84), channel_id=1, source_target_pairs={{0,1},{1,0},{2,3},{3,2},{4,5},{5,4},{6,7},{7,6},{8,9},{9,8},{10,11... | collective-permute-start | bytes 589832 | tf_op jit(solution)/shard_map/ppermute | solution.py:21
  67.3 8.0 %collective-permute-start.24 = (bf16[256,384]{1,0:T(8,128)(2,1)S(1)}, bf16[256,384]{1,0:T(8,128)(2,1)S(1)}, u32[]{:S(2)}, u32[]{:S(2)}) collective-permute-start(bf16[256,384]{1,0:T(8,128)(2,1)S(1)} %get-tuple-element.83.p0), channel_id=1, source_target_pairs={{0,2},{2,0},{1,3},{3,1},{4,6},{6,4},{5,7},{7,5},{8,10},{10,8},{9,1... | collective-permute-start | bytes 589832 | tf_op jit(solution)/shard_map/ppermute | solution.py:21
  68.8 9.1 %collective-permute-start.25 = (bf16[256,384]{1,0:T(8,128)(2,1)S(1)}, bf16[256,384]{1,0:T(8,128)(2,1)S(1)}, u32[]{:S(2)}, u32[]{:S(2)}) collective-permute-start(bf16[256,384]{1,0:T(8,128)(2,1)S(1)} %get-tuple-element.84), channel_id=1, source_target_pairs={{0,3},{1,2},{2,1},{3,0},{4,7},{5,6},{6,5},{7,4},{8,11},{9,10},{10,... | collective-permute-start | bytes 589832 | tf_op jit(solution)/shard_map/ppermute | solution.py:25
  68.9 11.2 %collective-permute-start.26 = (bf16[128,384]{1,0:T(8,128)(2,1)S(1)}, bf16[128,384]{1,0:T(8,128)(2,1)S(1)}, u32[]{:S(2)}, u32[]{:S(2)}) collective-permute-start(bf16[128,384]{1,0:T(8,128)(2,1)S(1)} %get-tuple-element.92), channel_id=1, source_target_pairs={{0,4},{4,8},{8,12},{12,0},{1,5},{5,9},{9,13},{13,1},{2,6},{6,10},{... | collective-permute-start | bytes 294920 | tf_op jit(solution)/shard_map/ppermute | solution.py:30
  72.5 9.9 %collective-permute-start.27 = (bf16[128,384]{1,0:T(8,128)(2,1)S(1)}, bf16[128,384]{1,0:T(8,128)(2,1)S(1)}, u32[]{:S(2)}, u32[]{:S(2)}) collective-permute-start(bf16[128,384]{1,0:T(8,128)(2,1)S(1)} %get-tuple-element.94), channel_id=1, source_target_pairs={{0,8},{4,12},{8,0},{12,4},{1,9},{5,13},{9,1},{13,5},{2,10},{6,14},... | collective-permute-start | bytes 294920 | tf_op jit(solution)/shard_map/ppermute | solution.py:30
  75.2 7.2 %collective-permute-start.28 = (bf16[128,384]{1,0:T(8,128)(2,1)S(1)}, bf16[128,384]{1,0:T(8,128)(2,1)S(1)}, u32[]{:S(2)}, u32[]{:S(2)}) collective-permute-start(bf16[128,384]{1,0:T(8,128)(2,1)S(1)} %get-tuple-element.96), channel_id=1, source_target_pairs={{0,12},{4,0},{8,4},{12,8},{1,13},{5,1},{9,5},{13,9},{2,14},{6,2},{... | collective-permute-start | bytes 294920 | tf_op jit(solution)/shard_map/ppermute | solution.py:30
  82.4 19.7 %collective-permute-start.44 = (bf16[256,768]{1,0:T(8,128)(2,1)S(1)}, bf16[256,768]{1,0:T(8,128)(2,1)S(1)}, u32[]{:S(2)}, u32[]{:S(2)}) collective-permute-start(bf16[256,768]{1,0:T(8,128)(2,1)S(1)} %get-tuple-element.114), channel_id=1, source_target_pairs={{0,2},{2,0},{1,3},{3,1},{4,6},{6,4},{5,7},{7,5},{8,10},{10,8},{9,1... | collective-permute-start | bytes 1179656 | tf_op jit(solution)/shard_map/ppermute | solution.py:21
  83.9 9.6 %collective-permute-start.29 = (bf16[256,384]{1,0:T(8,128)(2,1)S(1)}, bf16[256,384]{1,0:T(8,128)(2,1)S(1)}, u32[]{:S(2)}, u32[]{:S(2)}) collective-permute-start(bf16[256,384]{1,0:T(8,128)(2,1)S(1)} %get-tuple-element.98), channel_id=1, source_target_pairs={{0,4},{4,8},{8,12},{12,0},{1,5},{5,9},{9,13},{13,1},{2,6},{6,10},{... | collective-permute-start | bytes 589832 | tf_op jit(solution)/shard_map/ppermute | solution.py:30
  86.5 15.1 %collective-permute-start.30 = (bf16[256,384]{1,0:T(8,128)(2,1)S(1)}, bf16[256,384]{1,0:T(8,128)(2,1)S(1)}, u32[]{:S(2)}, u32[]{:S(2)}) collective-permute-start(bf16[256,384]{1,0:T(8,128)(2,1)S(1)} %get-tuple-element.99), channel_id=1, source_target_pairs={{0,8},{4,12},{8,0},{12,4},{1,9},{5,13},{9,1},{13,5},{2,10},{6,14},... | collective-permute-start | bytes 589832 | tf_op jit(solution)/shard_map/ppermute | solution.py:30
  88.1 13.6 %collective-permute-start.31 = (bf16[256,384]{1,0:T(8,128)(2,1)S(1)}, bf16[256,384]{1,0:T(8,128)(2,1)S(1)}, u32[]{:S(2)}, u32[]{:S(2)}) collective-permute-start(bf16[256,384]{1,0:T(8,128)(2,1)S(1)} %get-tuple-element.100), channel_id=1, source_target_pairs={{0,12},{4,0},{8,4},{12,8},{1,13},{5,1},{9,5},{13,9},{2,14},{6,2},{... | collective-permute-start | bytes 589832 | tf_op jit(solution)/shard_map/ppermute | solution.py:30
  88.9 13.3 %collective-permute-start.32 = (bf16[256,384]{1,0:T(8,128)(2,1)S(1)}, bf16[256,384]{1,0:T(8,128)(2,1)S(1)}, u32[]{:S(2)}, u32[]{:S(2)}) collective-permute-start(bf16[256,384]{1,0:T(8,128)(2,1)S(1)} %get-tuple-element.97.refs_0_), channel_id=1, source_target_pairs={{0,1},{1,0},{2,3},{3,2},{4,5},{5,4},{6,7},{7,6},{8,9},{9,8},{10,11... | collective-permute-start | bytes 589832 | tf_op jit(solution)/shard_map/ppermute | solution.py:21
  93.6 8.7 %collective-permute-start.33 = (bf16[256,384]{1,0:T(8,128)(2,1)S(1)}, bf16[256,384]{1,0:T(8,128)(2,1)S(1)}, u32[]{:S(2)}, u32[]{:S(2)}) collective-permute-start(bf16[256,384]{1,0:T(8,128)(2,1)S(1)} %collective-permute-done.29.refs_1_), channel_id=1, source_target_pairs={{0,1},{1,0},{2,3},{3,2},{4,5},{5,4},{6,7},{7,6},{8,9},{9,8},{10,11... | collective-permute-start | bytes 589832 | tf_op jit(solution)/shard_map/ppermute | solution.py:21
  101.6 1.4 %collective-permute-start.34 = (bf16[256,384]{1,0:T(8,128)(2,1)S(1)}, bf16[256,384]{1,0:T(8,128)(2,1)S(1)}, u32[]{:S(2)}, u32[]{:S(2)}) collective-permute-start(bf16[256,384]{1,0:T(8,128)(2,1)S(1)} %collective-permute-done.30.refs_2_), channel_id=1, source_target_pairs={{0,1},{1,0},{2,3},{3,2},{4,5},{5,4},{6,7},{7,6},{8,9},{9,8},{10,11... | collective-permute-start | bytes 589832 | tf_op jit(solution)/shard_map/ppermute | solution.py:21
  101.6 1.7 %collective-permute-start.35 = (bf16[256,384]{1,0:T(8,128)(2,1)S(1)}, bf16[256,384]{1,0:T(8,128)(2,1)S(1)}, u32[]{:S(2)}, u32[]{:S(2)}) collective-permute-start(bf16[256,384]{1,0:T(8,128)(2,1)S(1)} %collective-permute-done.31.refs_3_), channel_id=1, source_target_pairs={{0,1},{1,0},{2,3},{3,2},{4,5},{5,4},{6,7},{7,6},{8,9},{9,8},{10,11... | collective-permute-start | bytes 589832 | tf_op jit(solution)/shard_map/ppermute | solution.py:21
  102.2 23.2 %collective-permute-start.45 = (bf16[256,768]{1,0:T(8,128)(2,1)S(1)}, bf16[256,768]{1,0:T(8,128)(2,1)S(1)}, u32[]{:S(2)}, u32[]{:S(2)}) collective-permute-start(bf16[256,768]{1,0:T(8,128)(2,1)S(1)} %collective-permute-done.44.refs_11_), channel_id=1, source_target_pairs={{0,1},{1,0},{2,3},{3,2},{4,5},{5,4},{6,7},{7,6},{8,9},{9,8},{10,11... | collective-permute-start | bytes 1179656 | tf_op jit(solution)/shard_map/ppermute | solution.py:21
  107.5 5.9 %collective-permute-start.37 = (bf16[256,128]{1,0:T(8,128)(2,1)S(1)}, bf16[256,128]{1,0:T(8,128)(2,1)S(1)}, u32[]{:S(2)}, u32[]{:S(2)}) collective-permute-start(bf16[256,128]{1,0:T(8,128)(2,1)S(1)} %get-tuple-element.107), channel_id=1, source_target_pairs={{0,8},{4,12},{8,0},{12,4},{1,9},{5,13},{9,1},{13,5},{2,10},{6,14},... | collective-permute-start | bytes 196616 | tf_op jit(solution)/shard_map/ppermute | solution.py:30
  110.9 14.5 %collective-permute-start.43 = (bf16[256,384]{1,0:T(8,128)(2,1)S(1)}, bf16[256,384]{1,0:T(8,128)(2,1)S(1)}, u32[]{:S(2)}, u32[]{:S(2)}) collective-permute-start(bf16[256,384]{1,0:T(8,128)(2,1)S(1)} %get-tuple-element.111), channel_id=1, source_target_pairs={{0,1},{1,0},{2,3},{3,2},{4,5},{5,4},{6,7},{7,6},{8,9},{9,8},{10,11... | collective-permute-start | bytes 589832 | tf_op jit(solution)/shard_map/ppermute | solution.py:21
  110.9 7.5 %collective-permute-start.38 = (bf16[256,128]{1,0:T(8,128)(2,1)S(1)}, bf16[256,128]{1,0:T(8,128)(2,1)S(1)}, u32[]{:S(2)}, u32[]{:S(2)}) collective-permute-start(bf16[256,128]{1,0:T(8,128)(2,1)S(1)} %get-tuple-element.105.refs_0_), channel_id=1, source_target_pairs={{0,2},{2,0},{1,3},{3,1},{4,6},{6,4},{5,7},{7,5},{8,10},{10,8},{9,1... | collective-permute-start | bytes 196616 | tf_op jit(solution)/shard_map/ppermute | solution.py:21
  111.4 6.9 %collective-permute-start.36 = (bf16[256,128]{1,0:T(8,128)(2,1)S(1)}, bf16[256,128]{1,0:T(8,128)(2,1)S(1)}, u32[]{:S(2)}, u32[]{:S(2)}) collective-permute-start(bf16[256,128]{1,0:T(8,128)(2,1)S(1)} %get-tuple-element.106), channel_id=1, source_target_pairs={{0,4},{4,8},{8,12},{12,0},{1,5},{5,9},{9,13},{13,1},{2,6},{6,10},{... | collective-permute-start | bytes 196616 | tf_op jit(solution)/shard_map/ppermute | solution.py:30
  113.3 6.9 %collective-permute-start.39 = (bf16[256,128]{1,0:T(8,128)(2,1)S(1)}, bf16[256,128]{1,0:T(8,128)(2,1)S(1)}, u32[]{:S(2)}, u32[]{:S(2)}) collective-permute-start(bf16[256,128]{1,0:T(8,128)(2,1)S(1)} %get-tuple-element.109), channel_id=1, source_target_pairs={{0,12},{4,0},{8,4},{12,8},{1,13},{5,1},{9,5},{13,9},{2,14},{6,2},{... | collective-permute-start | bytes 196616 | tf_op jit(solution)/shard_map/ppermute | solution.py:30
  118.4 5.0 %collective-permute-start.40 = (bf16[256,128]{1,0:T(8,128)(2,1)S(1)}, bf16[256,128]{1,0:T(8,128)(2,1)S(1)}, u32[]{:S(2)}, u32[]{:S(2)}) collective-permute-start(bf16[256,128]{1,0:T(8,128)(2,1)S(1)} %collective-permute-done.36.refs_1_), channel_id=1, source_target_pairs={{0,2},{2,0},{1,3},{3,1},{4,6},{6,4},{5,7},{7,5},{8,10},{10,8},{9,1... | collective-permute-start | bytes 196616 | tf_op jit(solution)/shard_map/ppermute | solution.py:21
  120.3 4.4 %collective-permute-start.42 = (bf16[256,128]{1,0:T(8,128)(2,1)S(1)}, bf16[256,128]{1,0:T(8,128)(2,1)S(1)}, u32[]{:S(2)}, u32[]{:S(2)}) collective-permute-start(bf16[256,128]{1,0:T(8,128)(2,1)S(1)} %collective-permute-done.39.refs_3_), channel_id=1, source_target_pairs={{0,2},{2,0},{1,3},{3,1},{4,6},{6,4},{5,7},{7,5},{8,10},{10,8},{9,1... | collective-permute-start | bytes 196616 | tf_op jit(solution)/shard_map/ppermute | solution.py:21
  120.8 4.6 %collective-permute-start.41 = (bf16[256,128]{1,0:T(8,128)(2,1)S(1)}, bf16[256,128]{1,0:T(8,128)(2,1)S(1)}, u32[]{:S(2)}, u32[]{:S(2)}) collective-permute-start(bf16[256,128]{1,0:T(8,128)(2,1)S(1)} %collective-permute-done.37.refs_2_), channel_id=1, source_target_pairs={{0,2},{2,0},{1,3},{3,1},{4,6},{6,4},{5,7},{7,5},{8,10},{10,8},{9,1... | collective-permute-start | bytes 196616 | tf_op jit(solution)/shard_map/ppermute | solution.py:21

commit v5 on v4

--- a/solution.py
+++ b/solution.py
@@ -455,9 +455,7 @@
     )
     got = swap(give, "sub")
     heads = [attended[0]] + [rotate(attended[s], s) for s in range(1, n)]
-    others = [swap(heads[0], "mp")]
-    heads[2] = after(heads[2], others[0])
-    others += [swap(x, "mp") for x in heads[1:]]
+    others = [swap(x, "mp") for x in heads]
     (out,) = call(
         finish_kernel,
         scalars,

time: 128 us -> 127 us (level)
  starting transfers between devices: 50.4 us -> 46.9 us
  waiting for transfers between devices: 40.9 us -> 44.2 us
    ppermute x12, starting transfers between devices: 30.6 us -> 27.2 us  [rotate(): return lax.ppermute(x, 'seq', [(i, (i + by) % n) for i in range(n)])]
    ppermute x12, waiting for transfers between devices: 20.3 us -> 22.4 us  [rotate(): return lax.ppermute(x, 'seq', [(i, (i + by) % n) for i in range(n)])]
  transfers between devices with their start and end apart: 46 -> 46, of which waited for: 20 -> 21; matrix products, arithmetic and copies ran while one was open for 0% -> 0% of each run, Pallas kernels for 18% -> 18%
where the time goes in v5:
time: 127 us
  starting transfers between devices  46.9 us (37%)
  waiting for transfers between devices  44.2 us (35%)
  Pallas kernels  35.7 us (28%)
    pallas_call x13, Pallas kernels, call(): pl.pallas_call(kernel, out_shape=outs, grid_spec=pltpu.PrefetchScalarGrid...  35.7 us
    ppermute x12, starting transfers between devices, rotate(): return lax.ppermute(x, 'seq', [(i, (i + by) % n) for i in range(n)])  27.2 us
    ppermute x12, waiting for transfers between devices, rotate(): return lax.ppermute(x, 'seq', [(i, (i + by) % n) for i in range(n)])  22.4 us
    ppermute x31, waiting for transfers between devices, swap(): return lax.ppermute(x, axis, [(0, 1), (1, 0)])  19.1 us
    ppermute x31, starting transfers between devices, swap(): return lax.ppermute(x, axis, [(0, 1), (1, 0)])  17 us
    ppermute x1, waiting for transfers between devices, swap_both(): return lax.ppermute(x, ('mp', 'sub'), [(i, 3 - i) for i in range(4)])  2.66 us
  transfers between devices with their start and end apart: 46, of which 21 were waited for; matrix products, arithmetic and copies ran while one was open for 0% of the time, Pallas kernels for 18%

profile of v5, /device:TPU:0, one launch (start us, length us, event | category | flops | bytes accessed | tf_op | source)
XLA Modules:
  0.0 127.1 jit_solution(12169513616697471328)
XLA Ops:
  0.1 1.6 %cut_kernel.1 = (bf16[256,384]{1,0:T(8,128)(2,1)S(1)}, bf16[256,384]{1,0:T(8,128)(2,1)S(1)}) custom-call(s32[7]{0:T(128)S(1)} %stack.31.scalars, bf16[512,384]{1,0:T(8,128)(2,1)} %x.1), custom_call_target="tpu_custom_call" | custom-call | bytes 786432 | tf_op jit(solution)/shard_map/cut_kernel/pallas_call | solution.py:295
  1.7 3.0 %collective-permute-start.4 = (bf16[256,384]{1,0:T(8,128)(2,1)S(1)}, bf16[256,384]{1,0:T(8,128)(2,1)S(1)}, u32[]{:S(2)}, u32[]{:S(2)}) collective-permute-start(bf16[256,384]{1,0:T(8,128)(2,1)S(1)} %get-tuple-element.62.p0), channel_id=1, source_target_pairs={{0,2},{2,0},{1,3},{3,1},{4,6},{6,4},{5,7},{7,5},{8,10},{10,8},{9,1... | collective-permute-start | bytes 589832 | tf_op jit(solution)/shard_map/ppermute | solution.py:21
  4.8 2.6 %load_taps_kernel.3 = (bf16[3,1536,384]{2,1,0:T(8,128)(2,1)S(1)}, f32[3,1536]{1,0:T(4,128)S(1)}) custom-call(s32[7]{0:T(128)S(1)} %stack.31.scalars, bf16[3,3,1536,384]{3,2,1,0:T(8,128)(2,1)} %w.5, f32[3,1536]{1,0:T(4,128)} %gains.5), custom_call_target="tpu_custom_call" | custom-call | bytes 14192640 | tf_op jit(solution)/shard_map/load_taps_kernel/pallas_call | solution.py:295
  7.5 3.0 %collective-permute-done.4.p2 = bf16[256,384]{1,0:T(8,128)(2,1)S(1)} collective-permute-done((bf16[256,384]{1,0:T(8,128)(2,1)S(1)}, bf16[256,384]{1,0:T(8,128)(2,1)S(1)}, u32[]{:S(2)}, u32[]{:S(2)}) %collective-permute-start.4) | collective-permute-done | bytes 196640 | tf_op jit(solution)/shard_map/ppermute | solution.py:21
  11.0 2.9 %collective-permute-done.1.p2 = bf16[256,384]{1,0:T(8,128)(2,1)S(1)} collective-permute-done((bf16[256,384]{1,0:T(8,128)(2,1)S(1)}, bf16[256,384]{1,0:T(8,128)(2,1)S(1)}, u32[]{:S(2)}, u32[]{:S(2)}) %collective-permute-start.1) | collective-permute-done | bytes 196640 | tf_op jit(solution)/shard_map/ppermute | solution.py:21
  13.9 2.8 %first_edge_kernel.1 = (f32[4,128,384]{2,1,0:T(8,128)S(1)}, bf16[128,384]{1,0:T(8,128)(2,1)S(1)}, bf16[128,384]{1,0:T(8,128)(2,1)S(1)}) custom-call(s32[7]{0:T(128)S(1)} %stack.31.scalars, bf16[256,384]{1,0:T(8,128)(2,1)S(1)} %get-tuple-element.62.p0, bf16[256,384]{1,0:T(8,128)(2,1)S(1)} %collective-permute-done.3.p1, ...), custom_call_target="tpu_custom_call" | custom-call | flops 905969664 | bytes 5326848 | tf_op jit(solution)/shard_map/first_edge_kernel/pallas_call | solution.py:295
  16.6 1.9 %collective-permute-start.6 = (bf16[128,384]{1,0:T(8,128)(2,1)S(1)}, bf16[128,384]{1,0:T(8,128)(2,1)S(1)}, u32[]{:S(2)}, u32[]{:S(2)}) collective-permute-start(bf16[128,384]{1,0:T(8,128)(2,1)S(1)} %get-tuple-element.65), channel_id=1, source_target_pairs={{0,4},{4,0},{8,12},{12,8},{1,5},{5,1},{9,13},{13,9},{2,6},{6,2},{1... | collective-permute-start | bytes 294920 | tf_op jit(solution)/shard_map/ppermute | solution.py:373
  19.2 2.8 %first_middle_kernel.1.partial = f32[4,128,384]{2,1,0:T(8,128)S(1)} custom-call(s32[7]{0:T(128)S(1)} %stack.31.scalars, bf16[256,384]{1,0:T(8,128)(2,1)S(1)} %get-tuple-element.59.p0, bf16[256,384]{1,0:T(8,128)(2,1)S(1)} %collective-permute-done.p1, bf16[256,384]{1,0:T(8,128)(2,1)S(1)} %collective-permute-done.1.p2, ...), custom_call_target="tpu_custom_call" | custom-call | flops 905969664 | bytes 5916672 | tf_op jit(solution)/shard_map/first_middle_kernel/pallas_call | solution.py:295
  22.0 0.7 deal_kernel.1
  22.7 4.8 %collective-permute-start.8 = (bf16[128,384]{1,0:T(8,128)(2,1)S(1)}, bf16[128,384]{1,0:T(8,128)(2,1)S(1)}, u32[]{:S(2)}, u32[]{:S(2)}) collective-permute-start(bf16[128,384]{1,0:T(8,128)(2,1)S(1)} %get-tuple-element.68), channel_id=1, source_target_pairs={{0,4},{4,8},{8,12},{12,0},{1,5},{5,9},{9,13},{13,1},{2,6},{6,10},{... | collective-permute-start | bytes 294920 | tf_op jit(solution)/shard_map/ppermute | solution.py:30
  27.5 1.2 collective-permute-start.9
  28.7 2.8 %collective-permute-start.10 = (bf16[128,384]{1,0:T(8,128)(2,1)S(1)}, bf16[128,384]{1,0:T(8,128)(2,1)S(1)}, u32[]{:S(2)}, u32[]{:S(2)}) collective-permute-start(bf16[128,384]{1,0:T(8,128)(2,1)S(1)} %get-tuple-element.70), channel_id=1, source_target_pairs={{0,12},{4,0},{8,4},{12,8},{1,13},{5,1},{9,5},{13,9},{2,14},{6,2},{... | collective-permute-start | bytes 294920 | tf_op jit(solution)/shard_map/ppermute | solution.py:30
  31.6 4.1 %collective-permute-done.9 = bf16[128,384]{1,0:T(8,128)(2,1)S(1)} collective-permute-done((bf16[128,384]{1,0:T(8,128)(2,1)S(1)}, bf16[128,384]{1,0:T(8,128)(2,1)S(1)}, u32[]{:S(2)}, u32[]{:S(2)}) %collective-permute-start.9) | collective-permute-done | bytes 98336 | tf_op jit(solution)/shard_map/ppermute | solution.py:30
  35.7 1.6 %collective-permute-start.14 = (bf16[256,384]{1,0:T(8,128)(2,1)S(1)}, bf16[256,384]{1,0:T(8,128)(2,1)S(1)}, u32[]{:S(2)}, u32[]{:S(2)}) collective-permute-start(bf16[256,384]{1,0:T(8,128)(2,1)S(1)} %constant_dynamic-update-slice_fusion.2.refs_1_), channel_id=1, source_target_pairs={{0,2},{2,0},{1,3},{3,1},{4,6},{6,4},{5,7},{7,5},{8,10},{10,8},{9,1... | collective-permute-start | bytes 589832 | tf_op jit(solution)/shard_map/ppermute | solution.py:21
  37.9 2.6 %load_taps_kernel.4 = (bf16[3,1536,384]{2,1,0:T(8,128)(2,1)S(1)}, f32[3,1536]{1,0:T(4,128)S(1)}) custom-call(s32[7]{0:T(128)S(1)} %stack.31.scalars, bf16[3,3,1536,384]{3,2,1,0:T(8,128)(2,1)} %w.5, f32[3,1536]{1,0:T(4,128)} %gains.5), custom_call_target="tpu_custom_call" | custom-call | bytes 14192640 | tf_op jit(solution)/shard_map/load_taps_kernel/pallas_call | solution.py:295
  41.1 0.7 collective-permute-done.14.refs_5_
  41.7 2.1 %collective-permute-done.13.refs_4_ = bf16[256,384]{1,0:T(8,128)(2,1)S(1)} collective-permute-done((bf16[256,384]{1,0:T(8,128)(2,1)S(1)}, bf16[256,384]{1,0:T(8,128)(2,1)S(1)}, u32[]{:S(2)}, u32[]{:S(2)}) %collective-permute-start.13) | collective-permute-done | bytes 196640 | tf_op jit(solution)/shard_map/ppermute | solution.py:21
  44.4 0.9 collective-permute-done.15.refs_6_
  45.6 4.3 %second_kernel.1 = (bf16[256,384]{1,0:T(8,128)(2,1)S(1)}, bf16[256,384]{1,0:T(8,128)(2,1)S(1)}) custom-call(s32[7]{0:T(128)S(1)} %stack.31.scalars, bf16[256,384]{1,0:T(8,128)(2,1)S(1)} %constant_dynamic-update-slice_fusion.refs_0_, bf16[256,384]{1,0:T(8,128)(2,1)S(1)} %constant_dynamic-update-slice_fusion.2.refs_1_, ...), custom_call_target="tpu_custom_call" | custom-call | flops 1811939328 | bytes 5523456 | tf_op jit(solution)/shard_map/second_kernel/pallas_call | solution.py:295
  49.9 1.6 %collective-permute-start.19 = (bf16[256,384]{1,0:T(8,128)(2,1)S(1)}, bf16[256,384]{1,0:T(8,128)(2,1)S(1)}, u32[]{:S(2)}, u32[]{:S(2)}) collective-permute-start(bf16[256,384]{1,0:T(8,128)(2,1)S(1)} %get-tuple-element.75.refs_0_), channel_id=1, source_target_pairs={{0,2},{2,0},{1,3},{3,1},{4,6},{6,4},{5,7},{7,5},{8,10},{10,8},{9,1... | collective-permute-start | bytes 589832 | tf_op jit(solution)/shard_map/ppermute | solution.py:21
  52.0 2.6 %load_taps_kernel.5 = (bf16[3,1536,384]{2,1,0:T(8,128)(2,1)S(1)}, f32[3,1536]{1,0:T(4,128)S(1)}) custom-call(s32[7]{0:T(128)S(1)} %stack.31.scalars, bf16[3,3,1536,384]{3,2,1,0:T(8,128)(2,1)} %w.5, f32[3,1536]{1,0:T(4,128)} %gains.5), custom_call_target="tpu_custom_call" | custom-call | bytes 14192640 | tf_op jit(solution)/shard_map/load_taps_kernel/pallas_call | solution.py:295
  54.6 3.3 %load_projections_kernel.1 = (bf16[3,1536,512]{2,1,0:T(8,128)(2,1)S(1)}, bf16[512,768]{1,0:T(8,128)(2,1)S(1)}, bf16[256,768]{1,0:T(8,128)(2,1)S(1)}) custom-call(s32[7]{0:T(128)S(1)} %stack.31.scalars, bf16[1536,512]{1,0:T(8,128)(2,1)} %w_q.1, bf16[1536,512]{1,0:T(8,128)(2,1)} %w_k.1, bf16[1536,512]{1,0:T(8,128)(2,1)} %w_v.1, bf16[512,1536]{1,0:T(8,128)(2,1)} %w_o.1), custom_call_target="tpu_custom_call" | custom-call | bytes 12189696 | tf_op jit(solution)/shard_map/load_projections_kernel/pallas_call | solution.py:295
  58.5 2.7 %collective-permute-done.20.refs_5_ = bf16[256,384]{1,0:T(8,128)(2,1)S(1)} collective-permute-done((bf16[256,384]{1,0:T(8,128)(2,1)S(1)}, bf16[256,384]{1,0:T(8,128)(2,1)S(1)}, u32[]{:S(2)}, u32[]{:S(2)}) %collective-permute-start.20) | collective-permute-done | bytes 196640 | tf_op jit(solution)/shard_map/ppermute | solution.py:21
  61.7 0.9 collective-permute-done.21.refs_6_
  62.9 4.0 %third_kernel.1 = (bf16[256,384]{1,0:T(8,128)(2,1)S(1)}, bf16[256,384]{1,0:T(8,128)(2,1)S(1)}, bf16[128,384]{1,0:T(8,128)(2,1)S(1)}, bf16[128,384]{1,0:T(8,128)(...) custom-call(s32[7]{0:T(128)S(1)} %stack.31.scalars, ...), custom_call_target="tpu_custom_call" | custom-call | flops 1811939328 | bytes 5916672 | tf_op jit(solution)/shard_map/third_kernel/pallas_call | solution.py:295
  67.3 1.5 %collective-permute-start.24 = (bf16[256,384]{1,0:T(8,128)(2,1)S(1)}, bf16[256,384]{1,0:T(8,128)(2,1)S(1)}, u32[]{:S(2)}, u32[]{:S(2)}) collective-permute-start(bf16[256,384]{1,0:T(8,128)(2,1)S(1)} %get-tuple-element.82.p0), channel_id=1, source_target_pairs={{0,2},{2,0},{1,3},{3,1},{4,6},{6,4},{5,7},{7,5},{8,10},{10,8},{9,1... | collective-permute-start | bytes 589832 | tf_op jit(solution)/shard_map/ppermute | solution.py:21
  68.9 3.6 %collective-permute-start.26 = (bf16[128,384]{1,0:T(8,128)(2,1)S(1)}, bf16[128,384]{1,0:T(8,128)(2,1)S(1)}, u32[]{:S(2)}, u32[]{:S(2)}) collective-permute-start(bf16[128,384]{1,0:T(8,128)(2,1)S(1)} %get-tuple-element.91), channel_id=1, source_target_pairs={{0,4},{4,8},{8,12},{12,0},{1,5},{5,9},{9,13},{13,1},{2,6},{6,10},{... | collective-permute-start | bytes 294920 | tf_op jit(solution)/shard_map/ppermute | solution.py:30
  72.5 2.7 %collective-permute-start.27 = (bf16[128,384]{1,0:T(8,128)(2,1)S(1)}, bf16[128,384]{1,0:T(8,128)(2,1)S(1)}, u32[]{:S(2)}, u32[]{:S(2)}) collective-permute-start(bf16[128,384]{1,0:T(8,128)(2,1)S(1)} %get-tuple-element.93), channel_id=1, source_target_pairs={{0,8},{4,12},{8,0},{12,4},{1,9},{5,13},{9,1},{13,5},{2,10},{6,14},... | collective-permute-start | bytes 294920 | tf_op jit(solution)/shard_map/ppermute | solution.py:30
  75.3 2.7 %collective-permute-done.25.p3 = bf16[256,384]{1,0:T(8,128)(2,1)S(1)} collective-permute-done((bf16[256,384]{1,0:T(8,128)(2,1)S(1)}, bf16[256,384]{1,0:T(8,128)(2,1)S(1)}, u32[]{:S(2)}, u32[]{:S(2)}) %collective-permute-start.25) | collective-permute-done | bytes 196640 | tf_op jit(solution)/shard_map/ppermute | solution.py:25
  77.9 2.2 %project_kernel.1 = (bf16[256,384]{1,0:T(8,128)(2,1)S(1)}, bf16[256,384]{1,0:T(8,128)(2,1)S(1)}, bf16[256,384]{1,0:T(8,128)(2,1)S(1)}, bf16[256,384]{1,0:T(8,128)(2,1)S(1)}) custom-call(s32[7]{0:T(128)S(1)} %stack.31.scalars, bf16[256,384]{1,0:T(8,128)(2,1)S(1)} %get-tuple-element.82.p0, bf16[256,384]{1,0:T(8,128)(2,1)S(1)} %collective-permute-done.23.p1, ...), custom_call_target="tpu_custom_call" | custom-call | flops 1207959552 | bytes 6291456 | tf_op jit(solution)/shard_map/project_kernel/pallas_call | solution.py:295
  80.1 2.3 %collective-permute-done.27.refs_10_ = bf16[128,384]{1,0:T(8,128)(2,1)S(1)} collective-permute-done((bf16[128,384]{1,0:T(8,128)(2,1)S(1)}, bf16[128,384]{1,0:T(8,128)(2,1)S(1)}, u32[]{:S(2)}, u32[]{:S(2)}) %collective-permute-start.27) | collective-permute-done | bytes 98336 | tf_op jit(solution)/shard_map/ppermute | solution.py:30
  82.4 1.5 %collective-permute-start.44 = (bf16[256,768]{1,0:T(8,128)(2,1)S(1)}, bf16[256,768]{1,0:T(8,128)(2,1)S(1)}, u32[]{:S(2)}, u32[]{:S(2)}) collective-permute-start(bf16[256,768]{1,0:T(8,128)(2,1)S(1)} %get-tuple-element.112), channel_id=1, source_target_pairs={{0,2},{2,0},{1,3},{3,1},{4,6},{6,4},{5,7},{7,5},{8,10},{10,8},{9,1... | collective-permute-start | bytes 1179656 | tf_op jit(solution)/shard_map/ppermute | solution.py:21
  83.9 2.6 %collective-permute-start.29 = (bf16[256,384]{1,0:T(8,128)(2,1)S(1)}, bf16[256,384]{1,0:T(8,128)(2,1)S(1)}, u32[]{:S(2)}, u32[]{:S(2)}) collective-permute-start(bf16[256,384]{1,0:T(8,128)(2,1)S(1)} %get-tuple-element.97), channel_id=1, source_target_pairs={{0,4},{4,8},{8,12},{12,0},{1,5},{5,9},{9,13},{13,1},{2,6},{6,10},{... | collective-permute-start | bytes 589832 | tf_op jit(solution)/shard_map/ppermute | solution.py:30
  86.5 1.6 %collective-permute-start.30 = (bf16[256,384]{1,0:T(8,128)(2,1)S(1)}, bf16[256,384]{1,0:T(8,128)(2,1)S(1)}, u32[]{:S(2)}, u32[]{:S(2)}) collective-permute-start(bf16[256,384]{1,0:T(8,128)(2,1)S(1)} %get-tuple-element.98), channel_id=1, source_target_pairs={{0,8},{4,12},{8,0},{12,4},{1,9},{5,13},{9,1},{13,5},{2,10},{6,14},... | collective-permute-start | bytes 589832 | tf_op jit(solution)/shard_map/ppermute | solution.py:30
  88.1 0.8 collective-permute-start.31
  88.9 4.7 %collective-permute-done.29.refs_1_ = bf16[256,384]{1,0:T(8,128)(2,1)S(1)} collective-permute-done((bf16[256,384]{1,0:T(8,128)(2,1)S(1)}, bf16[256,384]{1,0:T(8,128)(2,1)S(1)}, u32[]{:S(2)}, u32[]{:S(2)}) %collective-permute-start.29) | collective-permute-done | bytes 196640 | tf_op jit(solution)/shard_map/ppermute | solution.py:30
  93.6 8.1 %collective-permute-done.30.refs_2_ = bf16[256,384]{1,0:T(8,128)(2,1)S(1)} collective-permute-done((bf16[256,384]{1,0:T(8,128)(2,1)S(1)}, bf16[256,384]{1,0:T(8,128)(2,1)S(1)}, u32[]{:S(2)}, u32[]{:S(2)}) %collective-permute-start.30) | collective-permute-done | bytes 196640 | tf_op jit(solution)/shard_map/ppermute | solution.py:30
  102.2 0.8 collective-permute-done.34.refs_6_
  103.4 4.1 %attend_kernel.1 = (bf16[256,128]{1,0:T(8,128)(2,1)S(1)}, bf16[256,128]{1,0:T(8,128)(2,1)S(1)}, bf16[256,128]{1,0:T(8,128)(2,1)S(1)}, bf16[256,128]{1,0:T(8,128)...) custom-call(s32[7]{0:T(128)S(1)} %stack.31.scalars, ...), custom_call_target="tpu_custom_call" | custom-call | flops 1073741824 | bytes 2621440 | tf_op jit(solution)/shard_map/attend_kernel/pallas_call | solution.py:295
  107.5 4.4 %collective-permute-start.36 = (bf16[256,128]{1,0:T(8,128)(2,1)S(1)}, bf16[256,128]{1,0:T(8,128)(2,1)S(1)}, u32[]{:S(2)}, u32[]{:S(2)}) collective-permute-start(bf16[256,128]{1,0:T(8,128)(2,1)S(1)} %get-tuple-element.105), channel_id=1, source_target_pairs={{0,4},{4,8},{8,12},{12,0},{1,5},{5,9},{9,13},{13,1},{2,6},{6,10},{... | collective-permute-start | bytes 196616 | tf_op jit(solution)/shard_map/ppermute | solution.py:30
  111.9 0.9 collective-permute-start.37
  112.8 1.7 %collective-permute-start.38 = (bf16[256,128]{1,0:T(8,128)(2,1)S(1)}, bf16[256,128]{1,0:T(8,128)(2,1)S(1)}, u32[]{:S(2)}, u32[]{:S(2)}) collective-permute-start(bf16[256,128]{1,0:T(8,128)(2,1)S(1)} %get-tuple-element.107), channel_id=1, source_target_pairs={{0,12},{4,0},{8,4},{12,8},{1,13},{5,1},{9,5},{13,9},{2,14},{6,2},{... | collective-permute-start | bytes 196616 | tf_op jit(solution)/shard_map/ppermute | solution.py:30
  115.3 3.1 %collective-permute-done.37.refs_2_ = bf16[256,128]{1,0:T(8,128)(2,1)S(1)} collective-permute-done((bf16[256,128]{1,0:T(8,128)(2,1)S(1)}, bf16[256,128]{1,0:T(8,128)(2,1)S(1)}, u32[]{:S(2)}, u32[]{:S(2)}) %collective-permute-start.37) | collective-permute-done | bytes 65568 | tf_op jit(solution)/shard_map/ppermute | solution.py:30
  118.9 1.5 %collective-permute-start.41 = (bf16[256,128]{1,0:T(8,128)(2,1)S(1)}, bf16[256,128]{1,0:T(8,128)(2,1)S(1)}, u32[]{:S(2)}, u32[]{:S(2)}) collective-permute-start(bf16[256,128]{1,0:T(8,128)(2,1)S(1)} %collective-permute-done.37.refs_2_), channel_id=1, source_target_pairs={{0,2},{2,0},{1,3},{3,1},{4,6},{6,4},{5,7},{7,5},{8,10},{10,8},{9,1... | collective-permute-start | bytes 196616 | tf_op jit(solution)/shard_map/ppermute | solution.py:21
  120.9 2.4 %collective-permute-done.40.refs_5_ = bf16[256,128]{1,0:T(8,128)(2,1)S(1)} collective-permute-done((bf16[256,128]{1,0:T(8,128)(2,1)S(1)}, bf16[256,128]{1,0:T(8,128)(2,1)S(1)}, u32[]{:S(2)}, u32[]{:S(2)}) %collective-permute-start.40) | collective-permute-done | bytes 65568 | tf_op jit(solution)/shard_map/ppermute | solution.py:21
  123.3 1.2 collective-permute-done.41.refs_6_
  124.5 0.7 collective-permute-done.42.refs_7_
  125.2 2.0 %finish_kernel.1 = bf16[256,768]{1,0:T(8,128)(2,1)} custom-call(s32[7]{0:T(128)S(1)} %stack.31.scalars, bf16[256,128]{1,0:T(8,128)(2,1)S(1)} %get-tuple-element.104.refs_0_, bf16[256,128]{1,0:T(8,128)(2,1)S(1)} %collective-permute-done.36.refs_1_, bf16[256,128]{1,0:T(8,128)(2,1)S(1)} %collective-permute-done.37.refs_2_, ...), custom_call_target="tpu_custom_call" | custom-call | flops 402653184 | bytes 2883584 | tf_op jit(solution)/shard_map/finish_kernel/pallas_call | solution.py:295
  (62 shorter events, 8.4 us)
Async XLA Ops:
  1.7 8.7 %collective-permute-start.4 = (bf16[256,384]{1,0:T(8,128)(2,1)S(1)}, bf16[256,384]{1,0:T(8,128)(2,1)S(1)}, u32[]{:S(2)}, u32[]{:S(2)}) collective-permute-start(bf16[256,384]{1,0:T(8,128)(2,1)S(1)} %get-tuple-element.62.p0), channel_id=1, source_target_pairs={{0,2},{2,0},{1,3},{3,1},{4,6},{6,4},{5,7},{7,5},{8,10},{10,8},{9,1... | collective-permute-start | bytes 589832 | tf_op jit(solution)/shard_map/ppermute | solution.py:21
  4.7 9.1 %collective-permute-start.1 = (bf16[256,384]{1,0:T(8,128)(2,1)S(1)}, bf16[256,384]{1,0:T(8,128)(2,1)S(1)}, u32[]{:S(2)}, u32[]{:S(2)}) collective-permute-start(bf16[256,384]{1,0:T(8,128)(2,1)S(1)} %get-tuple-element.59.p0), channel_id=1, source_target_pairs={{0,2},{2,0},{1,3},{3,1},{4,6},{6,4},{5,7},{7,5},{8,10},{10,8},{9,1... | collective-permute-start | bytes 589832 | tf_op jit(solution)/shard_map/ppermute | solution.py:21
  4.8 9.0 %collective-permute-start.3 = (bf16[256,384]{1,0:T(8,128)(2,1)S(1)}, bf16[256,384]{1,0:T(8,128)(2,1)S(1)}, u32[]{:S(2)}, u32[]{:S(2)}) collective-permute-start(bf16[256,384]{1,0:T(8,128)(2,1)S(1)} %get-tuple-element.62.p0), channel_id=1, source_target_pairs={{0,1},{1,0},{2,3},{3,2},{4,5},{5,4},{6,7},{7,6},{8,9},{9,8},{10,11... | collective-permute-start | bytes 589832 | tf_op jit(solution)/shard_map/ppermute | solution.py:21
  10.5 3.4 %collective-permute-start.5 = (bf16[256,384]{1,0:T(8,128)(2,1)S(1)}, bf16[256,384]{1,0:T(8,128)(2,1)S(1)}, u32[]{:S(2)}, u32[]{:S(2)}) collective-permute-start(bf16[256,384]{1,0:T(8,128)(2,1)S(1)} %collective-permute-done.4.p2), channel_id=1, source_target_pairs={{0,1},{1,0},{2,3},{3,2},{4,5},{5,4},{6,7},{7,6},{8,9},{9,8},{10,11... | collective-permute-start | bytes 589832 | tf_op jit(solution)/shard_map/ppermute | solution.py:21
  10.5 8.7 %collective-permute-start = (bf16[256,384]{1,0:T(8,128)(2,1)S(1)}, bf16[256,384]{1,0:T(8,128)(2,1)S(1)}, u32[]{:S(2)}, u32[]{:S(2)}) collective-permute-start(bf16[256,384]{1,0:T(8,128)(2,1)S(1)} %get-tuple-element.59.p0), channel_id=1, source_target_pairs={{0,1},{1,0},{2,3},{3,2},{4,5},{5,4},{6,7},{7,6},{8,9},{9,8},{10,11... | collective-permute-start | bytes 589832 | tf_op jit(solution)/shard_map/ppermute | solution.py:21
  13.9 5.3 %collective-permute-start.2 = (bf16[256,384]{1,0:T(8,128)(2,1)S(1)}, bf16[256,384]{1,0:T(8,128)(2,1)S(1)}, u32[]{:S(2)}, u32[]{:S(2)}) collective-permute-start(bf16[256,384]{1,0:T(8,128)(2,1)S(1)} %collective-permute-done.1.p2), channel_id=1, source_target_pairs={{0,1},{1,0},{2,3},{3,2},{4,5},{5,4},{6,7},{7,6},{8,9},{9,8},{10,11... | collective-permute-start | bytes 589832 | tf_op jit(solution)/shard_map/ppermute | solution.py:21
  16.6 5.4 %collective-permute-start.6 = (bf16[128,384]{1,0:T(8,128)(2,1)S(1)}, bf16[128,384]{1,0:T(8,128)(2,1)S(1)}, u32[]{:S(2)}, u32[]{:S(2)}) collective-permute-start(bf16[128,384]{1,0:T(8,128)(2,1)S(1)} %get-tuple-element.65), channel_id=1, source_target_pairs={{0,4},{4,0},{8,12},{12,8},{1,5},{5,1},{9,13},{13,9},{2,6},{6,2},{1... | collective-permute-start | bytes 294920 | tf_op jit(solution)/shard_map/ppermute | solution.py:373
  18.5 3.5 %collective-permute-start.7 = (bf16[128,384]{1,0:T(8,128)(2,1)S(1)}, bf16[128,384]{1,0:T(8,128)(2,1)S(1)}, u32[]{:S(2)}, u32[]{:S(2)}) collective-permute-start(bf16[128,384]{1,0:T(8,128)(2,1)S(1)} %get-tuple-element.66), channel_id=1, source_target_pairs={{4,8},{8,4},{5,9},{9,5},{6,10},{10,6},{7,11},{11,7},{20,24},{24,20... | collective-permute-start | bytes 294920 | tf_op jit(solution)/shard_map/ppermute | solution.py:374
  22.7 14.6 %collective-permute-start.8 = (bf16[128,384]{1,0:T(8,128)(2,1)S(1)}, bf16[128,384]{1,0:T(8,128)(2,1)S(1)}, u32[]{:S(2)}, u32[]{:S(2)}) collective-permute-start(bf16[128,384]{1,0:T(8,128)(2,1)S(1)} %get-tuple-element.68), channel_id=1, source_target_pairs={{0,4},{4,8},{8,12},{12,0},{1,5},{5,9},{9,13},{13,1},{2,6},{6,10},{... | collective-permute-start | bytes 294920 | tf_op jit(solution)/shard_map/ppermute | solution.py:30
  27.5 8.2 %collective-permute-start.9 = (bf16[128,384]{1,0:T(8,128)(2,1)S(1)}, bf16[128,384]{1,0:T(8,128)(2,1)S(1)}, u32[]{:S(2)}, u32[]{:S(2)}) collective-permute-start(bf16[128,384]{1,0:T(8,128)(2,1)S(1)} %get-tuple-element.69), channel_id=1, source_target_pairs={{0,8},{4,12},{8,0},{12,4},{1,9},{5,13},{9,1},{13,5},{2,10},{6,14},... | collective-permute-start | bytes 294920 | tf_op jit(solution)/shard_map/ppermute | solution.py:30
  28.7 6.9 %collective-permute-start.10 = (bf16[128,384]{1,0:T(8,128)(2,1)S(1)}, bf16[128,384]{1,0:T(8,128)(2,1)S(1)}, u32[]{:S(2)}, u32[]{:S(2)}) collective-permute-start(bf16[128,384]{1,0:T(8,128)(2,1)S(1)} %get-tuple-element.70), channel_id=1, source_target_pairs={{0,12},{4,0},{8,4},{12,8},{1,13},{5,1},{9,5},{13,9},{2,14},{6,2},{... | collective-permute-start | bytes 294920 | tf_op jit(solution)/shard_map/ppermute | solution.py:30
  35.7 6.1 %collective-permute-start.14 = (bf16[256,384]{1,0:T(8,128)(2,1)S(1)}, bf16[256,384]{1,0:T(8,128)(2,1)S(1)}, u32[]{:S(2)}, u32[]{:S(2)}) collective-permute-start(bf16[256,384]{1,0:T(8,128)(2,1)S(1)} %constant_dynamic-update-slice_fusion.2.refs_1_), channel_id=1, source_target_pairs={{0,2},{2,0},{1,3},{3,1},{4,6},{6,4},{5,7},{7,5},{8,10},{10,8},{9,1... | collective-permute-start | bytes 589832 | tf_op jit(solution)/shard_map/ppermute | solution.py:21
  37.3 6.6 %collective-permute-start.13 = (bf16[256,384]{1,0:T(8,128)(2,1)S(1)}, bf16[256,384]{1,0:T(8,128)(2,1)S(1)}, u32[]{:S(2)}, u32[]{:S(2)}) collective-permute-start(bf16[256,384]{1,0:T(8,128)(2,1)S(1)} %constant_dynamic-update-slice_fusion.refs_0_), channel_id=1, source_target_pairs={{0,2},{2,0},{1,3},{3,1},{4,6},{6,4},{5,7},{7,5},{8,10},{10,8},{9,1... | collective-permute-start | bytes 589832 | tf_op jit(solution)/shard_map/ppermute | solution.py:21
  40.5 3.9 %collective-permute-start.12 = (bf16[256,384]{1,0:T(8,128)(2,1)S(1)}, bf16[256,384]{1,0:T(8,128)(2,1)S(1)}, u32[]{:S(2)}, u32[]{:S(2)}) collective-permute-start(bf16[256,384]{1,0:T(8,128)(2,1)S(1)} %constant_dynamic-update-slice_fusion.2.refs_1_), channel_id=1, source_target_pairs={{0,1},{1,0},{2,3},{3,2},{4,5},{5,4},{6,7},{7,6},{8,9},{9,8},{10,11... | collective-permute-start | bytes 589832 | tf_op jit(solution)/shard_map/ppermute | solution.py:21
  40.6 3.8 %collective-permute-start.11 = (bf16[256,384]{1,0:T(8,128)(2,1)S(1)}, bf16[256,384]{1,0:T(8,128)(2,1)S(1)}, u32[]{:S(2)}, u32[]{:S(2)}) collective-permute-start(bf16[256,384]{1,0:T(8,128)(2,1)S(1)} %constant_dynamic-update-slice_fusion.refs_0_), channel_id=1, source_target_pairs={{0,1},{1,0},{2,3},{3,2},{4,5},{5,4},{6,7},{7,6},{8,9},{9,8},{10,11... | collective-permute-start | bytes 589832 | tf_op jit(solution)/shard_map/ppermute | solution.py:21
  43.9 1.4 %collective-permute-start.15 = (bf16[256,384]{1,0:T(8,128)(2,1)S(1)}, bf16[256,384]{1,0:T(8,128)(2,1)S(1)}, u32[]{:S(2)}, u32[]{:S(2)}) collective-permute-start(bf16[256,384]{1,0:T(8,128)(2,1)S(1)} %collective-permute-done.13.refs_4_), channel_id=1, source_target_pairs={{0,1},{1,0},{2,3},{3,2},{4,5},{5,4},{6,7},{7,6},{8,9},{9,8},{10,11... | collective-permute-start | bytes 589832 | tf_op jit(solution)/shard_map/ppermute | solution.py:21
  43.9 1.7 %collective-permute-start.16 = (bf16[256,384]{1,0:T(8,128)(2,1)S(1)}, bf16[256,384]{1,0:T(8,128)(2,1)S(1)}, u32[]{:S(2)}, u32[]{:S(2)}) collective-permute-start(bf16[256,384]{1,0:T(8,128)(2,1)S(1)} %collective-permute-done.14.refs_5_), channel_id=1, source_target_pairs={{0,1},{1,0},{2,3},{3,2},{4,5},{5,4},{6,7},{7,6},{8,9},{9,8},{10,11... | collective-permute-start | bytes 589832 | tf_op jit(solution)/shard_map/ppermute | solution.py:21
  49.9 8.7 %collective-permute-start.19 = (bf16[256,384]{1,0:T(8,128)(2,1)S(1)}, bf16[256,384]{1,0:T(8,128)(2,1)S(1)}, u32[]{:S(2)}, u32[]{:S(2)}) collective-permute-start(bf16[256,384]{1,0:T(8,128)(2,1)S(1)} %get-tuple-element.75.refs_0_), channel_id=1, source_target_pairs={{0,2},{2,0},{1,3},{3,1},{4,6},{6,4},{5,7},{7,5},{8,10},{10,8},{9,1... | collective-permute-start | bytes 589832 | tf_op jit(solution)/shard_map/ppermute | solution.py:21
  51.5 9.7 %collective-permute-start.20 = (bf16[256,384]{1,0:T(8,128)(2,1)S(1)}, bf16[256,384]{1,0:T(8,128)(2,1)S(1)}, u32[]{:S(2)}, u32[]{:S(2)}) collective-permute-start(bf16[256,384]{1,0:T(8,128)(2,1)S(1)} %get-tuple-element.76.refs_1_), channel_id=1, source_target_pairs={{0,2},{2,0},{1,3},{3,1},{4,6},{6,4},{5,7},{7,5},{8,10},{10,8},{9,1... | collective-permute-start | bytes 589832 | tf_op jit(solution)/shard_map/ppermute | solution.py:21
  58.0 3.8 %collective-permute-start.17 = (bf16[256,384]{1,0:T(8,128)(2,1)S(1)}, bf16[256,384]{1,0:T(8,128)(2,1)S(1)}, u32[]{:S(2)}, u32[]{:S(2)}) collective-permute-start(bf16[256,384]{1,0:T(8,128)(2,1)S(1)} %get-tuple-element.75.refs_0_), channel_id=1, source_target_pairs={{0,1},{1,0},{2,3},{3,2},{4,5},{5,4},{6,7},{7,6},{8,9},{9,8},{10,11... | collective-permute-start | bytes 589832 | tf_op jit(solution)/shard_map/ppermute | solution.py:21
  58.0 3.7 %collective-permute-start.18 = (bf16[256,384]{1,0:T(8,128)(2,1)S(1)}, bf16[256,384]{1,0:T(8,128)(2,1)S(1)}, u32[]{:S(2)}, u32[]{:S(2)}) collective-permute-start(bf16[256,384]{1,0:T(8,128)(2,1)S(1)} %get-tuple-element.76.refs_1_), channel_id=1, source_target_pairs={{0,1},{1,0},{2,3},{3,2},{4,5},{5,4},{6,7},{7,6},{8,9},{9,8},{10,11... | collective-permute-start | bytes 589832 | tf_op jit(solution)/shard_map/ppermute | solution.py:21
  61.2 1.4 %collective-permute-start.21 = (bf16[256,384]{1,0:T(8,128)(2,1)S(1)}, bf16[256,384]{1,0:T(8,128)(2,1)S(1)}, u32[]{:S(2)}, u32[]{:S(2)}) collective-permute-start(bf16[256,384]{1,0:T(8,128)(2,1)S(1)} %collective-permute-done.19.refs_4_), channel_id=1, source_target_pairs={{0,1},{1,0},{2,3},{3,2},{4,5},{5,4},{6,7},{7,6},{8,9},{9,8},{10,11... | collective-permute-start | bytes 589832 | tf_op jit(solution)/shard_map/ppermute | solution.py:21
  61.2 1.7 %collective-permute-start.22 = (bf16[256,384]{1,0:T(8,128)(2,1)S(1)}, bf16[256,384]{1,0:T(8,128)(2,1)S(1)}, u32[]{:S(2)}, u32[]{:S(2)}) collective-permute-start(bf16[256,384]{1,0:T(8,128)(2,1)S(1)} %collective-permute-done.20.refs_5_), channel_id=1, source_target_pairs={{0,1},{1,0},{2,3},{3,2},{4,5},{5,4},{6,7},{7,6},{8,9},{9,8},{10,11... | collective-permute-start | bytes 589832 | tf_op jit(solution)/shard_map/ppermute | solution.py:21
  67.0 1.9 %collective-permute-start.23 = (bf16[256,384]{1,0:T(8,128)(2,1)S(1)}, bf16[256,384]{1,0:T(8,128)(2,1)S(1)}, u32[]{:S(2)}, u32[]{:S(2)}) collective-permute-start(bf16[256,384]{1,0:T(8,128)(2,1)S(1)} %get-tuple-element.83), channel_id=1, source_target_pairs={{0,1},{1,0},{2,3},{3,2},{4,5},{5,4},{6,7},{7,6},{8,9},{9,8},{10,11... | collective-permute-start | bytes 589832 | tf_op jit(solution)/shard_map/ppermute | solution.py:21
  67.3 8.0 %collective-permute-start.24 = (bf16[256,384]{1,0:T(8,128)(2,1)S(1)}, bf16[256,384]{1,0:T(8,128)(2,1)S(1)}, u32[]{:S(2)}, u32[]{:S(2)}) collective-permute-start(bf16[256,384]{1,0:T(8,128)(2,1)S(1)} %get-tuple-element.82.p0), channel_id=1, source_target_pairs={{0,2},{2,0},{1,3},{3,1},{4,6},{6,4},{5,7},{7,5},{8,10},{10,8},{9,1... | collective-permute-start | bytes 589832 | tf_op jit(solution)/shard_map/ppermute | solution.py:21
  68.8 9.1 %collective-permute-start.25 = (bf16[256,384]{1,0:T(8,128)(2,1)S(1)}, bf16[256,384]{1,0:T(8,128)(2,1)S(1)}, u32[]{:S(2)}, u32[]{:S(2)}) collective-permute-start(bf16[256,384]{1,0:T(8,128)(2,1)S(1)} %get-tuple-element.83), channel_id=1, source_target_pairs={{0,3},{1,2},{2,1},{3,0},{4,7},{5,6},{6,5},{7,4},{8,11},{9,10},{10,... | collective-permute-start | bytes 589832 | tf_op jit(solution)/shard_map/ppermute | solution.py:25
  68.9 11.2 %collective-permute-start.26 = (bf16[128,384]{1,0:T(8,128)(2,1)S(1)}, bf16[128,384]{1,0:T(8,128)(2,1)S(1)}, u32[]{:S(2)}, u32[]{:S(2)}) collective-permute-start(bf16[128,384]{1,0:T(8,128)(2,1)S(1)} %get-tuple-element.91), channel_id=1, source_target_pairs={{0,4},{4,8},{8,12},{12,0},{1,5},{5,9},{9,13},{13,1},{2,6},{6,10},{... | collective-permute-start | bytes 294920 | tf_op jit(solution)/shard_map/ppermute | solution.py:30
  72.5 9.9 %collective-permute-start.27 = (bf16[128,384]{1,0:T(8,128)(2,1)S(1)}, bf16[128,384]{1,0:T(8,128)(2,1)S(1)}, u32[]{:S(2)}, u32[]{:S(2)}) collective-permute-start(bf16[128,384]{1,0:T(8,128)(2,1)S(1)} %get-tuple-element.93), channel_id=1, source_target_pairs={{0,8},{4,12},{8,0},{12,4},{1,9},{5,13},{9,1},{13,5},{2,10},{6,14},... | collective-permute-start | bytes 294920 | tf_op jit(solution)/shard_map/ppermute | solution.py:30
  75.2 7.2 %collective-permute-start.28 = (bf16[128,384]{1,0:T(8,128)(2,1)S(1)}, bf16[128,384]{1,0:T(8,128)(2,1)S(1)}, u32[]{:S(2)}, u32[]{:S(2)}) collective-permute-start(bf16[128,384]{1,0:T(8,128)(2,1)S(1)} %get-tuple-element.95), channel_id=1, source_target_pairs={{0,12},{4,0},{8,4},{12,8},{1,13},{5,1},{9,5},{13,9},{2,14},{6,2},{... | collective-permute-start | bytes 294920 | tf_op jit(solution)/shard_map/ppermute | solution.py:30
  82.4 19.7 %collective-permute-start.44 = (bf16[256,768]{1,0:T(8,128)(2,1)S(1)}, bf16[256,768]{1,0:T(8,128)(2,1)S(1)}, u32[]{:S(2)}, u32[]{:S(2)}) collective-permute-start(bf16[256,768]{1,0:T(8,128)(2,1)S(1)} %get-tuple-element.112), channel_id=1, source_target_pairs={{0,2},{2,0},{1,3},{3,1},{4,6},{6,4},{5,7},{7,5},{8,10},{10,8},{9,1... | collective-permute-start | bytes 1179656 | tf_op jit(solution)/shard_map/ppermute | solution.py:21
  83.9 9.6 %collective-permute-start.29 = (bf16[256,384]{1,0:T(8,128)(2,1)S(1)}, bf16[256,384]{1,0:T(8,128)(2,1)S(1)}, u32[]{:S(2)}, u32[]{:S(2)}) collective-permute-start(bf16[256,384]{1,0:T(8,128)(2,1)S(1)} %get-tuple-element.97), channel_id=1, source_target_pairs={{0,4},{4,8},{8,12},{12,0},{1,5},{5,9},{9,13},{13,1},{2,6},{6,10},{... | collective-permute-start | bytes 589832 | tf_op jit(solution)/shard_map/ppermute | solution.py:30
  86.5 15.1 %collective-permute-start.30 = (bf16[256,384]{1,0:T(8,128)(2,1)S(1)}, bf16[256,384]{1,0:T(8,128)(2,1)S(1)}, u32[]{:S(2)}, u32[]{:S(2)}) collective-permute-start(bf16[256,384]{1,0:T(8,128)(2,1)S(1)} %get-tuple-element.98), channel_id=1, source_target_pairs={{0,8},{4,12},{8,0},{12,4},{1,9},{5,13},{9,1},{13,5},{2,10},{6,14},... | collective-permute-start | bytes 589832 | tf_op jit(solution)/shard_map/ppermute | solution.py:30
  88.1 13.6 %collective-permute-start.31 = (bf16[256,384]{1,0:T(8,128)(2,1)S(1)}, bf16[256,384]{1,0:T(8,128)(2,1)S(1)}, u32[]{:S(2)}, u32[]{:S(2)}) collective-permute-start(bf16[256,384]{1,0:T(8,128)(2,1)S(1)} %get-tuple-element.99), channel_id=1, source_target_pairs={{0,12},{4,0},{8,4},{12,8},{1,13},{5,1},{9,5},{13,9},{2,14},{6,2},{... | collective-permute-start | bytes 589832 | tf_op jit(solution)/shard_map/ppermute | solution.py:30
  88.9 13.3 %collective-permute-start.32 = (bf16[256,384]{1,0:T(8,128)(2,1)S(1)}, bf16[256,384]{1,0:T(8,128)(2,1)S(1)}, u32[]{:S(2)}, u32[]{:S(2)}) collective-permute-start(bf16[256,384]{1,0:T(8,128)(2,1)S(1)} %get-tuple-element.96.refs_0_), channel_id=1, source_target_pairs={{0,1},{1,0},{2,3},{3,2},{4,5},{5,4},{6,7},{7,6},{8,9},{9,8},{10,11... | collective-permute-start | bytes 589832 | tf_op jit(solution)/shard_map/ppermute | solution.py:21
  93.6 8.7 %collective-permute-start.33 = (bf16[256,384]{1,0:T(8,128)(2,1)S(1)}, bf16[256,384]{1,0:T(8,128)(2,1)S(1)}, u32[]{:S(2)}, u32[]{:S(2)}) collective-permute-start(bf16[256,384]{1,0:T(8,128)(2,1)S(1)} %collective-permute-done.29.refs_1_), channel_id=1, source_target_pairs={{0,1},{1,0},{2,3},{3,2},{4,5},{5,4},{6,7},{7,6},{8,9},{9,8},{10,11... | collective-permute-start | bytes 589832 | tf_op jit(solution)/shard_map/ppermute | solution.py:21
  101.6 1.4 %collective-permute-start.34 = (bf16[256,384]{1,0:T(8,128)(2,1)S(1)}, bf16[256,384]{1,0:T(8,128)(2,1)S(1)}, u32[]{:S(2)}, u32[]{:S(2)}) collective-permute-start(bf16[256,384]{1,0:T(8,128)(2,1)S(1)} %collective-permute-done.30.refs_2_), channel_id=1, source_target_pairs={{0,1},{1,0},{2,3},{3,2},{4,5},{5,4},{6,7},{7,6},{8,9},{9,8},{10,11... | collective-permute-start | bytes 589832 | tf_op jit(solution)/shard_map/ppermute | solution.py:21
  101.6 1.7 %collective-permute-start.35 = (bf16[256,384]{1,0:T(8,128)(2,1)S(1)}, bf16[256,384]{1,0:T(8,128)(2,1)S(1)}, u32[]{:S(2)}, u32[]{:S(2)}) collective-permute-start(bf16[256,384]{1,0:T(8,128)(2,1)S(1)} %collective-permute-done.31.refs_3_), channel_id=1, source_target_pairs={{0,1},{1,0},{2,3},{3,2},{4,5},{5,4},{6,7},{7,6},{8,9},{9,8},{10,11... | collective-permute-start | bytes 589832 | tf_op jit(solution)/shard_map/ppermute | solution.py:21
  102.2 23.0 %collective-permute-start.45 = (bf16[256,768]{1,0:T(8,128)(2,1)S(1)}, bf16[256,768]{1,0:T(8,128)(2,1)S(1)}, u32[]{:S(2)}, u32[]{:S(2)}) collective-permute-start(bf16[256,768]{1,0:T(8,128)(2,1)S(1)} %collective-permute-done.44.refs_11_), channel_id=1, source_target_pairs={{0,1},{1,0},{2,3},{3,2},{4,5},{5,4},{6,7},{7,6},{8,9},{9,8},{10,11... | collective-permute-start | bytes 1179656 | tf_op jit(solution)/shard_map/ppermute | solution.py:21
  107.5 7.3 %collective-permute-start.36 = (bf16[256,128]{1,0:T(8,128)(2,1)S(1)}, bf16[256,128]{1,0:T(8,128)(2,1)S(1)}, u32[]{:S(2)}, u32[]{:S(2)}) collective-permute-start(bf16[256,128]{1,0:T(8,128)(2,1)S(1)} %get-tuple-element.105), channel_id=1, source_target_pairs={{0,4},{4,8},{8,12},{12,0},{1,5},{5,9},{9,13},{13,1},{2,6},{6,10},{... | collective-permute-start | bytes 196616 | tf_op jit(solution)/shard_map/ppermute | solution.py:30
  111.9 13.3 %collective-permute-start.43 = (bf16[256,384]{1,0:T(8,128)(2,1)S(1)}, bf16[256,384]{1,0:T(8,128)(2,1)S(1)}, u32[]{:S(2)}, u32[]{:S(2)}) collective-permute-start(bf16[256,384]{1,0:T(8,128)(2,1)S(1)} %get-tuple-element.109), channel_id=1, source_target_pairs={{0,1},{1,0},{2,3},{3,2},{4,5},{5,4},{6,7},{7,6},{8,9},{9,8},{10,11... | collective-permute-start | bytes 589832 | tf_op jit(solution)/shard_map/ppermute | solution.py:21
  111.9 6.4 %collective-permute-start.37 = (bf16[256,128]{1,0:T(8,128)(2,1)S(1)}, bf16[256,128]{1,0:T(8,128)(2,1)S(1)}, u32[]{:S(2)}, u32[]{:S(2)}) collective-permute-start(bf16[256,128]{1,0:T(8,128)(2,1)S(1)} %get-tuple-element.106), channel_id=1, source_target_pairs={{0,8},{4,12},{8,0},{12,4},{1,9},{5,13},{9,1},{13,5},{2,10},{6,14},... | collective-permute-start | bytes 196616 | tf_op jit(solution)/shard_map/ppermute | solution.py:30
  112.8 6.1 %collective-permute-start.38 = (bf16[256,128]{1,0:T(8,128)(2,1)S(1)}, bf16[256,128]{1,0:T(8,128)(2,1)S(1)}, u32[]{:S(2)}, u32[]{:S(2)}) collective-permute-start(bf16[256,128]{1,0:T(8,128)(2,1)S(1)} %get-tuple-element.107), channel_id=1, source_target_pairs={{0,12},{4,0},{8,4},{12,8},{1,13},{5,1},{9,5},{13,9},{2,14},{6,2},{... | collective-permute-start | bytes 196616 | tf_op jit(solution)/shard_map/ppermute | solution.py:30
  114.7 5.6 %collective-permute-start.39 = (bf16[256,128]{1,0:T(8,128)(2,1)S(1)}, bf16[256,128]{1,0:T(8,128)(2,1)S(1)}, u32[]{:S(2)}, u32[]{:S(2)}) collective-permute-start(bf16[256,128]{1,0:T(8,128)(2,1)S(1)} %get-tuple-element.104.refs_0_), channel_id=1, source_target_pairs={{0,2},{2,0},{1,3},{3,1},{4,6},{6,4},{5,7},{7,5},{8,10},{10,8},{9,1... | collective-permute-start | bytes 196616 | tf_op jit(solution)/shard_map/ppermute | solution.py:21
  118.3 5.0 %collective-permute-start.40 = (bf16[256,128]{1,0:T(8,128)(2,1)S(1)}, bf16[256,128]{1,0:T(8,128)(2,1)S(1)}, u32[]{:S(2)}, u32[]{:S(2)}) collective-permute-start(bf16[256,128]{1,0:T(8,128)(2,1)S(1)} %collective-permute-done.36.refs_1_), channel_id=1, source_target_pairs={{0,2},{2,0},{1,3},{3,1},{4,6},{6,4},{5,7},{7,5},{8,10},{10,8},{9,1... | collective-permute-start | bytes 196616 | tf_op jit(solution)/shard_map/ppermute | solution.py:21
  118.9 5.6 %collective-permute-start.41 = (bf16[256,128]{1,0:T(8,128)(2,1)S(1)}, bf16[256,128]{1,0:T(8,128)(2,1)S(1)}, u32[]{:S(2)}, u32[]{:S(2)}) collective-permute-start(bf16[256,128]{1,0:T(8,128)(2,1)S(1)} %collective-permute-done.37.refs_2_), channel_id=1, source_target_pairs={{0,2},{2,0},{1,3},{3,1},{4,6},{6,4},{5,7},{7,5},{8,10},{10,8},{9,1... | collective-permute-start | bytes 196616 | tf_op jit(solution)/shard_map/ppermute | solution.py:21
  120.4 4.8 %collective-permute-start.42 = (bf16[256,128]{1,0:T(8,128)(2,1)S(1)}, bf16[256,128]{1,0:T(8,128)(2,1)S(1)}, u32[]{:S(2)}, u32[]{:S(2)}) collective-permute-start(bf16[256,128]{1,0:T(8,128)(2,1)S(1)} %collective-permute-done.38.refs_3_), channel_id=1, source_target_pairs={{0,2},{2,0},{1,3},{3,1},{4,6},{6,4},{5,7},{7,5},{8,10},{10,8},{9,1... | collective-permute-start | bytes 196616 | tf_op jit(solution)/shard_map/ppermute | solution.py:21
